TPU v7x, 32 devices: a whole 2x2x4 slice. The times are simulated.
32 devices in a mesh: parts: 2 (over x), mesh: 16 (over z, y, core).
Axes of the slice: x: 2, y: 2, z: 4, core: 2. Of those that a mesh axis runs over, the one named last changes fastest.
Arguments:
- grid_in: bfloat16 [474, 8192], P(None, ('parts', 'mesh')), parts along dimension 1, may hold values from -6 to 6
- mesh_init: bfloat16 [512, 512], P(('parts', 'mesh')), parts along dimension 0, may hold values from -6 to 6
- embed_weight: bfloat16 [474, 512], replicated, may hold values from -0.25 to 0.25
- enc_send: bfloat16 [512, 512], replicated, may hold values from -0.25 to 0.25
- enc_recv: bfloat16 [512, 512], replicated, may hold values from -0.25 to 0.25
- enc_node: bfloat16 [512, 512], replicated, may hold values from -0.25 to 0.25
- mid_send: bfloat16 [512, 512], replicated, may hold values from -0.25 to 0.25
- mid_recv: bfloat16 [512, 512], replicated, may hold values from -0.25 to 0.25
- mid_node: bfloat16 [512, 512], replicated, may hold values from -0.25 to 0.25
- dec_send: bfloat16 [512, 512], replicated, may hold values from -0.25 to 0.25
- dec_recv: bfloat16 [512, 512], replicated, may hold values from -0.25 to 0.25
- dec_node: bfloat16 [512, 512], replicated, may hold values from -0.25 to 0.25
- mid_gain: float32 [512], replicated, may hold values from 0.5 to 1.5
- cotangent: bfloat16 [8192, 512], P(('parts', 'mesh')), parts along dimension 0, may hold values from -0.035888672 to 0.035888672
- enc_from: int32 [48, 256], P('mesh'), may hold values from 0 to 255
- enc_into: int32 [48, 256], P('mesh'), may hold values from 0 to 15
- enc_count: int32 [48], P('mesh'), may hold values from 1 to 256, as said below
- mid_from: int32 [256, 32], P('mesh'), may hold values from 0 to 15
- mid_into: int32 [256, 32], P('mesh'), may hold values from 0 to 15
- mid_count: int32 [256], P('mesh'), may hold values from 0 to 32, as said below
- dec_from: int32 [48, 512], P('mesh'), may hold values from 0 to 15
- dec_into: int32 [48, 512], P('mesh'), may hold values from 0 to 255
- dec_count: int32 [48], P('mesh'), may hold values from 1 to 512, as said below
Outputs:
- update: bfloat16 [8192, 512], P(('parts', 'mesh')), parts along dimension 0
- embed_grad: float32 [948, 512], P('parts'), parts along dimension 0
- encode_grad: float32 [1024, 512], P('parts'), parts along dimension 0
- process_grad: float32 [1024, 512], P('parts'), parts along dimension 0
- decode_grad: float32 [1024, 512], P('parts'), parts along dimension 0
- output_grad: float32 [1024, 512], P('parts'), parts along dimension 0
There are 2 independent parts, one for each index of `parts`. A program takes and returns all parts, laid end to end along the dimension named above; an argument that names none is the same for every part. Nothing has to cross between parts.
Inputs may be any that keep to these rules, and one draw needn't show every extreme that they name: `enc_count`: at most 256; in every draw one destination block is full from each of its 3 neighbouring source blocks. `mid_count`: at most 32; in every draw one destination block is full from every source block. `dec_count`: at most 512; in every draw one destination block is full from each of its 3 neighbouring source blocks.
All inputs are finite; a program needn't handle non-finite values.
Results may differ from a plain program's by a relative error of at most 0.018.
Values may be sent and summed in bfloat16 or wider, within the bound.
No kernel may reach another device: no remote copies, remote signals or barrier semaphores. Data moves between devices by JAX's collectives and lax.ppermute only.
A program may use at most 64 MiB of HBM per device.

v0:
```python
import jax
import jax.numpy as jnp
from jax import lax
from jax.sharding import PartitionSpec as P

EPSILON = 1e-05


def with_halo(cells, sides, width):
    for axis, dim in sides:
        count = lax.axis_size(axis)
        head = lax.slice_in_dim(cells, 0, width, axis=dim)
        tail = lax.slice_in_dim(cells, cells.shape[dim] - width, cells.shape[dim], axis=dim)
        cells = jnp.concatenate(
            [
                lax.ppermute(tail, axis, [(i, (i + 1) % count) for i in range(count)]),
                cells,
                lax.ppermute(head, axis, [((i + 1) % count, i) for i in range(count)]),
            ],
            axis=dim,
        )
    return cells


def shifted(shard, axis, by):
    count = lax.axis_size(axis)
    return lax.ppermute(shard, axis, [(i, (i + by) % count) for i in range(count)])


def layer_norm(values):
    center = values - jnp.mean(values, axis=-1, keepdims=True)
    spread = jnp.mean(center * center, axis=-1, keepdims=True)
    return center * lax.rsqrt(spread + EPSILON)


def silu_slope(values):
    sigma = jax.nn.sigmoid(values)
    return sigma * (1.0 + values * (1.0 - sigma))


def mm(left, right):
    return jnp.dot(left, right, preferred_element_type=jnp.float32)


def mm_right_t(left, right):
    return jnp.einsum("ae,de->ad", left, right, preferred_element_type=jnp.float32)


def mm_left_t(left, right):
    return jnp.einsum("ad,ae->de", left, right, preferred_element_type=jnp.float32)


def selector(index, valid, rows):
    flat = index.reshape(-1)
    picks = lax.broadcasted_iota(jnp.int32, (rows, flat.shape[0]), 0) == flat[None, :]
    if valid is not None:
        picks = picks & valid.reshape(-1)[None, :]
    return picks.astype(jnp.bfloat16)


def live_slots(index, count):
    return lax.broadcasted_iota(jnp.int32, index.shape, 1) < count[:, None]


def block_rows(index, rows):
    return lax.broadcasted_iota(jnp.int32, index.shape, 0) * rows + index


def collect(table, rows, shape):
    picked = jnp.einsum("rs,rd->sd", table, rows, preferred_element_type=jnp.float32)
    return picked.astype(jnp.bfloat16).reshape(shape + (rows.shape[1],))


def send_slots(block):
    return lax.all_to_all(block, "mesh", split_axis=0, concat_axis=0, tiled=True)


def margin(block):
    return with_halo(block, (("mesh", 0),), block.shape[0])


def return_margin(near_grad, rows):
    total = near_grad[rows : 2 * rows]
    for offset, piece in ((-1, near_grad[:rows]), (1, near_grad[2 * rows :])):
        total = total + shifted(piece.astype(jnp.bfloat16), "mesh", offset).astype(piece.dtype)
    return total


def edge_forward(arrived, target, table):
    width = arrived.shape[-1]
    target_at = jnp.einsum("rs,rd->sd", table, target, preferred_element_type=jnp.float32)
    inputs = arrived.reshape(-1, width).astype(jnp.float32) + target_at
    message = jax.nn.silu(inputs).astype(jnp.bfloat16)
    return (mm(table, message), inputs)


def edge_backward(grad_agg, inputs, table, shape):
    grad_at = jnp.einsum("rs,rd->sd", table, grad_agg, preferred_element_type=jnp.float32)
    grad_in = (grad_at * silu_slope(inputs)).astype(jnp.bfloat16)
    return (grad_in.reshape(shape), mm(table, grad_in))


def fetch(projected, asked):
    table = selector(asked, None, projected.shape[0])
    return (send_slots(collect(table, projected, asked.shape)), table)


def give_back(grad_slots, handle):
    width = grad_slots.shape[-1]
    returned = send_slots(grad_slots)
    return mm(handle, returned.reshape(-1, width))


def shards(
    grid_in,
    mesh_init,
    embed_weight,
    enc_send,
    enc_recv,
    enc_node,
    mid_send,
    mid_recv,
    mid_node,
    dec_send,
    dec_recv,
    dec_node,
    mid_gain,
    cotangent,
    enc_from,
    enc_into,
    enc_count,
    mid_from,
    mid_into,
    mid_count,
    dec_from,
    dec_into,
    dec_count,
):
    grid_rows = grid_in.shape[1]
    mesh_rows = mesh_init.shape[0]
    mid_asked = lax.all_to_all(mid_from, "mesh", split_axis=0, concat_axis=0, tiled=True)
    pre_act = jnp.einsum("cg,cd->gd", grid_in, embed_weight, preferred_element_type=jnp.float32)
    hidden = jax.nn.silu(pre_act).astype(jnp.bfloat16)
    enc_proj = mm(hidden, enc_send).astype(jnp.bfloat16)
    enc_near = margin(enc_proj)
    enc_source = selector(block_rows(enc_from, grid_rows), None, enc_near.shape[0])
    enc_arrived = collect(enc_source, enc_near, enc_from.shape)
    enc_table = selector(enc_into, live_slots(enc_into, enc_count), mesh_rows)
    enc_target = mm(mesh_init, enc_recv).astype(jnp.bfloat16)
    enc_agg, enc_inputs = edge_forward(enc_arrived, enc_target, enc_table)
    enc_norm = layer_norm(enc_agg).astype(jnp.bfloat16)
    latent = (mesh_init.astype(jnp.float32) + mm(enc_norm, enc_node)).astype(jnp.bfloat16)
    mid_proj = mm(latent, mid_send).astype(jnp.bfloat16)
    mid_target = mm(latent, mid_recv).astype(jnp.bfloat16)
    mid_arrived, mid_handle = fetch(mid_proj, mid_asked)
    mid_table = selector(mid_into, live_slots(mid_into, mid_count), mesh_rows)
    mid_agg, mid_inputs = edge_forward(mid_arrived, mid_target, mid_table)
    mid_norm = (layer_norm(mid_agg) * mid_gain).astype(jnp.bfloat16)
    latent_two = (latent.astype(jnp.float32) + mm(mid_norm, mid_node)).astype(jnp.bfloat16)
    dec_proj = mm(latent_two, dec_send).astype(jnp.bfloat16)
    dec_target = mm(hidden, dec_recv).astype(jnp.bfloat16)
    dec_near = margin(dec_proj)
    dec_source = selector(block_rows(dec_from, mesh_rows), None, dec_near.shape[0])
    dec_arrived = collect(dec_source, dec_near, dec_from.shape)
    dec_table = selector(dec_into, live_slots(dec_into, dec_count), grid_rows)
    dec_agg, dec_inputs = edge_forward(dec_arrived, dec_target, dec_table)
    dec_norm = layer_norm(dec_agg).astype(jnp.bfloat16)
    update = (hidden.astype(jnp.float32) + mm(dec_norm, dec_node)).astype(jnp.bfloat16)
    output_term = mm_left_t(dec_norm, cotangent)
    pull = jax.vjp(layer_norm, dec_agg)[1]
    dec_cot = pull(mm_right_t(cotangent, dec_node))[0].astype(jnp.bfloat16)
    dec_slots, dec_dst_sum = edge_backward(dec_cot, dec_inputs, dec_table, dec_arrived.shape)
    dec_near_grad = mm(dec_source, dec_slots.reshape(-1, dec_slots.shape[-1]))
    dec_src_grad = return_margin(dec_near_grad, mesh_rows).astype(jnp.bfloat16)
    dec_dst_grad = dec_dst_sum.astype(jnp.bfloat16)
    decode_term = mm_left_t(latent_two, dec_src_grad)
    latent_two_grad = mm_right_t(dec_src_grad, dec_send)
    pull = jax.vjp(lambda values: layer_norm(values) * mid_gain, mid_agg)[1]
    mid_cot = pull(mm_right_t(latent_two_grad.astype(jnp.bfloat16), mid_node))[0].astype(
        jnp.bfloat16
    )
    mid_slots, mid_dst_sum = edge_backward(mid_cot, mid_inputs, mid_table, mid_arrived.shape)
    mid_src_grad = give_back(mid_slots, mid_handle).astype(jnp.bfloat16)
    mid_dst_grad = mid_dst_sum.astype(jnp.bfloat16)
    process_term = mm_left_t(latent, mid_src_grad)
    latent_grad = (
        latent_two_grad + mm_right_t(mid_src_grad, mid_send) + mm_right_t(mid_dst_grad, mid_recv)
    ).astype(jnp.bfloat16)
    pull = jax.vjp(layer_norm, enc_agg)[1]
    enc_cot = pull(mm_right_t(latent_grad, enc_node))[0].astype(jnp.bfloat16)
    enc_slots, enc_dst_sum = edge_backward(enc_cot, enc_inputs, enc_table, enc_arrived.shape)
    enc_near_grad = mm(enc_source, enc_slots.reshape(-1, enc_slots.shape[-1]))
    enc_src_grad = return_margin(enc_near_grad, grid_rows).astype(jnp.bfloat16)
    encode_term = mm_left_t(hidden, enc_src_grad)
    hidden_grad = (
        cotangent.astype(jnp.float32)
        + mm_right_t(enc_src_grad, enc_send)
        + mm_right_t(dec_dst_grad, dec_recv)
    )
    pre_grad = (hidden_grad * silu_slope(pre_act)).astype(jnp.bfloat16)
    embed_term = jnp.einsum("cg,gd->cd", grid_in, pre_grad, preferred_element_type=jnp.float32)
    embed_grad, encode_grad, process_grad, decode_grad, output_grad = lax.psum(
        (embed_term, encode_term, process_term, decode_term, output_term), "mesh"
    )
    return (update, embed_grad, encode_grad, process_grad, decode_grad, output_grad)


def solution(mesh):
    placed = (
        P(None, ("parts", "mesh")),
        P(("parts", "mesh"), None),
        P(),
        P(),
        P(),
        P(),
        P(),
        P(),
        P(),
        P(),
        P(),
        P(),
        P(),
        P(("parts", "mesh"), None),
        P("mesh", None),
        P("mesh", None),
        P("mesh"),
        P("mesh", None),
        P("mesh", None),
        P("mesh"),
        P("mesh", None),
        P("mesh", None),
        P("mesh"),
    )
    return jax.shard_map(
        shards,
        mesh=mesh,
        in_specs=placed,
        out_specs=(
            P(("parts", "mesh"), None),
            P("parts", None),
            P("parts", None),
            P("parts", None),
            P("parts", None),
            P("parts", None),
        ),
        check_vma=False,
    )
```

profile of v0, /device:TPU:0, one launch (start us, length us, event | category | flops | bytes accessed | tf_op | source)
XLA Modules:
  0.0 256.2 jit_solution(13624631593324874992)
XLA Ops:
  7.2 2.4 multiply_convert_fusion.7
  9.9 5.5 %collective-permute-start.1 = (bf16[256,512]{1,0:T(8,128)(2,1)S(1)}, bf16[256,512]{1,0:T(8,128)(2,1)S(1)}, u32[]{:S(2)}, u32[]{:S(2)}) collective-permute-start(bf16[256,512]{1,0:T(8,128)(2,1)S(1)} %convolution_convert_fusion.3), channel_id=1, source_target_pairs={{1,0},{2,1},{3,2},{4,3},{5,4},{6,5},{7,6},{8,7},{9,8},{10,9},{11,1... | collective-permute-start | bytes 786440 | tf_op jit(solution)/shard_map/ppermute | solution.py:18
  15.5 5.8 %all-to-all-start = ((s32[16,1,32]{2,1,0:T(1,128)}), s32[16,1,32]{2,1,0:T(1,128)S(1)}, u32[]{:S(2)}, u32[]{:S(2)}) async-start(s32[16,1,32]{2,1,0:T(1,128)} %bitcast), calls=%async_computation | async-start | bytes 16384 | tf_op jit(solution)/shard_map/all_to_all | solution.py:141
  22.1 5.6 %all-to-all-done = s32[16,1,32]{2,1,0:T(1,128)S(1)} async-done(((s32[16,1,32]{2,1,0:T(1,128)}), s32[16,1,32]{2,1,0:T(1,128)S(1)}, u32[]{:S(2)}, u32[]{:S(2)}) %all-to-all-start) | async-done | bytes 2080 | tf_op jit(solution)/shard_map/all_to_all | solution.py:141
  28.2 0.7 reduce.3
  28.9 1.8 convert_add_fusion.1
  30.8 0.6 fusion.125
  32.5 1.3 convolution_convert_fusion.1
  33.8 3.6 %all-to-all-start.1 = ((bf16[16,32,512]{2,1,0:T(8,128)(2,1)}), bf16[16,32,512]{2,1,0:T(8,128)(2,1)S(1)}, u32[]{:S(2)}, u32[]{:S(2)}) async-start(bf16[16,32,512]{2,1,0:T(8,128)(2,1)} %bitcast.1), calls=%async_computation.1 | async-start | bytes 1048576 | tf_op jit(solution)/shard_map/all_to_all | solution.py:75
  37.8 2.5 fusion.9
  40.3 11.3 %all-to-all-done.1 = bf16[16,32,512]{2,1,0:T(8,128)(2,1)S(1)} async-done(((bf16[16,32,512]{2,1,0:T(8,128)(2,1)}), bf16[16,32,512]{2,1,0:T(8,128)(2,1)S(1)}, u32[]{:S(2)}, u32[]{:S(2)}) %all-to-all-start.1) | async-done | bytes 524320 | tf_op jit(solution)/shard_map/all_to_all | solution.py:75
  51.6 1.4 convolution_add_fusion
  53.1 1.8 fusion.126
  55.6 0.6 copy-done.56
  56.6 2.7 %collective-permute-start.3 = (bf16[16,512]{1,0:T(8,128)(2,1)S(1)}, bf16[16,512]{1,0:T(8,128)(2,1)S(1)}, u32[]{:S(2)}, u32[]{:S(2)}) collective-permute-start(bf16[16,512]{1,0:T(8,128)(2,1)S(1)} %convolution_convert_fusion.6), channel_id=1, source_target_pairs={{1,0},{2,1},{3,2},{4,3},{5,4},{6,5},{7,6},{8,7},{9,8},{10,9},{11,1... | collective-permute-start | bytes 49160 | tf_op jit(solution)/shard_map/ppermute | solution.py:18
  59.4 1.3 collective-permute-done.3
  60.8 4.4 %collective-permute-done.2 = bf16[16,512]{1,0:T(8,128)(2,1)S(1)} collective-permute-done((bf16[16,512]{1,0:T(8,128)(2,1)S(1)}, bf16[16,512]{1,0:T(8,128)(2,1)S(1)}, u32[]{:S(2)}, u32[]{:S(2)}) %collective-permute-start.2) | collective-permute-done | bytes 16416 | tf_op jit(solution)/shard_map/ppermute | solution.py:16
  65.2 2.5 convert_add_fusion
  67.7 1.3 fusion.127
  70.1 1.5 fusion
  72.6 0.9 collective-permute-done.4
  73.5 4.5 %collective-permute-done.5 = bf16[16,512]{1,0:T(8,128)(2,1)S(1)} collective-permute-done((bf16[16,512]{1,0:T(8,128)(2,1)S(1)}, bf16[16,512]{1,0:T(8,128)(2,1)S(1)}, u32[]{:S(2)}, u32[]{:S(2)}) %collective-permute-start.5) | collective-permute-done | bytes 16416 | tf_op jit(solution)/shard_map/ppermute | solution.py:27
  78.9 1.3 fusion.12
  80.3 3.7 %all-to-all-start.2 = ((bf16[16,32,512]{2,1,0:T(8,128)(2,1)}), bf16[16,32,512]{2,1,0:T(8,128)(2,1)S(1)}, u32[]{:S(2)}, u32[]{:S(2)}) async-start(bf16[16,32,512]{2,1,0:T(8,128)(2,1)} %bitcast.3), calls=%async_computation.2 | async-start | bytes 1048576 | tf_op jit(solution)/shard_map/all_to_all | solution.py:75
  84.3 1.4 fusion.119
  85.7 3.1 %fusion.23 = f32[256,512]{1,0:T(8,128)} fusion(bf16[512,512]{1,0:T(8,128)(2,1)S(1)} %copy-done, bf16[1536,512]{1,0:T(8,128)(2,1)} %copy-done.9, s32[1536]{0:T(1024)S(1)} %copy-done.23, pred[1536]{0:T(1024)(128)(4,1)S(1)} %copy-done.36), kind=kOutput, calls=%fused_computation.35 | convolution fusion | flops 537788416 | bytes 2629120 | tf_op jit(solution)/shard_map/ae,de->ad/dot_general | solution.py:46
  88.8 2.0 fusion.30
  90.8 7.4 %all-to-all-done.2 = bf16[16,32,512]{2,1,0:T(8,128)(2,1)S(1)} async-done(((bf16[16,32,512]{2,1,0:T(8,128)(2,1)}), bf16[16,32,512]{2,1,0:T(8,128)(2,1)S(1)}, u32[]{:S(2)}, u32[]{:S(2)}) %all-to-all-start.2) | async-done | bytes 524320 | tf_op jit(solution)/shard_map/all_to_all | solution.py:75
  98.4 1.3 multiply_reduce_fusion.2
  100.0 3.9 %fusion.129 = (bf16[768,512]{1,0:T(8,128)(2,1)S(1)}, f32[768,512]{1,0:T(8,128)}) fusion(f32[768,512]{1,0:T(8,128)} %copy-done.66, s32[768]{0:T(1024)S(1)} %copy-done.34, pred[768]{0:T(1024)(128)(4,1)S(1)} %copy-done.49, f32[16,512]{1,0:T(8,128)S(1)} %get-tuple-element.14, f32[16]{0:T(128)S(1)} %negate_multiply_fusion.1, s32[768]{0:T(1024)S(1)} %copy-done.53), kind=kOutput, calls=%fused_computation.178 | convolution fusion | flops 621125632 | bytes 3971904 | tf_op jit(solution)/shard_map/dot_general | solution.py:42
  103.9 2.8 %collective-permute-start.6 = (bf16[256,512]{1,0:T(8,128)(2,1)S(1)}, bf16[256,512]{1,0:T(8,128)(2,1)S(1)}, u32[]{:S(2)}, u32[]{:S(2)}) collective-permute-start(bf16[256,512]{1,0:T(8,128)(2,1)S(1)} %get-tuple-element.19), channel_id=1, source_target_pairs={{0,15},{1,0},{2,1},{3,2},{4,3},{5,4},{6,5},{7,6},{8,7},{9,8},{10,9... | collective-permute-start | bytes 786440 | tf_op jit(solution)/shard_map/ppermute | solution.py:27
  106.7 1.3 fusion.135
  108.0 1.3 fusion.134
  109.3 1.3 collective-permute-done.6
  110.6 4.6 %collective-permute-done.7 = bf16[256,512]{1,0:T(8,128)(2,1)S(1)} collective-permute-done((bf16[256,512]{1,0:T(8,128)(2,1)S(1)}, bf16[256,512]{1,0:T(8,128)(2,1)S(1)}, u32[]{:S(2)}, u32[]{:S(2)}) %collective-permute-start.7) | collective-permute-done | bytes 262176 | tf_op jit(solution)/shard_map/ppermute | solution.py:27
  115.2 1.1 fusion.50
  116.3 1.3 fusion.133
  117.6 2.8 %convolution_bitcast_fusion = f32[474,512]{1,0:T(8,128)} fusion(bf16[474,256]{1,0:T(8,128)(2,1)S(1)} %copy-done.64, f32[256,512]{1,0:T(8,128)} %fusion.23, bf16[256,512]{1,0:T(8,128)(2,1)S(1)} %fusion.50, bf16[512,512]{1,0:T(8,128)(2,1)S(1)} %copy-done.19, f32[256,512]{1,0:T(8,128)} %get-tuple-element.26, bf16[256,512]{1,0:T(8,128)(2,1)S(1)} %copy-done.17), kind=kOutput, calls=%fused_computation.21 | convolution fusion | flops 260046848 | bytes 3310592 | tf_op jit(solution)/shard_map/cg,gd->cd/dot_general | solution.py:201
  120.5 1.0 copy-done.6
  121.5 1.0 fusion.15
  122.6 119.3 %all-reduce.3.cloned.1.call-done = (f32[474,512]{1,0:T(8,128)}, f32[512,512]{1,0:T(8,128)}, f32[512,512]{1,0:T(8,128)}, f32[512,512]{1,0:T(8,128)}, f32[512,512]{1,0:T(8,128)}) async-done(((f32[474,512]{1,0:T(8,128)}, f32[512,512]{1,0:T(8,128)}, f32[512,512]{1,0:T(8,128)}, f32[512,512]{1,0:T(8,128)}, f32[512,512]{1,0:T(8,128)}), (f32[474,512]{1,0:T(8,128)}, f32[512,512]{1,0:T(8,128)}, f32[512,512]{1,0:T(8,128)}, ...) | async-done | bytes 5165072 | tf_op jit(solution)/shard_map/psum | solution.py:202
  241.9 2.4 copy.34
  244.2 1.0 copy.35
  245.2 1.0 copy.36
  246.2 0.6 copy-done.12
  246.8 1.0 copy.37
  247.8 0.6 copy-done.11
  248.4 1.0 copy.38
  (185 shorter events, 7.9 us)
Async XLA Ops:
  7.2 30.6 %copy-start = (bf16[512,512]{1,0:T(8,128)(2,1)S(1)}, bf16[512,512]{1,0:T(8,128)(2,1)}, u32[]{:S(2)}) copy-start(bf16[512,512]{1,0:T(8,128)(2,1)} %param.33) | copy-start | bytes 1572868
  7.2 14.1 %copy-start.65 = (s32[3]{0:T(128)S(1)}, s32[3]{0:T(128)}, u32[]{:S(2)}) copy-start(s32[3]{0:T(128)} %param.39) | copy-start | bytes 40
  7.2 14.2 %copy-start.50 = (s32[3,256]{1,0:T(4,128)S(1)}, s32[3,256]{1,0:T(4,128)}, u32[]{:S(2)}) copy-start(s32[3,256]{1,0:T(4,128)} %param.38) | copy-start | bytes 9220
  7.2 14.2 %copy-start.21 = (bf16[16,512]{1,0:T(8,128)(2,1)S(1)}, bf16[16,512]{1,0:T(8,128)(2,1)}, u32[]{:S(2)}) copy-start(bf16[16,512]{1,0:T(8,128)(2,1)} %param.24) | copy-start | bytes 49156
  7.2 14.2 %copy-start.20 = (bf16[512,512]{1,0:T(8,128)(2,1)S(1)}, bf16[512,512]{1,0:T(8,128)(2,1)}, u32[]{:S(2)}) copy-start(bf16[512,512]{1,0:T(8,128)(2,1)} %param.27) | copy-start | bytes 1572868
  9.6 12.4 %copy-start.51 = (s32[3,256]{1,0:T(4,128)S(1)}, s32[3,256]{1,0:T(4,128)}, u32[]{:S(2)}) copy-start(s32[3,256]{1,0:T(4,128)} %param.37) | copy-start | bytes 9220
  9.9 19.0 %collective-permute-start.1 = (bf16[256,512]{1,0:T(8,128)(2,1)S(1)}, bf16[256,512]{1,0:T(8,128)(2,1)S(1)}, u32[]{:S(2)}, u32[]{:S(2)}) collective-permute-start(bf16[256,512]{1,0:T(8,128)(2,1)S(1)} %convolution_convert_fusion.3), channel_id=1, source_target_pairs={{1,0},{2,1},{3,2},{4,3},{5,4},{6,5},{7,6},{8,7},{9,8},{10,9},{11,1... | collective-permute-start | bytes 786440 | tf_op jit(solution)/shard_map/ppermute | solution.py:18
  15.5 13.5 %collective-permute-start = (bf16[256,512]{1,0:T(8,128)(2,1)S(1)}, bf16[256,512]{1,0:T(8,128)(2,1)}, u32[]{:S(2)}, u32[]{:S(2)}) collective-permute-start(bf16[256,512]{1,0:T(8,128)(2,1)S(1)} %convolution_convert_fusion.3), channel_id=1, source_target_pairs={{0,1},{1,2},{2,3},{3,4},{4,5},{5,6},{6,7},{7,8},{8,9},{9,10},{10,1... | collective-permute-start | bytes 786440 | tf_op jit(solution)/shard_map/ppermute | solution.py:16
  15.5 12.2 %all-to-all-start = ((s32[16,1,32]{2,1,0:T(1,128)}), s32[16,1,32]{2,1,0:T(1,128)S(1)}, u32[]{:S(2)}, u32[]{:S(2)}) async-start(s32[16,1,32]{2,1,0:T(1,128)} %bitcast), calls=%async_computation | async-start | bytes 16384 | tf_op jit(solution)/shard_map/all_to_all | solution.py:141
  21.4 9.3 %copy-start.48 = (pred[768]{0:T(1024)(128)(4,1)}, pred[768]{0:T(1024)(128)(4,1)S(1)}, u32[]{:S(2)}) copy-start(pred[768]{0:T(1024)(128)(4,1)S(1)} %lt.50) | copy-start | bytes 2308
  21.4 9.3 %copy-start.33 = (s32[768]{0:T(1024)}, s32[768]{0:T(1024)S(1)}, u32[]{:S(2)}) copy-start(s32[768]{0:T(1024)S(1)} %eq.66) | copy-start | bytes 9220
  22.1 8.7 %copy-start.52 = (s32[768]{0:T(1024)}, s32[768]{0:T(1024)S(1)}, u32[]{:S(2)}) copy-start(s32[768]{0:T(1024)S(1)} %eq.69) | copy-start | bytes 9220
  31.9 5.6 %copy-start.62 = (s32[16]{0:T(128)S(1)}, s32[16]{0:T(128)}, u32[]{:S(2)}) copy-start(s32[16]{0:T(128)} %param.42) | copy-start | bytes 196
  31.9 5.7 %copy-start.63 = (s32[3]{0:T(128)S(1)}, s32[3]{0:T(128)}, u32[]{:S(2)}) copy-start(s32[3]{0:T(128)} %param.45) | copy-start | bytes 40
  31.9 5.8 %copy-start.44 = (s32[3,512]{1,0:T(4,128)S(1)}, s32[3,512]{1,0:T(4,128)}, u32[]{:S(2)}) copy-start(s32[3,512]{1,0:T(4,128)} %param.44) | copy-start | bytes 18436
  33.8 17.8 %all-to-all-start.1 = ((bf16[16,32,512]{2,1,0:T(8,128)(2,1)}), bf16[16,32,512]{2,1,0:T(8,128)(2,1)S(1)}, u32[]{:S(2)}, u32[]{:S(2)}) async-start(bf16[16,32,512]{2,1,0:T(8,128)(2,1)} %bitcast.1), calls=%async_computation.1 | async-start | bytes 1048576 | tf_op jit(solution)/shard_map/all_to_all | solution.py:75
  37.5 15.6 %copy-start.28 = (s32[512]{0:T(512)}, s32[512]{0:T(512)S(1)}, u32[]{:S(2)}) copy-start(s32[512]{0:T(512)S(1)} %eq.72) | copy-start | bytes 6148
  37.6 15.4 %copy-start.46 = (pred[512]{0:T(512)(128)(4,1)}, pred[512]{0:T(512)(128)(4,1)S(1)}, u32[]{:S(2)}) copy-start(pred[512]{0:T(512)(128)(4,1)S(1)} %lt.53) | copy-start | bytes 1540
  37.7 32.4 %copy-start.35 = (pred[1536]{0:T(1024)(128)(4,1)}, pred[1536]{0:T(1024)(128)(4,1)S(1)}, u32[]{:S(2)}) copy-start(pred[1536]{0:T(1024)(128)(4,1)S(1)} %lt.47) | copy-start | bytes 4612
  37.7 32.3 %copy-start.22 = (s32[1536]{0:T(1024)}, s32[1536]{0:T(1024)S(1)}, u32[]{:S(2)}) copy-start(s32[1536]{0:T(1024)S(1)} %eq.60) | copy-start | bytes 18436
  37.8 13.8 %copy-start.7 = (bf16[512,512]{1,0:T(8,128)(2,1)S(1)}, bf16[512,512]{1,0:T(8,128)(2,1)}, u32[]{:S(2)}) copy-start(bf16[512,512]{1,0:T(8,128)(2,1)} %param.30) | copy-start | bytes 1572868
  53.1 6.3 %copy-start.45 = (s32[3,512]{1,0:T(4,128)S(1)}, s32[3,512]{1,0:T(4,128)}, u32[]{:S(2)}) copy-start(s32[3,512]{1,0:T(4,128)} %param.43) | copy-start | bytes 18436
  56.6 4.2 %collective-permute-start.3 = (bf16[16,512]{1,0:T(8,128)(2,1)S(1)}, bf16[16,512]{1,0:T(8,128)(2,1)S(1)}, u32[]{:S(2)}, u32[]{:S(2)}) collective-permute-start(bf16[16,512]{1,0:T(8,128)(2,1)S(1)} %convolution_convert_fusion.6), channel_id=1, source_target_pairs={{1,0},{2,1},{3,2},{4,3},{5,4},{6,5},{7,6},{8,7},{9,8},{10,9},{11,1... | collective-permute-start | bytes 49160 | tf_op jit(solution)/shard_map/ppermute | solution.py:18
  59.3 5.9 %collective-permute-start.2 = (bf16[16,512]{1,0:T(8,128)(2,1)S(1)}, bf16[16,512]{1,0:T(8,128)(2,1)S(1)}, u32[]{:S(2)}, u32[]{:S(2)}) collective-permute-start(bf16[16,512]{1,0:T(8,128)(2,1)S(1)} %convolution_convert_fusion.6), channel_id=1, source_target_pairs={{0,1},{1,2},{2,3},{3,4},{4,5},{5,6},{6,7},{7,8},{8,9},{9,10},{10,1... | collective-permute-start | bytes 49160 | tf_op jit(solution)/shard_map/ppermute | solution.py:16
  71.6 7.3 %copy-start.9 = (bf16[1536,512]{1,0:T(8,128)(2,1)}, bf16[1536,512]{1,0:T(8,128)(2,1)S(1)}, u32[]{:S(2)}) copy-start(bf16[1536,512]{1,0:T(8,128)(2,1)S(1)} %fusion) | copy-start | bytes 4718596
  71.6 6.7 %copy-start.38 = (f32[512]{0:T(512)S(1)}, f32[512]{0:T(512)}, u32[]{:S(2)}) copy-start(f32[512]{0:T(512)} %param.35) | copy-start | bytes 6148
  71.6 6.7 %copy-start.42 = (f32[16]{0:T(128)S(1)}, f32[16]{0:T(128)}, u32[]{:S(2)}) copy-start(f32[16]{0:T(128)} %copy-done.41) | copy-start | bytes 196
  71.6 7.0 %copy-start.61 = (f32[16]{0:T(128)S(1)}, f32[16]{0:T(128)}, u32[]{:S(2)}) copy-start(f32[16]{0:T(128)} %copy-done.60) | copy-start | bytes 196
  71.6 7.1 %copy-start.57 = (f32[16]{0:T(128)S(1)}, f32[16]{0:T(128)}, u32[]{:S(2)}) copy-start(f32[16]{0:T(128)} %copy-done.56) | copy-start | bytes 196
  71.6 7.3 %copy-start.10 = (f32[512,512]{1,0:T(8,128)S(1)}, f32[512,512]{1,0:T(8,128)}, u32[]{:S(2)}) copy-start(f32[512,512]{1,0:T(8,128)} %convolution_add_fusion) | copy-start | bytes 3145732
  71.6 7.3 %copy-start.29 = (s32[512]{0:T(512)S(1)}, s32[512]{0:T(512)}, u32[]{:S(2)}) copy-start(s32[512]{0:T(512)} %copy-done.28) | copy-start | bytes 6148
  71.6 7.3 %copy-start.47 = (pred[512]{0:T(512)(128)(4,1)S(1)}, pred[512]{0:T(512)(128)(4,1)}, u32[]{:S(2)}) copy-start(pred[512]{0:T(512)(128)(4,1)} %copy-done.46) | copy-start | bytes 1540
  72.0 1.5 collective-permute-start.4
  72.1 5.9 %collective-permute-start.5 = (bf16[16,512]{1,0:T(8,128)(2,1)S(1)}, bf16[16,512]{1,0:T(8,128)(2,1)S(1)}, u32[]{:S(2)}, u32[]{:S(2)}) collective-permute-start(bf16[16,512]{1,0:T(8,128)(2,1)S(1)} %get-tuple-element.22), channel_id=1, source_target_pairs={{0,1},{1,2},{2,3},{3,4},{4,5},{5,6},{6,7},{7,8},{8,9},{9,10},{10,1... | collective-permute-start | bytes 49160 | tf_op jit(solution)/shard_map/ppermute | solution.py:27
  80.3 17.9 %all-to-all-start.2 = ((bf16[16,32,512]{2,1,0:T(8,128)(2,1)}), bf16[16,32,512]{2,1,0:T(8,128)(2,1)S(1)}, u32[]{:S(2)}, u32[]{:S(2)}) async-start(bf16[16,32,512]{2,1,0:T(8,128)(2,1)} %bitcast.3), calls=%async_computation.2 | async-start | bytes 1048576 | tf_op jit(solution)/shard_map/all_to_all | solution.py:75
  84.0 157.9 %all-reduce.3.cloned.1.call-start = ((), (), s32[]{:S(2)}) async-start(), calls=%async_computation.3 | async-start | bytes 10354688 | tf_op jit(solution)/shard_map/psum | solution.py:202
  85.7 12.6 %copy-start.27 = (s32[512]{0:T(512)S(1)}, s32[512]{0:T(512)}, u32[]{:S(2)}) copy-start(s32[512]{0:T(512)} %copy-done.26) | copy-start | bytes 6148
  88.8 11.2 %copy-start.34 = (s32[768]{0:T(1024)S(1)}, s32[768]{0:T(1024)}, u32[]{:S(2)}) copy-start(s32[768]{0:T(1024)} %copy-done.33) | copy-start | bytes 9220
  90.8 8.9 %copy-start.59 = (f32[16]{0:T(128)S(1)}, f32[16]{0:T(128)}, u32[]{:S(2)}) copy-start(f32[16]{0:T(128)} %copy-done.58) | copy-start | bytes 196
  90.8 9.0 %copy-start.40 = (f32[16]{0:T(128)S(1)}, f32[16]{0:T(128)}, u32[]{:S(2)}) copy-start(f32[16]{0:T(128)} %copy-done.39) | copy-start | bytes 196
  90.8 9.0 %copy-start.55 = (f32[16]{0:T(128)S(1)}, f32[16]{0:T(128)}, u32[]{:S(2)}) copy-start(f32[16]{0:T(128)} %copy-done.54) | copy-start | bytes 196
  90.8 9.2 %copy-start.49 = (pred[768]{0:T(1024)(128)(4,1)S(1)}, pred[768]{0:T(1024)(128)(4,1)}, u32[]{:S(2)}) copy-start(pred[768]{0:T(1024)(128)(4,1)} %copy-done.48) | copy-start | bytes 2308
  90.8 9.2 %copy-start.53 = (s32[768]{0:T(1024)S(1)}, s32[768]{0:T(1024)}, u32[]{:S(2)}) copy-start(s32[768]{0:T(1024)} %copy-done.52) | copy-start | bytes 9220
  103.9 6.6 %collective-permute-start.6 = (bf16[256,512]{1,0:T(8,128)(2,1)S(1)}, bf16[256,512]{1,0:T(8,128)(2,1)S(1)}, u32[]{:S(2)}, u32[]{:S(2)}) collective-permute-start(bf16[256,512]{1,0:T(8,128)(2,1)S(1)} %get-tuple-element.19), channel_id=1, source_target_pairs={{0,15},{1,0},{2,1},{3,2},{4,3},{5,4},{6,5},{7,6},{8,7},{9,8},{10,9... | collective-permute-start | bytes 786440 | tf_op jit(solution)/shard_map/ppermute | solution.py:27
  106.7 8.5 %collective-permute-start.7 = (bf16[256,512]{1,0:T(8,128)(2,1)S(1)}, bf16[256,512]{1,0:T(8,128)(2,1)S(1)}, u32[]{:S(2)}, u32[]{:S(2)}) collective-permute-start(bf16[256,512]{1,0:T(8,128)(2,1)S(1)} %get-tuple-element.20), channel_id=1, source_target_pairs={{0,1},{1,2},{2,3},{3,4},{4,5},{5,6},{6,7},{7,8},{8,9},{9,10},{10,1... | collective-permute-start | bytes 786440 | tf_op jit(solution)/shard_map/ppermute | solution.py:27
  109.3 8.4 %copy-start.17 = (bf16[256,512]{1,0:T(8,128)(2,1)S(1)}, bf16[256,512]{1,0:T(8,128)(2,1)}, u32[]{:S(2)}) copy-start(bf16[256,512]{1,0:T(8,128)(2,1)} %param.36) | copy-start | bytes 786436
  109.3 8.4 %copy-start.19 = (bf16[512,512]{1,0:T(8,128)(2,1)S(1)}, bf16[512,512]{1,0:T(8,128)(2,1)}, u32[]{:S(2)}) copy-start(bf16[512,512]{1,0:T(8,128)(2,1)} %param.26) | copy-start | bytes 1572868
  110.6 7.1 %copy-start.64 = (bf16[474,256]{1,0:T(8,128)(2,1)S(1)}, bf16[474,256]{1,0:T(8,128)(2,1)}, u32[]{:S(2)}) copy-start(bf16[474,256]{1,0:T(8,128)(2,1)} %param.23) | copy-start | bytes 728068
  (31 other events, 82.9 us)
Sparse Core Ops, SparseCore 0:
  120.6 121.2 all-reduce.2
where the time goes:
time: 257 us; the launch traced here: 256 us
  waiting for transfers between devices  161 us (63%)
  matrix products  40.9 us (16%)
  starting transfers between devices  24.9 us (10%)
  between operations  14.8 us (6%)
  local copies, waits for them, and re-layouts  11.7 us (5%)
  other arithmetic  3.28 us (1%)
    psum x1, waiting for transfers between devices, shards(): lax.psum((embed_term, encode_term, process_term, decode_term, output_term...  119 us
    all_to_all x2, waiting for transfers between devices, send_slots(): lax.all_to_all(block, 'mesh', split_axis=0, concat_axis=0, tiled=True)  18.7 us
    ppermute x4, waiting for transfers between devices, shifted(): lax.ppermute(shard, axis, [(i, (i + by) % count) for i in range(count)])  11.3 us
    unnamed x139, local copies, waits for them, and re-layouts  10.8 us
    dot_general x11, matrix products, mm(): return jnp.dot(left, right, preferred_element_type=jnp.float32)  10.1 us
    ppermute x2, starting transfers between devices, with_halo(): lax.ppermute(head, axis, [((i + 1) % count, i) for i in range(count)])  8.24 us
    dot_general x6, matrix products, mm_right_t(): jnp.einsum('ae,de->ad', left, right, preferred_element_type=jnp.float32)  7.47 us
    all_to_all x2, starting transfers between devices, send_slots(): lax.all_to_all(block, 'mesh', split_axis=0, concat_axis=0, tiled=True)  7.29 us
  transfers between devices with their start and end apart: 12, of which 10 were waited for; matrix products, arithmetic and copies ran while one was open for 6% of the time, Pallas kernels for 0%

commit v1 on v0

v1 whole, which is shorter than its diff:
```python
import jax
import jax.numpy as jnp
from jax import lax
from jax.sharding import PartitionSpec as P

EPSILON = 1e-05
BF = jnp.bfloat16
F32 = jnp.float32


def to_partner(x):
    count = lax.axis_size("mesh")
    return lax.ppermute(x, "mesh", [(i, i ^ 1) for i in range(count)])


def outer_of(i, count):
    return (i + 1) % count if i % 2 else (i - 1) % count


def to_outer(x):
    count = lax.axis_size("mesh")
    return lax.ppermute(x, "mesh", [(i, outer_of(i, count)) for i in range(count)])


def same_core_groups():
    count = lax.axis_size("mesh")
    return [[i for i in range(count) if i % 2 == core] for core in (0, 1)]


def chip_exchange(x):
    return lax.all_to_all(
        x, "mesh", split_axis=0, concat_axis=0, tiled=True, axis_index_groups=same_core_groups()
    )


def gather_chips(x):
    chips = lax.axis_size("mesh") // 2
    copies = jnp.broadcast_to(x[None], (chips,) + x.shape).reshape((chips * x.shape[0],) + x.shape[1:])
    return chip_exchange(copies)


def normalize(values):
    center = values - jnp.mean(values, axis=-1, keepdims=True)
    spread = jnp.mean(center * center, axis=-1, keepdims=True)
    scale = lax.rsqrt(spread + EPSILON)
    return center * scale, scale


def normalize_pull(unit, scale, grad):
    first = jnp.mean(grad, axis=-1, keepdims=True)
    second = jnp.mean(grad * unit, axis=-1, keepdims=True)
    return scale * (grad - first - unit * second)


def silu_both(values):
    sigma = jax.nn.sigmoid(values)
    return values * sigma, sigma * (1.0 + values * (1.0 - sigma))


def silu_slope(values):
    sigma = jax.nn.sigmoid(values)
    return sigma * (1.0 + values * (1.0 - sigma))


def mm(left, right):
    return jnp.dot(left, right, preferred_element_type=F32)


def mm_right_t(left, right):
    return lax.dot_general(left, right, (((1,), (1,)), ((), ())), preferred_element_type=F32)


def mm_left_t(left, right):
    return lax.dot_general(left, right, (((0,), (0,)), ((), ())), preferred_element_type=F32)


def picks(index, rows):
    flat = index.reshape(1, -1)
    return (lax.broadcasted_iota(jnp.int32, (rows, flat.shape[1]), 0) == flat).astype(BF)


def live(index, count):
    slot = lax.broadcasted_iota(jnp.int32, index.shape, 1)
    return jnp.where(slot < count[:, None], index, -1)


def shards(
    grid_in,
    mesh_init,
    embed_weight,
    enc_send,
    enc_recv,
    enc_node,
    mid_send,
    mid_recv,
    mid_node,
    dec_send,
    dec_recv,
    dec_node,
    mid_gain,
    cotangent,
    enc_from,
    enc_into,
    enc_count,
    mid_from,
    mid_into,
    mid_count,
    dec_from,
    dec_into,
    dec_count,
):
    count = lax.axis_size("mesh")
    chips = count // 2
    me = lax.axis_index("mesh")
    core = me % 2
    grid_rows = grid_in.shape[1]
    mesh_rows = mesh_init.shape[0]
    cap_mid = mid_from.shape[1]
    width = embed_weight.shape[1]

    order = jnp.stack([jnp.int32(1), 2 - 2 * core, 2 * core]).astype(jnp.int32)

    grid_partner = to_partner(grid_in)
    grid_outer = to_outer(grid_in)
    mid_codes = jnp.concatenate([mid_from, live(mid_into, mid_count)], axis=1)
    codes_partner = to_partner(mid_codes)
    codes_outer = to_outer(mid_codes)
    codes_sent = lax.all_to_all(mid_codes, "mesh", split_axis=0, concat_axis=0, tiled=True)

    grids = (grid_in, grid_partner, grid_outer)
    pre = [mm_left_t(g, embed_weight) for g in grids]
    hidden = [jax.nn.silu(p).astype(BF) for p in pre]
    enc_proj = [mm(h, enc_send).astype(BF) for h in hidden]
    enc_src = jnp.take(enc_from, order, axis=0)
    enc_dst = jnp.take(live(enc_into, enc_count), order, axis=0)
    enc_target = mm(mesh_init, enc_recv).astype(BF)
    enc_from_picks = [picks(enc_src[k], grid_rows) for k in range(3)]
    enc_into_picks = [picks(enc_dst[k], mesh_rows) for k in range(3)]
    enc_slope = []
    enc_agg = 0.0
    for k in range(3):
        inputs = mm_left_t(enc_from_picks[k], enc_proj[k]) + mm_left_t(enc_into_picks[k], enc_target)
        message, slope = silu_both(inputs)
        enc_slope.append(slope)
        enc_agg = enc_agg + mm(enc_into_picks[k], message.astype(BF))
    enc_unit, enc_scale = normalize(enc_agg)
    latent = (mesh_init.astype(F32) + mm(enc_unit.astype(BF), enc_node)).astype(BF)

    latent_chips = gather_chips(latent)
    latent_all = jnp.concatenate([latent_chips, to_partner(latent_chips)], axis=0)
    all_rows = count * mesh_rows
    block = lax.broadcasted_iota(jnp.int32, (count, cap_mid), 0)
    first_row = (jnp.where(block % 2 == core, 0, chips) + block // 2) * mesh_rows
    mid_proj = mm(latent_all, mid_send).astype(BF)
    mid_target = mm(latent_all, mid_recv).astype(BF)
    outer_block = jnp.where(core == 1, (me + 1) % count, (me + count - 1) % count)
    starts = (
        (me // 2) * mesh_rows,
        (chips + me // 2) * mesh_rows,
        (chips + outer_block // 2) * mesh_rows,
    )
    codes = (mid_codes, codes_partner, codes_outer)
    agg_near = []
    for k in range(3):
        src_picks = picks(first_row + codes[k][:, :cap_mid], all_rows)
        dst_picks = picks(codes[k][:, cap_mid:], mesh_rows)
        target = lax.dynamic_slice_in_dim(mid_target, starts[k], mesh_rows, 0)
        inputs = mm_left_t(src_picks, mid_proj) + mm_left_t(dst_picks, target)
        message, slope = silu_both(inputs)
        if k == 0:
            mid_in_picks, mid_in_slope = dst_picks, slope
        agg_near.append(mm(dst_picks, message.astype(BF)))
    mid_center = agg_near[0] - jnp.mean(agg_near[0], axis=-1, keepdims=True)
    near_latent = jnp.concatenate(
        [lax.dynamic_slice_in_dim(latent_all, s, mesh_rows, 0) for s in starts], axis=0
    )
    near_unit, _ = normalize(jnp.concatenate(agg_near, axis=0))
    near_norm = (near_unit * mid_gain).astype(BF)
    near_two = (near_latent.astype(F32) + mm(near_norm, mid_node)).astype(BF)
    dec_proj = mm(near_two, dec_send).astype(BF)

    out_dst = codes_sent[:, cap_mid:]
    out_picks = picks(jnp.where(out_dst >= 0, first_row + out_dst, -1), all_rows)
    out_src_picks = picks(jnp.where(out_dst >= 0, codes_sent[:, :cap_mid], -1), mesh_rows)
    own_proj = lax.dynamic_slice_in_dim(mid_proj, starts[0], mesh_rows, 0)
    out_slope = silu_slope(mm_left_t(out_picks, mid_target) + mm_left_t(out_src_picks, own_proj))

    dec_src = jnp.take(dec_from, order, axis=0)
    dec_dst = jnp.take(live(dec_into, dec_count), order, axis=0)
    dec_target = mm(hidden[0], dec_recv).astype(BF)
    dec_into_picks = picks(dec_dst, grid_rows)
    slots = dec_src.shape[1]
    near_index = dec_src + mesh_rows * lax.broadcasted_iota(jnp.int32, dec_src.shape, 0)
    dec_from_picks = picks(near_index, 3 * mesh_rows)
    inputs = mm_left_t(dec_from_picks, dec_proj) + mm_left_t(dec_into_picks, dec_target)
    message, dec_slope = silu_both(inputs)
    dec_agg = mm(dec_into_picks, message.astype(BF))
    dec_unit, dec_scale = normalize(dec_agg)
    dec_norm = dec_unit.astype(BF)
    dec_cot = normalize_pull(dec_unit, dec_scale, mm_right_t(cotangent, dec_node)).astype(BF)
    dec_edge = (mm_left_t(dec_into_picks, dec_cot) * dec_slope).astype(BF)
    dec_near = mm(dec_from_picks, dec_edge)
    update = (hidden[0].astype(F32) + mm(dec_norm, dec_node)).astype(BF)
    output_term = mm_left_t(dec_norm, cotangent)
    dec_dst_grad = mm(dec_into_picks, dec_edge).astype(BF)

    from_partner = to_partner(dec_near[mesh_rows : 2 * mesh_rows].astype(BF))
    dec_own = (dec_near[:mesh_rows] + from_partner.astype(F32)).astype(BF)
    packed = jnp.concatenate(
        [dec_own, dec_near[2 * mesh_rows :].astype(BF), mid_center.astype(BF)], axis=0
    )
    packed_chips = gather_chips(packed)
    packed_all = jnp.concatenate([packed_chips, to_partner(packed_chips)], axis=0)
    packed_all = packed_all.reshape(2, chips, 3, mesh_rows, width)
    owned = packed_all[:, :, 0]
    outer = packed_all[:, :, 1]
    forward = jnp.roll(outer, 1, axis=1)
    backward = jnp.roll(outer, -1, axis=1)
    crossed = jnp.where(
        core == 0,
        jnp.stack([forward[1], backward[0]]),
        jnp.stack([backward[1], forward[0]]),
    )
    dec_src_all = (owned.astype(F32) + crossed.astype(F32)).astype(BF).reshape(all_rows, width)
    agg_all = packed_all[:, :, 2].reshape(all_rows, width).astype(F32)
    mid_unit, mid_scale = normalize(agg_all)
    two_grad = mm_right_t(dec_src_all, dec_send)
    mid_pull = mm_right_t(two_grad.astype(BF), mid_node) * mid_gain
    mid_cot = normalize_pull(mid_unit, mid_scale, mid_pull).astype(BF)
    two_all = (latent_all.astype(F32) + mm((mid_unit * mid_gain).astype(BF), mid_node)).astype(BF)
    decode_grad = mm_left_t(two_all, dec_src_all)

    own_cot = lax.dynamic_slice_in_dim(mid_cot, starts[0], mesh_rows, 0)
    in_edge = (mm_left_t(mid_in_picks, own_cot) * mid_in_slope).astype(BF)
    mid_dst_grad = mm(mid_in_picks, in_edge).astype(BF)
    out_edge = (mm_left_t(out_picks, mid_cot) * out_slope).astype(BF)
    mid_src_grad = mm(out_src_picks, out_edge).astype(BF)
    latent_grad = (
        lax.dynamic_slice_in_dim(two_grad, starts[0], mesh_rows, 0)
        + mm_right_t(mid_src_grad, mid_send)
        + mm_right_t(mid_dst_grad, mid_recv)
    ).astype(BF)
    enc_cot = normalize_pull(enc_unit, enc_scale, mm_right_t(latent_grad, enc_node)).astype(BF)

    carried = cotangent.astype(F32) + mm_right_t(dec_dst_grad, dec_recv)
    encode_term = 0.0
    embed_term = 0.0
    for k in range(3):
        edge = (mm_left_t(enc_into_picks[k], enc_cot) * enc_slope[k]).astype(BF)
        src_grad = mm(enc_from_picks[k], edge).astype(BF)
        encode_term = encode_term + mm_left_t(hidden[k], src_grad)
        grad = mm_right_t(src_grad, enc_send)
        if k == 0:
            grad = grad + carried
        pre_grad = (grad * silu_slope(pre[k])).astype(BF)
        embed_term = embed_term + mm(grids[k], pre_grad)

    channels = embed_term.shape[0]
    terms = (embed_term, encode_term, output_term)
    sizes = [t.shape[0] for t in terms]
    piece = 16 * count
    padded = sum(-(-s // piece) * piece for s in sizes)
    flat = [jnp.pad(t.astype(BF), ((0, -(-s // piece) * piece - s), (0, 0))) for t, s in zip(terms, sizes)]
    flat = jnp.concatenate(flat, axis=0).reshape(2, padded // 2, width)
    kept = lax.dynamic_index_in_dim(flat, core, 0, False)
    sent = lax.dynamic_index_in_dim(flat, 1 - core, 0, False)
    half = (kept.astype(F32) + to_partner(sent).astype(F32)).astype(BF)
    rows = padded // count
    riders = jnp.broadcast_to(mid_src_grad[None], (chips, mesh_rows, width))
    arrived = chip_exchange(jnp.concatenate([half.reshape(chips, rows, width), riders], axis=1))
    src_chips = arrived[:, rows:].reshape(chips * mesh_rows, width)
    total = jnp.sum(arrived[:, :rows].astype(F32), axis=0).astype(BF)
    own_half = gather_chips(total)
    other = to_partner(jnp.concatenate([own_half, src_chips], axis=0))
    src_all = jnp.concatenate([src_chips, other[padded // 2 :]], axis=0)
    process_grad = mm_left_t(latent_all, src_all)
    other_half = other[: padded // 2]
    whole = jnp.concatenate(
        [jnp.where(core == 0, own_half, other_half), jnp.where(core == 0, other_half, own_half)], axis=0
    ).astype(F32)
    outs, at = [], 0
    for s in sizes:
        outs.append(whole[at : at + s])
        at += -(-s // piece) * piece
    embed_grad, encode_grad, output_grad = outs
    return (update, embed_grad, encode_grad, process_grad, decode_grad, output_grad)


def solution(mesh):
    both = ("parts", "mesh")
    placed = (
        (P(None, both), P(both, None))
        + (P(),) * 11
        + (P(both, None),)
        + (P("mesh", None), P("mesh", None), P("mesh")) * 3
    )
    return jax.shard_map(
        shards,
        mesh=mesh,
        in_specs=placed,
        out_specs=(P(both, None),) + (P("parts", None),) * 5,
        check_vma=False,
    )
```

time: 257 us -> 186 us (0.72)
  waiting for transfers between devices: 161 us -> 41 us
  blocking collectives: 0 us -> 27.2 us
  matrix products: 40.9 us -> 61.6 us
  between operations: 14.8 us -> 1.61 us
  other arithmetic: 3.28 us -> 14.8 us
    psum x1 -> x0, waiting for transfers between devices: 119 us -> none  [shards(): lax.psum((embed_term, encode_term, process_term, decode_term, output_term...]
    all_to_all x0 -> x1, blocking collectives: none -> 27.2 us  [chip_exchange(): lax.all_to_all(x, 'mesh', split_axis=0, concat_axis=0, tiled=True, axis_i...]
    dot_general x31 -> x53, matrix products: 40.9 us -> 61.6 us  [the longest x24 26.4 us: mm_left_t(): lax.dot_general(left, right, (((0,), (0,)), ((), ())), preferred_element_...]
    ppermute x8 -> x9, waiting for transfers between devices: 17.1 us -> 4.26 us  [the longest x7 4.25 us: to_partner(): return lax.ppermute(x, 'mesh', [(i, i ^ 1) for i in range(count)])]
    all_to_all x3 -> x4, waiting for transfers between devices: 24.3 us -> 36.7 us  [the longest x3 36.7 us: chip_exchange(): lax.all_to_all(x, 'mesh', split_axis=0, concat_axis=0, tiled=True, axis_i...]
    unnamed x139 -> x88, local copies, waits for them, and re-layouts: 10.8 us -> 3.33 us
    all_to_all x3 -> x4, starting transfers between devices: 13.1 us -> 19.3 us  [the longest x3 13.1 us: chip_exchange(): lax.all_to_all(x, 'mesh', split_axis=0, concat_axis=0, tiled=True, axis_i...]
    concatenate x0 -> x9, other arithmetic: none -> 4.94 us  [the longest x1 1.89 us: shards(): other = to_partner(jnp.concatenate([own_half, src_chips], axis=0))]
  transfers between devices with their start and end apart: 12 -> 13, of which waited for: 10 -> 6; matrix products, arithmetic and copies ran while one was open for 6% -> 14% of each run, Pallas kernels for 0% -> 0%
where the time goes in v1:
time: 186 us; the launch traced here: 184 us
  matrix products  61.6 us (33%)
  waiting for transfers between devices  41 us (22%)
  blocking collectives  27.2 us (15%)
  starting transfers between devices  26.2 us (14%)
  other arithmetic  14.8 us (8%)
  local copies, waits for them, and re-layouts  12.1 us (7%)
    all_to_all x3, waiting for transfers between devices, chip_exchange(): lax.all_to_all(x, 'mesh', split_axis=0, concat_axis=0, tiled=True, axis_i...  36.7 us
    all_to_all x1, blocking collectives, chip_exchange(): lax.all_to_all(x, 'mesh', split_axis=0, concat_axis=0, tiled=True, axis_i...  27.2 us
    dot_general x24, matrix products, mm_left_t(): lax.dot_general(left, right, (((0,), (0,)), ((), ())), preferred_element_...  26.4 us
    dot_general x22, matrix products, mm(): return jnp.dot(left, right, preferred_element_type=F32)  24.9 us
    all_to_all x3, starting transfers between devices, chip_exchange(): lax.all_to_all(x, 'mesh', split_axis=0, concat_axis=0, tiled=True, axis_i...  13.1 us
    dot_general x7, matrix products, mm_right_t(): lax.dot_general(left, right, (((1,), (1,)), ((), ())), preferred_element_...  10.3 us
    all_to_all x1, starting transfers between devices, shards(): lax.all_to_all(mid_codes, 'mesh', split_axis=0, concat_axis=0, tiled=True)  6.21 us
    ppermute x2, starting transfers between devices, to_outer(): lax.ppermute(x, 'mesh', [(i, outer_of(i, count)) for i in range(count)])  5.66 us
  transfers between devices with their start and end apart: 13, of which 6 were waited for; matrix products, arithmetic and copies ran while one was open for 14% of the time, Pallas kernels for 0%

profile of v1, /device:TPU:0, one launch (start us, length us, event | category | flops | bytes accessed | tf_op | source)
XLA Modules:
  0.0 184.5 jit_solution(10422911596411984135)
XLA Ops:
  1.3 5.7 %collective-permute-start.1 = (bf16[474,256]{1,0:T(8,128)(2,1)}, bf16[474,256]{1,0:T(8,128)(2,1)S(1)}, u32[]{:S(2)}, u32[]{:S(2)}) collective-permute-start(bf16[474,256]{1,0:T(8,128)(2,1)} %param.27), channel_id=1, source_target_pairs={{0,15},{1,2},{2,1},{3,4},{4,3},{5,6},{6,5},{7,8},{8,7},{9,10},{10,... | collective-permute-start | bytes 728072 | tf_op jit(solution)/shard_map/ppermute | solution.py:22
  7.7 1.4 pad_add_fusion
  9.1 6.2 %all-to-all-start.2 = ((s32[16,1,64]{2,1,0:T(1,128)}), s32[16,1,64]{2,1,0:T(1,128)S(1)}, u32[]{:S(2)}, u32[]{:S(2)}) async-start(s32[16,1,64]{2,1,0:T(1,128)} %bitcast.14), calls=%async_computation.2 | async-start | bytes 16384 | tf_op jit(solution)/shard_map/all_to_all | solution.py:128
  16.8 1.3 gather_fusion.3
  18.0 2.3 %multiply_convert_fusion.15 = (bf16[256,512]{1,0:T(8,128)(2,1)S(1)}, f32[256,512]{1,0:T(8,128)}) fusion(bf16[474,256]{1,0:T(8,128)(2,1)} %param.27, bf16[474,512]{1,0:T(8,128)(2,1)} %param.29), kind=kOutput, calls=%fused_computation.157 | convolution fusion | flops 124911616 | bytes 1514496 | tf_op jit(solution)/shard_map/dot_general | solution.py:74
  22.4 2.5 %fusion.7 = f32[1536,512]{1,0:T(8,128)} fusion(bf16[256,512]{1,0:T(8,128)(2,1)S(1)} %get-tuple-element.51, bf16[512,512]{1,0:T(8,128)(2,1)S(1)} %copy-done.19, s32[1536]{0:T(1024)S(1)} %eq.180), kind=kOutput, calls=%fused_computation.18 | convolution fusion | flops 537395200 | bytes 3938304 | tf_op jit(solution)/shard_map/dot_general | solution.py:74
  27.4 1.0 convolution_add_fusion.16
  31.9 5.9 %all-to-all-start = ((bf16[8,16,512]{2,1,0:T(8,128)(2,1)}), bf16[8,16,512]{2,1,0:T(8,128)(2,1)S(1)}, u32[]{:S(2)}, u32[]{:S(2)}) async-start(bf16[8,16,512]{2,1,0:T(8,128)(2,1)} %broadcast_in_dim.48), calls=%async_computation | async-start | bytes 262144 | tf_op jit(solution)/shard_map/all_to_all | solution.py:31
  38.1 7.0 %all-to-all-done = bf16[8,16,512]{2,1,0:T(8,128)(2,1)S(1)} async-done(((bf16[8,16,512]{2,1,0:T(8,128)(2,1)}), bf16[8,16,512]{2,1,0:T(8,128)(2,1)S(1)}, u32[]{:S(2)}, u32[]{:S(2)}) %all-to-all-start) | async-done | bytes 131104 | tf_op jit(solution)/shard_map/all_to_all | solution.py:31
  49.2 1.3 fusion.73
  51.1 1.9 %fusion.44 = f32[16,512]{1,0:T(8,128)S(1)} fusion(f32[512,512]{1,0:T(8,128)} %fusion.73, bf16[256,512]{1,0:T(8,128)(2,1)S(1)} %convolution_convert_fusion.5, s32[]{:T(128)S(6)} %select_n.126, s32[512]{0:T(512)S(1)} %eq.219), kind=kOutput, calls=%fused_computation.93 | convolution fusion | flops 18366464 | bytes 1101828 | tf_op jit(solution)/shard_map/dot_general | solution.py:66
  53.9 2.5 %convolution_add_fusion = f32[1536,512]{1,0:T(8,128)S(1)} fusion(f32[1536,512]{1,0:T(8,128)} %fusion.7, bf16[48,512]{1,0:T(8,128)(2,1)S(1)} %convolution_convert_fusion.10, s32[1536]{0:T(1024)S(1)} %eq.183), kind=kOutput, calls=%fused_computation.4 | convolution fusion | flops 76357632 | bytes 6346752 | tf_op jit(solution)/shard_map/dot_general | solution.py:74
  56.5 1.3 fusion.206
  58.5 1.5 fusion.1
  60.0 1.2 copy-done.12
  63.6 3.7 %all-to-all-start.1 = ((bf16[8,48,512]{2,1,0:T(8,128)(2,1)}), bf16[8,48,512]{2,1,0:T(8,128)(2,1)S(1)}, u32[]{:S(2)}, u32[]{:S(2)}) async-start(bf16[8,48,512]{2,1,0:T(8,128)(2,1)} %broadcast_in_dim.51), calls=%async_computation.1 | async-start | bytes 786432 | tf_op jit(solution)/shard_map/all_to_all | solution.py:31
  67.5 1.2 convolution_convert_fusion
  68.7 10.6 %all-to-all-done.1 = bf16[8,48,512]{2,1,0:T(8,128)(2,1)S(1)} async-done(((bf16[8,48,512]{2,1,0:T(8,128)(2,1)}), bf16[8,48,512]{2,1,0:T(8,128)(2,1)S(1)}, u32[]{:S(2)}, u32[]{:S(2)}) %all-to-all-start.1) | async-done | bytes 393248 | tf_op jit(solution)/shard_map/all_to_all | solution.py:31
  79.7 1.3 convolution_add_fusion.1
  82.5 1.4 fusion.217
  85.5 1.9 %fusion.28 = bf16[16,512]{1,0:T(8,128)(2,1)S(1)} fusion(f32[512,512]{1,0:T(8,128)} %copy-done.18, bf16[256,512]{1,0:T(8,128)(2,1)} %get-tuple-element.23, s32[]{:T(128)S(6)} %select_n.120, s32[512]{0:T(512)S(1)} %eq.205), kind=kOutput, calls=%fused_computation.75 | convolution fusion | flops 19161088 | bytes 1085444 | tf_op jit(solution)/shard_map/dot_general | solution.py:66
  87.4 1.9 %fusion.27 = bf16[16,512]{1,0:T(8,128)(2,1)S(1)} fusion(bf16[256,512]{1,0:T(8,128)(2,1)S(1)} %copy-done.35, f32[512,512]{1,0:T(8,128)} %convolution_add_fusion.1, s32[512]{0:T(512)S(1)} %eq.229, s32[512]{0:T(512)S(1)} %eq.226), kind=kOutput, calls=%fused_computation.74 | convolution fusion | flops 145113088 | bytes 1331200 | tf_op jit(solution)/shard_map/dot_general | solution.py:66
  89.4 1.3 convolution_add_fusion.18
  90.7 1.6 fusion.196
  92.4 2.3 %convolution_convert_fusion.2 = bf16[256,512]{1,0:T(8,128)(2,1)} fusion(bf16[16,512]{1,0:T(8,128)(2,1)S(1)} %multiply_convert_fusion.26, f32[256,512]{1,0:T(8,128)} %copy-done.22, s32[256]{0:T(256)S(1)} %bitcast.142, s32[256]{0:T(256)S(1)} %bitcast.136), kind=kOutput, calls=%fused_computation.54 | convolution fusion | flops 72683520 | bytes 804864 | tf_op jit(solution)/shard_map/dot_general | solution.py:66
  94.7 1.2 convolution_convert_fusion.3
  95.9 1.2 convolution_convert_fusion.1
  97.2 2.4 %fusion.220 = f32[512,512]{1,0:T(8,128)} fusion(bf16[256,512]{1,0:T(8,128)(2,1)S(1)} %get-tuple-element.51, bf16[256,512]{1,0:T(8,128)(2,1)} %convolution_convert_fusion.3), kind=kOutput, calls=%fused_computation.364 | convolution fusion | flops 134217728 | bytes 1572864 | tf_op jit(solution)/shard_map/dot_general | solution.py:74
  99.5 2.1 %fusion.218 = f32[256,512]{1,0:T(8,128)} fusion(bf16[256,512]{1,0:T(8,128)(2,1)} %convolution_convert_fusion.3, bf16[512,512]{1,0:T(8,128)(2,1)S(1)} %copy-done), kind=kOutput, calls=%fused_computation.362 | convolution fusion | flops 134217728 | bytes 1310720 | tf_op jit(solution)/shard_map/dot_general | solution.py:70
  101.6 3.0 %fusion.18 = bf16[256,512]{1,0:T(8,128)(2,1)} fusion(f32[256,512]{1,0:T(8,128)} %fusion.218, bf16[512,512]{1,0:T(8,128)(2,1)} %param.37, bf16[1536,512]{1,0:T(8,128)(2,1)S(1)} %copy-done.13, s32[1536]{0:T(1024)S(1)} %eq.180, f32[256,512]{1,0:T(8,128)} %get-tuple-element.52, bf16[256,512]{1,0:T(8,128)(2,1)} %param.40), kind=kOutput, calls=%fused_computation.49 | convolution fusion | flops 538968064 | bytes 3676160 | tf_op jit(solution)/shard_map/dot_general | solution.py:70
  104.6 1.3 fusion.219
  106.0 1.9 %convolution_add_fusion.6 = f32[512,512]{1,0:T(8,128)S(1)} fusion(f32[512,512]{1,0:T(8,128)} %fusion.220, bf16[256,512]{1,0:T(8,128)(2,1)} %convolution_convert_fusion.2, f32[256,512]{1,0:T(8,128)} %copy-done.29), kind=kOutput, calls=%fused_computation.25 | convolution fusion | flops 135135232 | bytes 2883584 | tf_op jit(solution)/shard_map/dot_general | solution.py:74
  107.9 1.2 fusion.10
  109.1 2.6 %convolution_add_fusion.8 = f32[512,474]{0,1:T(8,128)} fusion(f32[512,474]{0,1:T(8,128)S(1)} %fusion.219, bf16[474,256]{1,0:T(8,128)(2,1)} %copy-done.37, f32[256,512]{1,0:T(8,128)S(1)} %copy-done.30, bf16[256,512]{1,0:T(8,128)(2,1)} %convolution_convert_fusion.2, bf16[512,512]{1,0:T(8,128)(2,1)S(1)} %copy-done), kind=kOutput, calls=%fused_computation.28 | convolution fusion | flops 259896320 | bytes 3494912 | tf_op jit(solution)/shard_map/dot_general | solution.py:66
  111.7 3.0 %fusion.16 = bf16[474,512]{1,0:T(8,128)(2,1)} fusion(f32[512,474]{0,1:T(8,128)} %convolution_add_fusion.8, bf16[474,256]{1,0:T(8,128)(2,1)} %copy-done.36, f32[256,512]{1,0:T(8,128)} %copy-done.31, bf16[256,512]{1,0:T(8,128)(2,1)} %convolution_convert_fusion.1, bf16[512,512]{1,0:T(8,128)(2,1)S(1)} %copy-done), kind=kOutput, calls=%fused_computation.47 | convolution fusion | flops 260139008 | bytes 3009536 | tf_op jit(solution)/shard_map/dot_general | solution.py:66
  114.6 1.4 fusion.3
  117.5 2.3 %collective-permute-done.7 = bf16[768,512]{1,0:T(8,128)(2,1)} collective-permute-done((bf16[768,512]{1,0:T(8,128)(2,1)}, bf16[768,512]{1,0:T(8,128)(2,1)}, u32[]{:S(2)}, u32[]{:S(2)}) %collective-permute-start.7) | collective-permute-done | bytes 786464 | tf_op jit(solution)/shard_map/ppermute | solution.py:13
  119.8 1.3 fusion.4
  121.2 27.2 %all_to_all.44 = bf16[8,112,512]{2,1,0:T(8,128)(2,1)S(1)} all-to-all(bf16[8,112,512]{2,1,0:T(8,128)(2,1)S(1)} %pad_maximum_fusion), channel_id=1, replica_groups={{0,2,4,6,8,10,12,14},{1,3,5,7,9,11,13,15},{16,18,20,22,24,26,28,30},{17..., dimensions={0} | all-to-all | bytes 1835008 | tf_op jit(solution)/shard_map/all_to_all | solution.py:31
  149.5 3.5 %all-to-all-start.4 = ((bf16[8,96,512]{2,1,0:T(8,128)(2,1)}), bf16[8,96,512]{2,1,0:T(8,128)(2,1)S(1)}, u32[]{:S(2)}, u32[]{:S(2)}) async-start(bf16[8,96,512]{2,1,0:T(8,128)(2,1)} %broadcast_in_dim.53), calls=%async_computation.4 | async-start | bytes 1572864 | tf_op jit(solution)/shard_map/all_to_all | solution.py:31
  153.7 19.1 %all-to-all-done.4 = bf16[8,96,512]{2,1,0:T(8,128)(2,1)S(1)} async-done(((bf16[8,96,512]{2,1,0:T(8,128)(2,1)}), bf16[8,96,512]{2,1,0:T(8,128)(2,1)S(1)}, u32[]{:S(2)}, u32[]{:S(2)}) %all-to-all-start.4) | async-done | bytes 786464 | tf_op jit(solution)/shard_map/all_to_all | solution.py:31
  172.8 1.9 %pad_maximum_fusion.1 = bf16[896,512]{1,0:T(8,128)(2,1)} fusion(bf16[128,512]{1,0:T(8,128)(2,1)} %bitcast.124, bf16[768,512]{1,0:T(8,128)(2,1)S(1)} %bitcast.112), kind=kLoop, calls=%fused_computation.99 | loop fusion | flops 1835008 | bytes 1835008 | tf_op jit(solution)/shard_map/concatenate | solution.py:274
  174.7 1.0 fusion.17
  175.8 2.6 %fusion.77 = f32[512,512]{1,0:T(8,128)} fusion(bf16[256,512]{1,0:T(8,128)(2,1)S(1)} %copy-done.3, bf16[128,512]{1,0:T(8,128)(2,1)} %copy-done.15, bf16[128,512]{1,0:T(8,128)(2,1)S(1)} %bitcast.120, bf16[256,512]{1,0:T(8,128)(2,1)} %get-tuple-element.22, bf16[512,512]{1,0:T(8,128)(2,1)S(1)} %copy-done.1), kind=kOutput, calls=%fused_computation.176 | convolution fusion | flops 269221888 | bytes 2359296 | tf_op jit(solution)/shard_map/dot_general | solution.py:74
  178.3 1.2 broadcast_select_fusion.1
  179.6 1.6 fusion.51
  181.2 1.1 maximum_convert_fusion.1
  183.2 1.3 fusion.80
  (203 shorter events, 27.2 us)
Async XLA Ops:
  0.6 21.2 %copy-start = (bf16[512,512]{1,0:T(8,128)(2,1)S(1)}, bf16[512,512]{1,0:T(8,128)(2,1)}, u32[]{:S(2)}) copy-start(bf16[512,512]{1,0:T(8,128)(2,1)} %param.30) | copy-start | bytes 1572868
  0.7 19.6 %copy-start.41 = (s32[3,512]{1,0:T(4,128)S(1)}, s32[3,512]{1,0:T(4,128)}, u32[]{:S(2)}) copy-start(s32[3,512]{1,0:T(4,128)} %param.48) | copy-start | bytes 18436
  0.7 19.6 %copy-start.42 = (s32[3]{0:T(128)S(1)}, s32[3]{0:T(128)}, u32[]{:S(2)}) copy-start(s32[3]{0:T(128)} %param.49) | copy-start | bytes 40
  0.7 20.3 %copy-start.25 = (s32[3,512]{1,0:T(4,128)S(1)}, s32[3,512]{1,0:T(4,128)}, u32[]{:S(2)}) copy-start(s32[3,512]{1,0:T(4,128)} %param.47) | copy-start | bytes 18436
  0.7 21.0 %copy-start.38 = (bf16[16,512]{1,0:T(8,128)(2,1)S(1)}, bf16[16,512]{1,0:T(8,128)(2,1)}, u32[]{:S(2)}) copy-start(bf16[16,512]{1,0:T(8,128)(2,1)} %param.28) | copy-start | bytes 49156
  0.7 21.0 %copy-start.26 = (bf16[512,512]{1,0:T(8,128)(2,1)S(1)}, bf16[512,512]{1,0:T(8,128)(2,1)}, u32[]{:S(2)}) copy-start(bf16[512,512]{1,0:T(8,128)(2,1)} %param.31) | copy-start | bytes 1572868
  0.7 25.5 %collective-permute-start = (bf16[474,256]{1,0:T(8,128)(2,1)}, bf16[474,256]{1,0:T(8,128)(2,1)S(1)}, u32[]{:S(2)}, u32[]{:S(2)}) collective-permute-start(bf16[474,256]{1,0:T(8,128)(2,1)} %param.27), channel_id=1, source_target_pairs={{0,1},{1,0},{2,3},{3,2},{4,5},{5,4},{6,7},{7,6},{8,9},{9,8},{10,11... | collective-permute-start | bytes 728072 | tf_op jit(solution)/shard_map/ppermute | solution.py:13
  1.3 27.2 %collective-permute-start.1 = (bf16[474,256]{1,0:T(8,128)(2,1)}, bf16[474,256]{1,0:T(8,128)(2,1)S(1)}, u32[]{:S(2)}, u32[]{:S(2)}) collective-permute-start(bf16[474,256]{1,0:T(8,128)(2,1)} %param.27), channel_id=1, source_target_pairs={{0,15},{1,2},{2,1},{3,4},{4,3},{5,6},{6,5},{7,8},{8,7},{9,10},{10,... | collective-permute-start | bytes 728072 | tf_op jit(solution)/shard_map/ppermute | solution.py:22
  9.1 36.1 %collective-permute-start.4 = (s32[16,64]{1,0:T(8,128)}, s32[16,64]{1,0:T(8,128)S(1)}, u32[]{:S(2)}, u32[]{:S(2)}) collective-permute-start(s32[16,64]{1,0:T(8,128)} %pad_add_fusion), channel_id=1, source_target_pairs={{0,15},{1,2},{2,1},{3,4},{4,3},{5,6},{6,5},{7,8},{8,7},{9,10},{10,... | collective-permute-start | bytes 12296 | tf_op jit(solution)/shard_map/ppermute | solution.py:22
  9.1 28.7 %collective-permute-start.3 = (s32[16,64]{1,0:T(8,128)}, s32[16,64]{1,0:T(8,128)S(1)}, u32[]{:S(2)}, u32[]{:S(2)}) collective-permute-start(s32[16,64]{1,0:T(8,128)} %pad_add_fusion), channel_id=1, source_target_pairs={{0,1},{1,0},{2,3},{3,2},{4,5},{5,4},{6,7},{7,6},{8,9},{9,8},{10,11... | collective-permute-start | bytes 12296 | tf_op jit(solution)/shard_map/ppermute | solution.py:13
  9.1 22.2 %all-to-all-start.2 = ((s32[16,1,64]{2,1,0:T(1,128)}), s32[16,1,64]{2,1,0:T(1,128)S(1)}, u32[]{:S(2)}, u32[]{:S(2)}) async-start(s32[16,1,64]{2,1,0:T(1,128)} %bitcast.14), calls=%async_computation.2 | async-start | bytes 16384 | tf_op jit(solution)/shard_map/all_to_all | solution.py:128
  20.3 2.1 %copy-start.19 = (bf16[512,512]{1,0:T(8,128)(2,1)S(1)}, bf16[512,512]{1,0:T(8,128)(2,1)}, u32[]{:S(2)}) copy-start(bf16[512,512]{1,0:T(8,128)(2,1)} %param.37) | copy-start | bytes 1572868
  24.9 1.3 copy-start.11
  25.1 1.9 %copy-start.20 = (f32[256,512]{1,0:T(8,128)}, f32[256,512]{1,0:T(8,128)S(1)}, u32[]{:S(2)}) copy-start(f32[256,512]{1,0:T(8,128)S(1)} %convolution_add_fusion.11) | copy-start | bytes 1572868
  27.4 1.4 copy-start.22
  29.3 1.7 copy-start.9
  30.4 14.7 %copy-start.39 = (s32[16,32]{1,0:T(8,128)S(1)}, s32[16,32]{1,0:T(8,128)}, u32[]{:S(2)}) copy-start(s32[16,32]{1,0:T(8,128)} %param.44) | copy-start | bytes 6148
  30.4 16.1 %copy-start.27 = (bf16[512,512]{1,0:T(8,128)(2,1)S(1)}, bf16[512,512]{1,0:T(8,128)(2,1)}, u32[]{:S(2)}) copy-start(bf16[512,512]{1,0:T(8,128)(2,1)} %param.33) | copy-start | bytes 1572868
  30.8 16.4 %copy-start.28 = (bf16[512,512]{1,0:T(8,128)(2,1)S(1)}, bf16[512,512]{1,0:T(8,128)(2,1)}, u32[]{:S(2)}) copy-start(bf16[512,512]{1,0:T(8,128)(2,1)} %param.34) | copy-start | bytes 1572868
  31.9 13.2 %all-to-all-start = ((bf16[8,16,512]{2,1,0:T(8,128)(2,1)}), bf16[8,16,512]{2,1,0:T(8,128)(2,1)S(1)}, u32[]{:S(2)}, u32[]{:S(2)}) async-start(bf16[8,16,512]{2,1,0:T(8,128)(2,1)} %broadcast_in_dim.48), calls=%async_computation | async-start | bytes 262144 | tf_op jit(solution)/shard_map/all_to_all | solution.py:31
  45.1 8.3 %copy-start.4 = (bf16[8,16,512]{2,1,0:T(8,128)(2,1)}, bf16[8,16,512]{2,1,0:T(8,128)(2,1)S(1)}, u32[]{:S(2)}) copy-start(bf16[8,16,512]{2,1,0:T(8,128)(2,1)S(1)} %all-to-all-done) | copy-start | bytes 393220
  45.1 1.3 collective-permute-start.2
  46.5 6.9 %copy-start.15 = (bf16[128,512]{1,0:T(8,128)(2,1)}, bf16[128,512]{1,0:T(8,128)(2,1)S(1)}, u32[]{:S(2)}) copy-start(bf16[128,512]{1,0:T(8,128)(2,1)S(1)} %collective-permute-done.2) | copy-start | bytes 393220
  47.5 3.6 %copy-start.33 = (bf16[256,512]{1,0:T(8,128)(2,1)}, bf16[256,512]{1,0:T(8,128)(2,1)S(1)}, u32[]{:S(2)}) copy-start(bf16[256,512]{1,0:T(8,128)(2,1)S(1)} %convolution_convert_fusion.5) | copy-start | bytes 786436
  51.1 2.4 %copy-start.1 = (bf16[512,512]{1,0:T(8,128)(2,1)S(1)}, bf16[512,512]{1,0:T(8,128)(2,1)}, u32[]{:S(2)}) copy-start(bf16[512,512]{1,0:T(8,128)(2,1)} %param.35) | copy-start | bytes 1572868
  51.1 2.4 %copy-start.8 = (bf16[512,512]{1,0:T(8,128)(2,1)S(1)}, bf16[512,512]{1,0:T(8,128)(2,1)}, u32[]{:S(2)}) copy-start(bf16[512,512]{1,0:T(8,128)(2,1)} %param.36) | copy-start | bytes 1572868
  51.1 2.4 %copy-start.40 = (f32[512]{0:T(512)S(1)}, f32[512]{0:T(512)}, u32[]{:S(2)}) copy-start(f32[512]{0:T(512)} %param.39) | copy-start | bytes 6148
  56.4 1.5 copy-start.6
  56.4 1.5 copy-start.17
  61.6 17.7 %copy-start.34 = (bf16[256,512]{1,0:T(8,128)(2,1)S(1)}, bf16[256,512]{1,0:T(8,128)(2,1)}, u32[]{:S(2)}) copy-start(bf16[256,512]{1,0:T(8,128)(2,1)} %copy-done.33) | copy-start | bytes 786436
  61.6 1.2 collective-permute-start.5
  63.6 15.7 %all-to-all-start.1 = ((bf16[8,48,512]{2,1,0:T(8,128)(2,1)}), bf16[8,48,512]{2,1,0:T(8,128)(2,1)S(1)}, u32[]{:S(2)}, u32[]{:S(2)}) async-start(bf16[8,48,512]{2,1,0:T(8,128)(2,1)} %broadcast_in_dim.51), calls=%async_computation.1 | async-start | bytes 786432 | tf_op jit(solution)/shard_map/all_to_all | solution.py:31
  79.3 1.7 collective-permute-start.6
  85.5 1.9 %copy-start.35 = (bf16[256,512]{1,0:T(8,128)(2,1)S(1)}, bf16[256,512]{1,0:T(8,128)(2,1)}, u32[]{:S(2)}) copy-start(bf16[256,512]{1,0:T(8,128)(2,1)} %get-tuple-element.23) | copy-start | bytes 786436
  87.4 3.2 %copy-start.10 = (bf16[512,512]{1,0:T(8,128)(2,1)S(1)}, bf16[512,512]{1,0:T(8,128)(2,1)}, u32[]{:S(2)}) copy-start(bf16[512,512]{1,0:T(8,128)(2,1)} %param.32) | copy-start | bytes 1572868
  90.7 4.0 %copy-start.21 = (f32[256,512]{1,0:T(8,128)S(1)}, f32[256,512]{1,0:T(8,128)}, u32[]{:S(2)}) copy-start(f32[256,512]{1,0:T(8,128)} %copy-done.20) | copy-start | bytes 1572868
  94.7 1.2 copy-start.24
  97.2 4.4 %copy-start.13 = (bf16[1536,512]{1,0:T(8,128)(2,1)S(1)}, bf16[1536,512]{1,0:T(8,128)(2,1)}, u32[]{:S(2)}) copy-start(bf16[1536,512]{1,0:T(8,128)(2,1)} %copy-done.12) | copy-start | bytes 4718596
  105.9 1.9 %copy-start.32 = (f32[256,512]{1,0:T(8,128)S(1)}, f32[256,512]{1,0:T(8,128)}, u32[]{:S(2)}) copy-start(f32[256,512]{1,0:T(8,128)} %copy-done.31) | copy-start | bytes 1572868
  106.0 1.9 %copy-start.43 = (bf16[256,512]{1,0:T(8,128)(2,1)S(1)}, bf16[256,512]{1,0:T(8,128)(2,1)}, u32[]{:S(2)}) copy-start(bf16[256,512]{1,0:T(8,128)(2,1)} %convolution_convert_fusion.1) | copy-start | bytes 786436
  117.0 2.7 %collective-permute-start.7 = (bf16[768,512]{1,0:T(8,128)(2,1)}, bf16[768,512]{1,0:T(8,128)(2,1)}, u32[]{:S(2)}, u32[]{:S(2)}) collective-permute-start(bf16[768,512]{1,0:T(8,128)(2,1)} %dynamic-slice_bitcast_fusion), channel_id=1, source_target_pairs={{0,1},{1,0},{2,3},{3,2},{4,5},{5,4},{6,7},{7,6},{8,9},{9,8},{10,11... | collective-permute-start | bytes 2359304 | tf_op jit(solution)/shard_map/ppermute | solution.py:13
  149.5 23.3 %all-to-all-start.4 = ((bf16[8,96,512]{2,1,0:T(8,128)(2,1)}), bf16[8,96,512]{2,1,0:T(8,128)(2,1)S(1)}, u32[]{:S(2)}, u32[]{:S(2)}) async-start(bf16[8,96,512]{2,1,0:T(8,128)(2,1)} %broadcast_in_dim.53), calls=%async_computation.4 | async-start | bytes 1572864 | tf_op jit(solution)/shard_map/all_to_all | solution.py:31
  153.7 21.0 %copy-start.7 = (bf16[512,512]{1,0:T(8,128)(2,1)S(1)}, bf16[512,512]{1,0:T(8,128)(2,1)}, u32[]{:S(2)}) copy-start(bf16[512,512]{1,0:T(8,128)(2,1)} %param.38) | copy-start | bytes 1572868
  153.7 22.1 %copy-start.3 = (bf16[256,512]{1,0:T(8,128)(2,1)S(1)}, bf16[256,512]{1,0:T(8,128)(2,1)}, u32[]{:S(2)}) copy-start(bf16[256,512]{1,0:T(8,128)(2,1)} %copy-done.2) | copy-start | bytes 786436
  153.7 22.1 %copy-start.5 = (bf16[8,16,512]{2,1,0:T(8,128)(2,1)S(1)}, bf16[8,16,512]{2,1,0:T(8,128)(2,1)}, u32[]{:S(2)}) copy-start(bf16[8,16,512]{2,1,0:T(8,128)(2,1)} %copy-done.4) | copy-start | bytes 393220
  174.7 3.6 %collective-permute-start.8 = (bf16[896,512]{1,0:T(8,128)(2,1)}, bf16[896,512]{1,0:T(8,128)(2,1)}, u32[]{:S(2)}, u32[]{:S(2)}) collective-permute-start(bf16[896,512]{1,0:T(8,128)(2,1)} %pad_maximum_fusion.1), channel_id=1, source_target_pairs={{0,1},{1,0},{2,3},{3,2},{4,5},{5,4},{6,7},{7,6},{8,9},{9,8},{10,11... | collective-permute-start | bytes 2752520 | tf_op jit(solution)/shard_map/ppermute | solution.py:13
  181.2 2.0 %copy-start.14 = (bf16[8,16,512]{2,1,0:T(8,128)(2,1)S(1)}, bf16[8,16,512]{2,1,0:T(8,128)(2,1)}, u32[]{:S(2)}) copy-start(bf16[8,16,512]{2,1,0:T(8,128)(2,1)} %slice.173) | copy-start | bytes 393220
  181.2 2.0 %copy-start.16 = (bf16[128,512]{1,0:T(8,128)(2,1)S(1)}, bf16[128,512]{1,0:T(8,128)(2,1)}, u32[]{:S(2)}) copy-start(bf16[128,512]{1,0:T(8,128)(2,1)} %copy-done.15) | copy-start | bytes 393220
  (9 other events, 8.3 us)

commit v2 on v1

v2 whole, which is shorter than its diff:
```python
import jax
import jax.numpy as jnp
from jax import lax
from jax.experimental import pallas as pl
from jax.experimental.pallas import tpu as pltpu
from jax.sharding import PartitionSpec as P

EPSILON = 1e-05
BF = jnp.bfloat16
F32 = jnp.float32


def to_partner(x):
    count = lax.axis_size("mesh")
    return lax.ppermute(x, "mesh", [(i, i ^ 1) for i in range(count)])


def outer_of(i, count):
    return (i + 1) % count if i % 2 else (i - 1) % count


def to_outer(x):
    count = lax.axis_size("mesh")
    return lax.ppermute(x, "mesh", [(i, outer_of(i, count)) for i in range(count)])


def to_chip(x, m):
    count = lax.axis_size("mesh")
    return lax.ppermute(x, "mesh", [(i, i ^ (2 * m)) for i in range(count)])


def same_core_groups():
    count = lax.axis_size("mesh")
    return [[i for i in range(count) if i % 2 == core] for core in (0, 1)]


def chip_exchange(x):
    return lax.all_to_all(
        x, "mesh", split_axis=0, concat_axis=0, tiled=True, axis_index_groups=same_core_groups()
    )


def gather_chips(x):
    chips = lax.axis_size("mesh") // 2
    copies = jnp.broadcast_to(x[None], (chips,) + x.shape).reshape((chips * x.shape[0],) + x.shape[1:])
    return chip_exchange(copies)


def normalize(values):
    center = values - jnp.mean(values, axis=-1, keepdims=True)
    spread = jnp.mean(center * center, axis=-1, keepdims=True)
    scale = lax.rsqrt(spread + EPSILON)
    return center * scale, scale


def normalize_pull(unit, scale, grad):
    first = jnp.mean(grad, axis=-1, keepdims=True)
    second = jnp.mean(grad * unit, axis=-1, keepdims=True)
    return scale * (grad - first - unit * second)


def sigmoid(values):
    return 0.5 * jnp.tanh(0.5 * values) + 0.5


def silu_both(values):
    sigma = sigmoid(values)
    message = values * sigma
    return message, sigma + message * (1.0 - sigma)


def silu_slope(values):
    return silu_both(values)[1]


def mm(left, right):
    return jnp.dot(left, right, preferred_element_type=F32)


def mm_right_t(left, right):
    return lax.dot_general(left, right, (((1,), (1,)), ((), ())), preferred_element_type=F32)


def mm_left_t(left, right):
    return lax.dot_general(left, right, (((0,), (0,)), ((), ())), preferred_element_type=F32)


def by_slot(line, rows):
    hit = lax.broadcasted_iota(jnp.int32, (rows, line.shape[1]), 0) == line
    return jnp.where(hit, 1.0, 0.0).astype(BF)


def live(index, count):
    slot = lax.broadcasted_iota(jnp.int32, index.shape, 1)
    return jnp.where(slot < count[:, None], index, -1)


def call(body, outs, args, scalars=0, scratch=()):
    vmem = pl.BlockSpec(memory_space=pltpu.VMEM)
    smem = pl.BlockSpec(memory_space=pltpu.SMEM)
    return pl.pallas_call(
        body,
        out_shape=[jax.ShapeDtypeStruct(shape, dtype) for shape, dtype in outs],
        in_specs=[smem] * scalars + [vmem] * (len(args) - scalars),
        out_specs=[vmem] * len(outs),
        scratch_shapes=[pltpu.VMEM(shape, dtype) for shape, dtype in scratch],
    )(*args)


def own_nodes(grid, embed, enc_send, enc_recv, mesh_init, pre, hidden, proj, target):
    values = mm_left_t(grid[...], embed[...])
    pre[...] = values
    rows = (values * sigmoid(values)).astype(BF)
    hidden[...] = rows
    proj[...] = mm(rows, enc_send[...]).astype(BF)
    target[...] = mm(mesh_init[...], enc_recv[...]).astype(BF)


def own_targets(hidden, dec_recv, cot, dec_node, pre, pre_near, target, pulled, pre_slope):
    target[...] = mm(hidden[...], dec_recv[...]).astype(BF)
    pulled[...] = mm_right_t(cot[...], dec_node[...])
    pre_slope[0] = silu_slope(pre[...])
    for k in range(2):
        pre_slope[k + 1] = silu_slope(pre_near[k])


def encode(
    grid_p, grid_o, embed, enc_send, own_proj, target, lines, mesh_init, enc_node, codes,
    pre, hidden, slope, unit, scale, latent,
):
    rows = own_proj.shape[0]
    slots = lines.shape[1] // 3
    mesh_rows = mesh_init.shape[0]
    agg = None
    for k in range(3):
        at = slice(k * slots, (k + 1) * slots)
        if k == 0:
            proj = own_proj[...]
        else:
            values = mm_left_t((grid_p, grid_o)[k - 1][...], embed[...])
            pre[k - 1] = values
            near = (values * sigmoid(values)).astype(BF)
            hidden[k - 1] = near
            proj = mm(near, enc_send[...]).astype(BF)
        into = by_slot(lines[1:2, at], mesh_rows)
        inputs = mm_left_t(by_slot(lines[0:1, at], rows), proj) + mm_left_t(into, target[...])
        message, grad = silu_both(inputs)
        slope[at, :] = grad
        part = mm(into, message.astype(BF))
        agg = part if agg is None else agg + part
    rowwise, size = normalize(agg)
    unit[...] = rowwise
    scale[...] = size
    rows = (mesh_init[...].astype(F32) + mm(rowwise.astype(BF), enc_node[...])).astype(BF)
    for c in range(latent.shape[0]):
        latent[c, :mesh_rows, :] = rows
        latent[c, mesh_rows:, :] = codes[...]


def decode(
    where, chips_own, chips_other, first_row, mid_send, mid_recv, mid_node, gain, dec_send, dec_lines, dec_target, pulled,
    latent_all, proj_own, target_all, mid_slope, mid_line, packed, dec_norm, dec_edge, slope, proj_all,
):
    chips = chips_own.shape[0]
    edges = first_row.shape[1]
    mesh_rows = latent_all.shape[0] // (2 * chips)
    for c in range(chips):
        latent_all[c * mesh_rows : (c + 1) * mesh_rows, :] = chips_own[c, :mesh_rows, :]
        latent_all[(chips + c) * mesh_rows : (chips + c + 1) * mesh_rows, :] = chips_other[c, :mesh_rows, :]
    all_rows = latent_all.shape[0]
    everyone = latent_all[...]
    proj = mm(everyone, mid_send[...]).astype(BF)
    proj_all[...] = proj
    proj_own[...] = proj_all[pl.ds(pl.multiple_of(where[1], mesh_rows), mesh_rows), :]
    target_all[...] = mm(everyone, mid_recv[...]).astype(BF)
    parts, latents = [], []
    for k, (gathered, chip, start) in enumerate(
        ((chips_own, where[2], where[1]), (chips_other, where[2], where[3]), (chips_other, where[5], where[4]))
    ):
        words = gathered[chip, mesh_rows:, :].astype(F32)
        source = first_row[...] + words[0:1, :edges].astype(jnp.int32)
        line = words[1:2, :edges].astype(jnp.int32)
        into = by_slot(line, mesh_rows)
        rows = pl.ds(pl.multiple_of(start, mesh_rows), mesh_rows)
        inputs = mm_left_t(by_slot(source, all_rows), proj) + mm_left_t(into, target_all[rows, :])
        message, grad = silu_both(inputs)
        if k == 0:
            mid_slope[...] = grad
            mid_line[...] = line
        parts.append(mm(into, message.astype(BF)))
        latents.append(latent_all[rows, :])
    center = (parts[0] - jnp.mean(parts[0], axis=-1, keepdims=True)).astype(BF)
    unit, _ = normalize(jnp.concatenate(parts, axis=0))
    latents = jnp.concatenate(latents, axis=0).astype(F32)
    latent_two = (latents + mm((unit * gain[...]).astype(BF), mid_node[...])).astype(BF)
    dec_proj = mm(latent_two, dec_send[...]).astype(BF)

    rows = dec_target.shape[0]
    slots = dec_lines.shape[1] // 3
    agg = None
    for k in range(3):
        at = slice(k * slots, (k + 1) * slots)
        into = by_slot(dec_lines[1:2, at], rows)
        source = by_slot(dec_lines[0:1, at], mesh_rows)
        inputs = mm_left_t(source, dec_proj[k * mesh_rows : (k + 1) * mesh_rows]) + mm_left_t(into, dec_target[...])
        message, grad = silu_both(inputs)
        slope[at, :] = grad
        part = mm(into, message.astype(BF))
        agg = part if agg is None else agg + part
    unit, scale = normalize(agg)
    dec_norm[...] = unit.astype(BF)
    cot = normalize_pull(unit, scale, pulled[...]).astype(BF)
    for k in range(3):
        at = slice(k * slots, (k + 1) * slots)
        edge = (mm_left_t(by_slot(dec_lines[1:2, at], rows), cot) * slope[at, :]).astype(BF)
        dec_edge[at, :] = edge
        near_grad = mm(by_slot(dec_lines[0:1, at], mesh_rows), edge).astype(BF)
        for c in range(chips):
            packed[c, k * mesh_rows : (k + 1) * mesh_rows, :] = near_grad
    for c in range(chips):
        packed[c, 3 * mesh_rows :, :] = center


def settle(
    where, hidden, dec_norm, dec_node, cot, dec_edge, dec_lines, dec_recv, proj_own, target_all, out_lines,
    update, out_kept, out_sent, carried, out_slope,
):
    core = where[0]
    half = out_kept.shape[0]
    update[...] = (hidden[...].astype(F32) + mm(dec_norm[...], dec_node[...])).astype(BF)
    term = mm_left_t(dec_norm[...], cot[...]).astype(BF)

    @pl.when(core == 0)
    def _():
        out_kept[...] = term[:half]
        out_sent[...] = term[half:]

    @pl.when(core == 1)
    def _():
        out_kept[...] = term[half:]
        out_sent[...] = term[:half]

    dst = mm(by_slot(dec_lines[1:2, :], hidden.shape[0]), dec_edge[...]).astype(BF)
    carried[...] = cot[...].astype(F32) + mm_right_t(dst, dec_recv[...])
    own = proj_own[...]
    inputs = mm_left_t(by_slot(out_lines[0:1, :], own.shape[0]), own)
    inputs = inputs + mm_left_t(by_slot(out_lines[1:2, :], target_all.shape[0]), target_all[...])
    out_slope[...] = silu_slope(inputs)


def mesh_grads(
    where, packed_own, packed_other, dec_send, mid_node, gain, in_line, out_lines,
    in_slope, out_slope, mid_send, mid_recv, enc_node, enc_unit, enc_scale,
    dec_src, unit_all, src_grad, enc_cot, two_grad, cot_all,
):
    core, own = where[0], where[1]
    mesh_rows = enc_unit.shape[0]
    chips = packed_own.shape[0] // (4 * mesh_rows)
    step = jnp.where(core == 0, chips - 1, 1)
    back = jnp.where(core == 0, 1, chips - 1)

    def chip(c, carry):
        base = c * (4 * mesh_rows)
        for part, (owned, crossed, turn) in enumerate(
            ((packed_own, packed_other, step), (packed_other, packed_own, back))
        ):
            there = lax.rem(c + turn, chips) * (4 * mesh_rows) + 2 * mesh_rows

            def part_at(ref, start):
                return ref[pl.ds(pl.multiple_of(start, mesh_rows), mesh_rows), :].astype(F32)

            put = pl.ds(pl.multiple_of((part * chips + c) * mesh_rows, mesh_rows), mesh_rows)
            total = part_at(owned, base) + part_at(crossed, base + mesh_rows) + part_at(crossed, there)
            dec_src[put, :] = total.astype(BF)
            two_grad[put, :] = part_at(owned, base + 3 * mesh_rows)
        return carry

    lax.fori_loop(0, chips, chip, 0)
    unit, scale = normalize(two_grad[...])
    unit_all[...] = (unit * gain[...]).astype(BF)
    two = mm_right_t(dec_src[...], dec_send[...])
    two_grad[...] = two
    pulled = mm_right_t(two.astype(BF), mid_node[...]) * gain[...]
    cot = normalize_pull(unit, scale, pulled).astype(BF)
    cot_all[...] = cot
    mine = pl.ds(pl.multiple_of(own, mesh_rows), mesh_rows)
    into = by_slot(in_line[...], mesh_rows)
    in_edge = (mm_left_t(into, cot_all[mine, :]) * in_slope[...]).astype(BF)
    dst = mm(into, in_edge).astype(BF)
    out_edge = (mm_left_t(by_slot(out_lines[1:2, :], cot.shape[0]), cot) * out_slope[...]).astype(BF)
    src = mm(by_slot(out_lines[0:1, :], mesh_rows), out_edge).astype(BF)
    src_grad[...] = src
    latent_grad = two_grad[mine, :]
    latent_grad = latent_grad + mm_right_t(src, mid_send[...]) + mm_right_t(dst, mid_recv[...])
    pulled = mm_right_t(latent_grad.astype(BF), enc_node[...])
    enc_cot[...] = normalize_pull(enc_unit[...], enc_scale[...], pulled).astype(BF)


def node_grads(
    where, enc_cot, lines, slope, hidden, hidden_near, enc_send, carried, pre_slope, grid, grid_p, grid_o,
    kept, sent,
):
    core = where[0]
    mesh_rows = enc_cot.shape[0]
    rows = hidden.shape[0]
    slots = lines.shape[1] // 3
    encode_term, embed_term = None, None
    for k in range(3):
        at = slice(k * slots, (k + 1) * slots)
        edge = (mm_left_t(by_slot(lines[1:2, at], mesh_rows), enc_cot[...]) * slope[at, :]).astype(BF)
        src = mm(by_slot(lines[0:1, at], rows), edge).astype(BF)
        part = mm_left_t(hidden[...] if k == 0 else hidden_near[k - 1], src)
        encode_term = part if k == 0 else encode_term + part
        grad = mm_right_t(src, enc_send[...])
        if k == 0:
            grad = grad + carried[...]
        grad = grad * pre_slope[k]
        part = mm((grid, grid_p, grid_o)[k][...], grad.astype(BF))
        embed_term = part if k == 0 else embed_term + part

    def put(ref, term):
        used, room = term.shape[0], ref.shape[0]
        ref[:used, :] = term.astype(BF)
        if used < room:
            ref[used:, :] = jnp.zeros((room - used, ref.shape[1]), BF)

    @pl.when(core == 0)
    def _():
        put(kept, embed_term)
        put(sent, encode_term)

    @pl.when(core == 1)
    def _():
        put(kept, encode_term)
        put(sent, embed_term)


def fold(where, kept, came, out_kept, out_came, src, *pieces):
    chip = where[2]
    chips = len(pieces)
    rows, out_rows = kept.shape[0] // chips, out_kept.shape[0] // chips
    for m, piece in enumerate(pieces):
        c = jnp.bitwise_xor(chip, m)
        at = pl.ds(pl.multiple_of(c * rows, rows), rows)
        piece[:rows, :] = (kept[at, :].astype(F32) + came[at, :].astype(F32)).astype(BF)
        at = pl.ds(pl.multiple_of(c * out_rows, out_rows), out_rows)
        piece[rows : rows + out_rows, :] = (out_kept[at, :].astype(F32) + out_came[at, :].astype(F32)).astype(BF)
        piece[rows + out_rows :, :] = src[...]


def add_up(where, *refs):
    pieces, (total, src) = refs[:-2], refs[-2:]
    chip = where[2]
    both = total.shape[0]
    mesh_rows = src.shape[0] // len(pieces)
    value = None
    for m, piece in enumerate(pieces):
        part = piece[:both, :].astype(F32)
        value = part if m == 0 else value + part
        c = jnp.bitwise_xor(chip, m)
        src[pl.ds(pl.multiple_of(c * mesh_rows, mesh_rows), mesh_rows), :] = piece[both:, :]
    total[...] = value.astype(BF)


def assemble(where, *refs):
    pieces, own = refs[:-1], refs[-1]
    chip = where[2]
    chips = len(pieces)
    out_rows = own.shape[1] // 2 // chips
    rows = pieces[0].shape[0] - out_rows
    for m, piece in enumerate(pieces):
        c = jnp.bitwise_xor(chip, m)
        own[pl.ds(pl.multiple_of(c * rows, rows), rows), :] = piece[:rows, :]
        at = pl.multiple_of(chips * rows + c * out_rows, out_rows)
        own[pl.ds(at, out_rows), :] = piece[rows:, :]


def mesh_terms(latent_all, unit_all, mid_node, dec_src, decode_grad):
    two = (latent_all[...].astype(F32) + mm(unit_all[...], mid_node[...])).astype(BF)
    decode_grad[...] = mm_left_t(two, dec_src[...])


def finish(where, own, other, latent_all, src_own, src_other, embed_grad, encode_grad, process_grad, output_grad):
    core = where[0]
    width = embed_grad.shape[1]
    channels = embed_grad.shape[0]
    room = own.shape[0] - width // 2

    @pl.when(core == 0)
    def _():
        embed_grad[...] = own[:channels, :].astype(F32)
        encode_grad[...] = other[:width, :].astype(F32)
        output_grad[: width // 2, :] = own[room:, :].astype(F32)
        output_grad[width // 2 :, :] = other[room:, :].astype(F32)

    @pl.when(core == 1)
    def _():
        embed_grad[...] = other[:channels, :].astype(F32)
        encode_grad[...] = own[:width, :].astype(F32)
        output_grad[: width // 2, :] = other[room:, :].astype(F32)
        output_grad[width // 2 :, :] = own[room:, :].astype(F32)

    half = src_own.shape[0]
    process_grad[...] = mm_left_t(latent_all[:half, :], src_own[...]) + mm_left_t(latent_all[half:, :], src_other[...])


def shards(
    grid_in,
    mesh_init,
    embed_weight,
    enc_send,
    enc_recv,
    enc_node,
    mid_send,
    mid_recv,
    mid_node,
    dec_send,
    dec_recv,
    dec_node,
    mid_gain,
    cotangent,
    enc_from,
    enc_into,
    enc_count,
    mid_from,
    mid_into,
    mid_count,
    dec_from,
    dec_into,
    dec_count,
):
    count = lax.axis_size("mesh")
    chips = count // 2
    me = lax.axis_index("mesh")
    core = me % 2
    channels, grid_rows = grid_in.shape
    mesh_rows = mesh_init.shape[0]
    cap_mid = mid_from.shape[1]
    width = embed_weight.shape[1]
    all_rows = count * mesh_rows
    gain = mid_gain.reshape(1, width)

    grid_partner = to_partner(grid_in)
    grid_outer = to_outer(grid_in)

    nodes = (grid_rows, width)
    pre, hidden, enc_proj, enc_target = call(
        own_nodes,
        [(nodes, F32), (nodes, BF), (nodes, BF), ((mesh_rows, width), BF)],
        (grid_in, embed_weight, enc_send, enc_recv, mesh_init),
    )
    enc_target, enc_from, enc_into, enc_count, mid_from, mid_into, mid_count, dec_from, dec_into, dec_count = (
        lax.optimization_barrier(
            (enc_target, enc_from, enc_into, enc_count, mid_from, mid_into, mid_count, dec_from, dec_into, dec_count)
        )
    )

    def near(x):
        return jnp.concatenate(
            [x[1:2], jnp.where(core == 0, x[2:3], x[0:1]), jnp.where(core == 0, x[0:1], x[2:3])], axis=0
        )

    enc_lines = jnp.stack([near(enc_from).reshape(-1), near(live(enc_into, enc_count)).reshape(-1)])
    dec_lines = jnp.stack([near(dec_from).reshape(-1), near(live(dec_into, dec_count)).reshape(-1)])
    edges = count * cap_mid
    block = lax.broadcasted_iota(jnp.int32, (count, cap_mid), 0)
    first_row = ((jnp.where(block % 2 == core, 0, chips) + block // 2) * mesh_rows).reshape(1, edges)
    outer_chip = jnp.where(core == 1, (me + 1) % count, (me + count - 1) % count) // 2
    own_start = (me // 2) * mesh_rows
    where = jnp.stack(
        [core, own_start, me // 2, own_start + chips * mesh_rows, (chips + outer_chip) * mesh_rows, outer_chip]
    ).astype(jnp.int32)
    codes = jnp.concatenate([mid_from.reshape(1, edges), live(mid_into, mid_count).reshape(1, edges)], axis=0)
    codes = jnp.pad(codes.astype(BF), ((0, 6), (0, width - edges)))
    enc_slots = enc_lines.shape[1]
    pre_near, hidden_near, enc_slope, enc_unit, enc_scale, latent = call(
        encode,
        [
            ((2,) + nodes, F32),
            ((2,) + nodes, BF),
            ((enc_slots, width), F32),
            ((mesh_rows, width), F32),
            ((mesh_rows, 1), F32),
            ((chips, mesh_rows + 8, width), BF),
        ],
        (
            grid_partner, grid_outer, embed_weight, enc_send, enc_proj, enc_target, enc_lines,
            mesh_init, enc_node, codes,
        ),
    )

    latent_chips = chip_exchange(latent)
    dec_target, dec_pulled, pre_slope = call(
        own_targets,
        [(nodes, BF), (nodes, F32), ((3,) + nodes, F32)],
        (hidden, dec_recv, cotangent, dec_node, pre, pre_near),
    )
    latent_other = to_partner(latent_chips)
    dec_slots = dec_lines.shape[1]
    everyone = (all_rows, width)
    latent_all, proj_own, target_all, in_slope, in_line, packed, dec_norm, dec_edge = call(
        decode,
        [
            (everyone, BF),
            ((mesh_rows, width), BF),
            (everyone, BF),
            ((edges, width), F32),
            ((1, edges), jnp.int32),
            ((chips, 4 * mesh_rows, width), BF),
            (nodes, BF),
            ((dec_slots, width), BF),
        ],
        (
            where, latent_chips, latent_other, first_row, mid_send, mid_recv, mid_node, gain, dec_send, dec_lines,
            dec_target, dec_pulled,
        ),
        scalars=1,
        scratch=[((dec_slots, width), F32), (everyone, BF)],
    )

    def leaving(row):
        lanes = [lax.dynamic_slice_in_dim(x[:, mesh_rows + row], me * cap_mid, cap_mid, 1) for x in gathered]
        return jnp.concatenate(lanes, axis=0).astype(jnp.int32)

    packed, *gathered = lax.optimization_barrier((packed, latent_chips, latent_other))
    leaving_into = leaving(1)
    base = mesh_rows * lax.broadcasted_iota(jnp.int32, leaving_into.shape, 0)
    out_lines = jnp.stack(
        [
            jnp.where(leaving_into >= 0, leaving(0), -1).reshape(-1),
            jnp.where(leaving_into >= 0, base + leaving_into, -1).reshape(-1),
        ]
    )
    packed_chips = chip_exchange(packed.reshape(chips * 4 * mesh_rows, width))
    packed_other = to_partner(packed_chips)
    out_half = (width // 2, width)
    update, out_kept, out_sent, carried, out_slope = call(
        settle,
        [(nodes, BF), (out_half, BF), (out_half, BF), (nodes, F32), ((edges, width), F32)],
        (
            where, hidden, dec_norm, dec_node, cotangent, dec_edge, dec_lines, dec_recv, proj_own, target_all, out_lines,
        ),
        scalars=1,
    )
    out_came = to_partner(out_sent)

    dec_src_all, unit_all, src_grad, enc_cot = call(
        mesh_grads,
        [(everyone, BF), (everyone, BF), ((mesh_rows, width), BF), ((mesh_rows, width), BF)],
        (
            where, packed_chips, packed_other, dec_send, mid_node, gain, in_line, out_lines,
            in_slope, out_slope, mid_send, mid_recv, enc_node, enc_unit, enc_scale,
        ),
        scalars=1,
        scratch=[(everyone, F32), (everyone, BF)],
    )
    piece = 16 * chips
    room = -(-max(channels, width) // piece) * piece
    kept, sent = call(
        node_grads,
        [((room, width), BF), ((room, width), BF)],
        (
            where, enc_cot, enc_lines, enc_slope, hidden, hidden_near, enc_send, carried, pre_slope,
            grid_in, grid_partner, grid_outer,
        ),
        scalars=1,
    )
    (decode_grad,) = call(
        mesh_terms, [((width, width), F32)], (latent_all, unit_all, mid_node, dec_src_all)
    )

    came = to_partner(sent)
    rows, out_rows = room // chips, width // 2 // chips
    both = rows + out_rows
    direct = chips <= 8 and chips & (chips - 1) == 0
    if direct:
        pieces = call(
            fold,
            [((both + mesh_rows, width), BF)] * chips,
            (where, kept, came, out_kept, out_came, src_grad),
            scalars=1,
        )
        arrived = [pieces[0]]
        for m in range(1, chips):
            arrived.append(to_chip(pieces[m], m))
        total, src_own = call(
            add_up, [((both, width), BF), ((chips * mesh_rows, width), BF)], (where, *arrived), scalars=1
        )
        totals = [total]
        for m in range(1, chips):
            totals.append(to_chip(total, m))
        (own,) = call(assemble, [((chips * both, width), BF)], (where, *totals), scalars=1)
    else:
        half = (kept.astype(F32) + came.astype(F32)).astype(BF).reshape(chips, rows, width)
        out = (out_kept.astype(F32) + out_came.astype(F32)).astype(BF).reshape(chips, out_rows, width)
        riders = jnp.broadcast_to(src_grad[None], (chips, mesh_rows, width))
        arrived = chip_exchange(jnp.concatenate([half, out, riders], axis=1))
        src_own = arrived[:, both:].reshape(chips * mesh_rows, width)
        total = jnp.sum(arrived[:, :both].astype(F32), axis=0).astype(BF)
        gathered = gather_chips(total).reshape(chips, both, width)
        own = jnp.concatenate(
            [gathered[:, :rows].reshape(room, width), gathered[:, rows:].reshape(width // 2, width)], axis=0
        )
    src_other = to_partner(src_own)
    other = to_partner(own)
    embed_grad, encode_grad, process_grad, output_grad = call(
        finish,
        [((channels, width), F32)] + [((width, width), F32)] * 3,
        (where, own, other, latent_all, src_own, src_other),
        scalars=1,
    )
    return (update, embed_grad, encode_grad, process_grad, decode_grad, output_grad)


def solution(mesh):
    both = ("parts", "mesh")
    placed = (
        (P(None, both), P(both, None))
        + (P(),) * 11
        + (P(both, None),)
        + (P("mesh", None), P("mesh", None), P("mesh")) * 3
    )

    return jax.shard_map(
        shards,
        mesh=mesh,
        in_specs=placed,
        out_specs=(P(both, None),) + (P("parts", None),) * 5,
        check_vma=False,
    )
```

time: 186 us -> 147 us (0.79)
  matrix products: 61.6 us -> 0 us
  Pallas kernels: 0 us -> 50.3 us
  blocking collectives: 27.2 us -> 0 us
  starting transfers between devices: 26.2 us -> 41.7 us
  other arithmetic: 14.8 us -> 2.88 us
    dot_general x53 -> x0, matrix products: 61.6 us -> none  [the longest x24 26.4 us: mm_left_t(): lax.dot_general(left, right, (((0,), (0,)), ((), ())), preferred_element_...]
    pallas_call x0 -> x12, Pallas kernels: none -> 50.3 us  [call(): pl.pallas_call(body, out_shape=[jax.ShapeDtypeStruct(shape, dtype) for sh...]
    all_to_all x1 -> x0, blocking collectives: 27.2 us -> none  [chip_exchange(): lax.all_to_all(x, 'mesh', split_axis=0, concat_axis=0, tiled=True, axis_i...]
    ppermute x0 -> x14, starting transfers between devices: none -> 26.5 us  [to_chip(): return lax.ppermute(x, 'mesh', [(i, i ^ 2 * m) for i in range(count)])]
    ppermute x0 -> x14, waiting for transfers between devices: none -> 18 us  [to_chip(): return lax.ppermute(x, 'mesh', [(i, i ^ 2 * m) for i in range(count)])]
    all_to_all x3 -> x2, waiting for transfers between devices: 36.7 us -> 20.4 us  [chip_exchange(): lax.all_to_all(x, 'mesh', split_axis=0, concat_axis=0, tiled=True, axis_i...]
    all_to_all x1 -> x0, starting transfers between devices: 6.21 us -> none  [shards(): lax.all_to_all(mid_codes, 'mesh', split_axis=0, concat_axis=0, tiled=True)]
    all_to_all x3 -> x2, starting transfers between devices: 13.1 us -> 7.49 us  [chip_exchange(): lax.all_to_all(x, 'mesh', split_axis=0, concat_axis=0, tiled=True, axis_i...]
  transfers between devices with their start and end apart: 13 -> 24, of which waited for: 6 -> 10; matrix products, arithmetic and copies ran while one was open for 14% -> 5% of each run, Pallas kernels for 0% -> 10%
where the time goes in v2:
time: 147 us
  Pallas kernels  50.3 us (34%)
  starting transfers between devices  41.7 us (28%)
  waiting for transfers between devices  40.5 us (28%)
  local copies, waits for them, and re-layouts  10.4 us (7%)
  other arithmetic  2.88 us (2%)
    pallas_call x12, Pallas kernels, call(): pl.pallas_call(body, out_shape=[jax.ShapeDtypeStruct(shape, dtype) for sh...  50.3 us
    ppermute x14, starting transfers between devices, to_chip(): return lax.ppermute(x, 'mesh', [(i, i ^ 2 * m) for i in range(count)])  26.5 us
    all_to_all x2, waiting for transfers between devices, chip_exchange(): lax.all_to_all(x, 'mesh', split_axis=0, concat_axis=0, tiled=True, axis_i...  20.4 us
    ppermute x14, waiting for transfers between devices, to_chip(): return lax.ppermute(x, 'mesh', [(i, i ^ 2 * m) for i in range(count)])  18 us
    all_to_all x2, starting transfers between devices, chip_exchange(): lax.all_to_all(x, 'mesh', split_axis=0, concat_axis=0, tiled=True, axis_i...  7.49 us
    unnamed x78, local copies, waits for them, and re-layouts  6.59 us
    ppermute x1, starting transfers between devices, to_outer(): lax.ppermute(x, 'mesh', [(i, outer_of(i, count)) for i in range(count)])  5.66 us
  transfers between devices with their start and end apart: 24, of which 10 were waited for; matrix products, arithmetic and copies ran while one was open for 5% of the time, Pallas kernels for 10%

profile of v2, /device:TPU:0, one launch (start us, length us, event | category | flops | bytes accessed | tf_op | source)
XLA Modules:
  0.0 146.8 jit_solution(976592973462754650)
XLA Ops:
  1.3 5.7 %collective-permute-start.1 = (bf16[474,256]{1,0:T(8,128)(2,1)}, bf16[474,256]{1,0:T(8,128)(2,1)S(1)}, u32[]{:S(2)}, u32[]{:S(2)}) collective-permute-start(bf16[474,256]{1,0:T(8,128)(2,1)} %grid.3), channel_id=1, source_target_pairs={{0,15},{1,2},{2,1},{3,4},{4,3},{5,6},{6,5},{7,8},{8,7},{9,10},{10,... | collective-permute-start | bytes 728072 | tf_op jit(solution)/shard_map/ppermute | solution.py:24
  7.0 2.7 %shard_map.262 = (f32[256,512]{1,0:T(8,128)}, bf16[256,512]{1,0:T(8,128)(2,1)}, bf16[256,512]{1,0:T(8,128)(2,1)}, bf16[16,512]{1,0:T(8,128)(2,1)}) custom-call(bf16[474,256]{1,0:T(8,128)(2,1)} %grid.3, bf16[474,512]{1,0:T(8,128)(2,1)} %embed.3, bf16[512,512]{1,0:T(8,128)(2,1)} %enc_send.5, bf16[512,512]{1,0:T(8,128)(2,1)} %enc_recv.1, bf16[16,512]{1,0:T(8,128)(2,1)} %mesh_init.3), custom_call_target="tpu_custom_call" | custom-call | tf_op jit(solution)/shard_map/pallas_call | solution.py:101
  10.2 0.6 fusion.3.codes
  10.8 0.6 pad_add_fusion.1.lines
  11.5 0.7 copy-done.1
  12.3 4.8 %shard_map.263 = (f32[2,256,512]{2,1,0:T(8,128)}, bf16[2,256,512]{2,1,0:T(8,128)(2,1)}, f32[768,512]{1,0:T(8,128)}, f32[16,512]{1,0:T(8,128)}, f32[16,1]{1,0:T(8,128)}, /*index=5*/bf16[8,24,512]{2,1,0:T(8,128)(2,1)}) custom-call(bf16[474,256]{1,0:T(8,128)(2,1)} %copy-done.1, bf16[474,256]{1,0:T(8,128)(2,1)} %copy-done.2, bf16[474,512]{1,0:T(8,128)(2,1)} %embed.3, ...), custom_call_target="tpu_custom_call" | custom-call | tf_op jit(solution)/shard_map/pallas_call | solution.py:101
  17.1 4.0 %all-to-all-start = ((bf16[8,24,512]{2,1,0:T(8,128)(2,1)}), bf16[8,24,512]{2,1,0:T(8,128)(2,1)S(1)}, u32[]{:S(2)}, u32[]{:S(2)}) async-start(bf16[8,24,512]{2,1,0:T(8,128)(2,1)} %get-tuple-element.75), calls=%async_computation | async-start | bytes 393216 | tf_op jit(solution)/shard_map/all_to_all | solution.py:38
  21.2 0.7 reshape.199.first_row
  21.9 0.6 stack.36.where
  22.5 7.5 %all-to-all-done.chips_own = bf16[8,24,512]{2,1,0:T(8,128)(2,1)S(1)} async-done(((bf16[8,24,512]{2,1,0:T(8,128)(2,1)}), bf16[8,24,512]{2,1,0:T(8,128)(2,1)S(1)}, u32[]{:S(2)}, u32[]{:S(2)}) %all-to-all-start) | async-done | bytes 196640 | tf_op jit(solution)/shard_map/all_to_all | solution.py:38
  30.3 0.6 pad_add_fusion.dec_lines
  30.9 4.1 %shard_map.264 = (bf16[256,512]{1,0:T(8,128)(2,1)}, f32[256,512]{1,0:T(8,128)}, f32[3,256,512]{2,1,0:T(8,128)}) custom-call(bf16[256,512]{1,0:T(8,128)(2,1)} %get-tuple-element.65.hidden, bf16[512,512]{1,0:T(8,128)(2,1)} %dec_recv.3, bf16[256,512]{1,0:T(8,128)(2,1)} %cot.3, bf16[512,512]{1,0:T(8,128)(2,1)} %dec_node.3, f32[256,512]{1,0:T(8,128)} %get-tuple-element.79.pre, ...), custom_call_target="tpu_custom_call" | custom-call | tf_op jit(solution)/shard_map/pallas_call | solution.py:101
  35.0 0.7 copy-done.7
  35.7 8.8 %shard_map.265 = (bf16[256,512]{1,0:T(8,128)(2,1)}, bf16[16,512]{1,0:T(8,128)(2,1)}, bf16[256,512]{1,0:T(8,128)(2,1)}, f32[512,512]{1,0:T(8,128)}, s32[1,512]{1,...) custom-call(s32[6]{0:T(128)} %stack.36.where, ...), custom_call_target="tpu_custom_call" | custom-call | tf_op jit(solution)/shard_map/pallas_call | solution.py:101
  44.5 3.5 %all-to-all-start.1 = ((bf16[8,64,512]{2,1,0:T(8,128)(2,1)}), bf16[8,64,512]{2,1,0:T(8,128)(2,1)S(1)}, u32[]{:S(2)}, u32[]{:S(2)}) async-start(bf16[8,64,512]{2,1,0:T(8,128)(2,1)} %get-tuple-element.91), calls=%async_computation.1 | async-start | bytes 1048576 | tf_op jit(solution)/shard_map/all_to_all | solution.py:38
  48.0 0.9 fusion.6
  49.1 0.9 fusion.7
  50.1 12.9 %all-to-all-done.1 = bf16[8,64,512]{2,1,0:T(8,128)(2,1)S(1)} async-done(((bf16[8,64,512]{2,1,0:T(8,128)(2,1)}), bf16[8,64,512]{2,1,0:T(8,128)(2,1)S(1)}, u32[]{:S(2)}, u32[]{:S(2)}) %all-to-all-start.1) | async-done | bytes 524320 | tf_op jit(solution)/shard_map/all_to_all | solution.py:38
  63.4 0.6 pad_add_fusion.2.out_lines
  64.0 4.9 %shard_map.266 = (bf16[256,512]{1,0:T(8,128)(2,1)}, bf16[256,512]{1,0:T(8,128)(2,1)}, bf16[256,512]{1,0:T(8,128)(2,1)}, f32[256,512]{1,0:T(8,128)}, f32[512,512]{1,0:T(8,128)}) custom-call(s32[6]{0:T(128)} %stack.36.where, bf16[256,512]{1,0:T(8,128)(2,1)} %get-tuple-element.65.hidden, bf16[256,512]{1,0:T(8,128)(2,1)} %get-tuple-element.83.dec_norm, ...), custom_call_target="tpu_custom_call" | custom-call | tf_op jit(solution)/shard_map/pallas_call | solution.py:101
  68.9 0.8 copy-done.5
  69.7 5.4 %shard_map.267 = (bf16[256,512]{1,0:T(8,128)(2,1)}, bf16[256,512]{1,0:T(8,128)(2,1)}, bf16[16,512]{1,0:T(8,128)(2,1)}, bf16[16,512]{1,0:T(8,128)(2,1)}) custom-call(s32[6]{0:T(128)} %stack.36.where, bf16[512,512]{1,0:T(8,128)(2,1)} %bitcast.37, bf16[512,512]{1,0:T(8,128)(2,1)} %copy-done.5, bf16[512,512]{1,0:T(8,128)(2,1)} %dec_send.3, ...), custom_call_target="tpu_custom_call" | custom-call | tf_op jit(solution)/shard_map/pallas_call | solution.py:101
  75.1 6.5 %shard_map.268 = (bf16[512,512]{1,0:T(8,128)(2,1)}, bf16[512,512]{1,0:T(8,128)(2,1)}) custom-call(s32[6]{0:T(128)} %stack.36.where, bf16[16,512]{1,0:T(8,128)(2,1)} %get-tuple-element.97.enc_cot, s32[2,768]{1,0:T(2,128)} %pad_add_fusion.1.lines, f32[768,512]{1,0:T(8,128)} %get-tuple-element.98.slope, bf16[256,512]{1,0:T(8,128)(2,1)} %get-tuple-element.65.hidden, ...), custom_call_target="tpu_custom_call" | custom-call | tf_op jit(solution)/shard_map/pallas_call | solution.py:101
  82.2 2.0 %collective-permute-done.5.out_came = bf16[256,512]{1,0:T(8,128)(2,1)S(1)} collective-permute-done((bf16[256,512]{1,0:T(8,128)(2,1)S(1)}, bf16[256,512]{1,0:T(8,128)(2,1)S(1)}, u32[]{:S(2)}, u32[]{:S(2)}) %collective-permute-start.5) | collective-permute-done | bytes 262176 | tf_op jit(solution)/shard_map/ppermute | solution.py:15
  84.3 0.7 copy-done.8
  85.2 2.3 %shard_map.269 = (bf16[112,512]{1,0:T(8,128)(2,1)}, bf16[112,512]{1,0:T(8,128)(2,1)}, bf16[112,512]{1,0:T(8,128)(2,1)}, bf16[112,512]{1,0:T(8,128)(2,1)}, bf16[1...) custom-call(s32[6]{0:T(128)} %stack.36.where, ...), custom_call_target="tpu_custom_call" | custom-call | tf_op jit(solution)/shard_map/pallas_call | solution.py:101
  87.5 1.5 collective-permute-start.6
  88.9 2.0 %collective-permute-start.8 = (bf16[112,512]{1,0:T(8,128)(2,1)}, bf16[112,512]{1,0:T(8,128)(2,1)S(1)}, u32[]{:S(2)}, u32[]{:S(2)}) collective-permute-start(bf16[112,512]{1,0:T(8,128)(2,1)} %get-tuple-element.110), channel_id=1, source_target_pairs={{0,6},{1,7},{2,4},{3,5},{4,2},{5,3},{6,0},{7,1},{8,14},{9,15},{10,... | collective-permute-start | bytes 344072 | tf_op jit(solution)/shard_map/ppermute | solution.py:29
  91.1 3.7 %collective-permute-start.10 = (bf16[112,512]{1,0:T(8,128)(2,1)}, bf16[112,512]{1,0:T(8,128)(2,1)S(1)}, u32[]{:S(2)}, u32[]{:S(2)}) collective-permute-start(bf16[112,512]{1,0:T(8,128)(2,1)} %get-tuple-element.112), channel_id=1, source_target_pairs={{0,10},{1,11},{2,8},{3,9},{4,14},{5,15},{6,12},{7,13},{8,2},{9,3},... | collective-permute-start | bytes 344072 | tf_op jit(solution)/shard_map/ppermute | solution.py:29
  94.8 1.4 collective-permute-start.11
  96.2 1.2 collective-permute-done.7.refs_2_
  97.5 1.2 collective-permute-start.12
  98.6 9.3 %collective-permute-done.9.refs_4_ = bf16[112,512]{1,0:T(8,128)(2,1)S(1)} collective-permute-done((bf16[112,512]{1,0:T(8,128)(2,1)}, bf16[112,512]{1,0:T(8,128)(2,1)S(1)}, u32[]{:S(2)}, u32[]{:S(2)}) %collective-permute-start.9) | collective-permute-done | bytes 114720 | tf_op jit(solution)/shard_map/ppermute | solution.py:29
  107.9 2.7 %collective-permute-done.10.refs_5_ = bf16[112,512]{1,0:T(8,128)(2,1)S(1)} collective-permute-done((bf16[112,512]{1,0:T(8,128)(2,1)}, bf16[112,512]{1,0:T(8,128)(2,1)S(1)}, u32[]{:S(2)}, u32[]{:S(2)}) %collective-permute-start.10) | collective-permute-done | bytes 114720 | tf_op jit(solution)/shard_map/ppermute | solution.py:29
  111.4 2.0 %shard_map.270 = (bf16[96,512]{1,0:T(8,128)(2,1)}, bf16[128,512]{1,0:T(8,128)(2,1)}) custom-call(s32[6]{0:T(128)} %stack.36.where, bf16[112,512]{1,0:T(8,128)(2,1)} %get-tuple-element.107.refs_0_, bf16[112,512]{1,0:T(8,128)(2,1)} %copy-done.11, bf16[112,512]{1,0:T(8,128)(2,1)} %copy-done.12, bf16[112,512]{1,0:T(8,128)(2,1)} %copy-done.13, ...), custom_call_target="tpu_custom_call" | custom-call | tf_op jit(solution)/shard_map/pallas_call | solution.py:101
  113.4 1.3 collective-permute-start.19
  114.6 3.2 %collective-permute-start.18 = (bf16[96,512]{1,0:T(8,128)(2,1)}, bf16[96,512]{1,0:T(8,128)(2,1)S(1)}, u32[]{:S(2)}, u32[]{:S(2)}) collective-permute-start(bf16[96,512]{1,0:T(8,128)(2,1)} %get-tuple-element.115.refs_0_), channel_id=1, source_target_pairs={{0,12},{1,13},{2,14},{3,15},{4,8},{5,9},{6,10},{7,11},{8,4},{9,5},... | collective-permute-start | bytes 294920 | tf_op jit(solution)/shard_map/ppermute | solution.py:29
  117.9 3.2 %collective-permute-start.17 = (bf16[96,512]{1,0:T(8,128)(2,1)}, bf16[96,512]{1,0:T(8,128)(2,1)S(1)}, u32[]{:S(2)}, u32[]{:S(2)}) collective-permute-start(bf16[96,512]{1,0:T(8,128)(2,1)} %get-tuple-element.115.refs_0_), channel_id=1, source_target_pairs={{0,10},{1,11},{2,8},{3,9},{4,14},{5,15},{6,12},{7,13},{8,2},{9,3},... | collective-permute-start | bytes 294920 | tf_op jit(solution)/shard_map/ppermute | solution.py:29
  121.1 2.8 %collective-permute-start.15 = (bf16[96,512]{1,0:T(8,128)(2,1)}, bf16[96,512]{1,0:T(8,128)(2,1)S(1)}, u32[]{:S(2)}, u32[]{:S(2)}) collective-permute-start(bf16[96,512]{1,0:T(8,128)(2,1)} %get-tuple-element.115.refs_0_), channel_id=1, source_target_pairs={{0,6},{1,7},{2,4},{3,5},{4,2},{5,3},{6,0},{7,1},{8,14},{9,15},{10,... | collective-permute-start | bytes 294920 | tf_op jit(solution)/shard_map/ppermute | solution.py:29
  123.9 6.1 %collective-permute-start.14 = (bf16[96,512]{1,0:T(8,128)(2,1)}, bf16[96,512]{1,0:T(8,128)(2,1)S(1)}, u32[]{:S(2)}, u32[]{:S(2)}) collective-permute-start(bf16[96,512]{1,0:T(8,128)(2,1)} %get-tuple-element.115.refs_0_), channel_id=1, source_target_pairs={{0,4},{1,5},{2,6},{3,7},{4,0},{5,1},{6,2},{7,3},{8,12},{9,13},{10,... | collective-permute-start | bytes 294920 | tf_op jit(solution)/shard_map/ppermute | solution.py:29
  130.0 3.6 %collective-permute-done.17.refs_5_ = bf16[96,512]{1,0:T(8,128)(2,1)S(1)} collective-permute-done((bf16[96,512]{1,0:T(8,128)(2,1)}, bf16[96,512]{1,0:T(8,128)(2,1)S(1)}, u32[]{:S(2)}, u32[]{:S(2)}) %collective-permute-start.17) | collective-permute-done | bytes 98336 | tf_op jit(solution)/shard_map/ppermute | solution.py:29
  133.7 0.9 collective-permute-done.14.refs_2_
  135.3 0.6 copy-done.24
  136.0 2.2 %shard_map.271.own = bf16[768,512]{1,0:T(8,128)(2,1)} custom-call(s32[6]{0:T(128)} %stack.36.where, bf16[96,512]{1,0:T(8,128)(2,1)} %get-tuple-element.115.refs_0_, bf16[96,512]{1,0:T(8,128)(2,1)} %copy-done.24, bf16[96,512]{1,0:T(8,128)(2,1)} %copy-done.23, bf16[96,512]{1,0:T(8,128)(2,1)} %copy-done.22, bf16[96,512]{1,0:T(8,128)(2,1)} %copy-done.21, ...), custom_call_target="tpu_custom_call" | custom-call | tf_op jit(solution)/shard_map/pallas_call | solution.py:101
  138.7 2.8 %shard_map.273 = f32[512,512]{1,0:T(8,128)} custom-call(bf16[256,512]{1,0:T(8,128)(2,1)} %get-tuple-element.116.latent_all, bf16[256,512]{1,0:T(8,128)(2,1)} %get-tuple-element.121.unit_all, bf16[512,512]{1,0:T(8,128)(2,1)} %mid_node.5, bf16[256,512]{1,0:T(8,128)(2,1)} %get-tuple-element.122.dec_src), custom_call_target="tpu_custom_call" | custom-call | tf_op jit(solution)/shard_map/pallas_call | solution.py:101
  141.6 0.6 copy-done.10
  142.2 0.9 copy-done.4
  143.1 3.7 %shard_map.272 = (f32[474,512]{1,0:T(8,128)}, f32[512,512]{1,0:T(8,128)}, f32[512,512]{1,0:T(8,128)}, f32[512,512]{1,0:T(8,128)}) custom-call(s32[6]{0:T(128)} %stack.36.where, bf16[768,512]{1,0:T(8,128)(2,1)} %shard_map.271.own, bf16[768,512]{1,0:T(8,128)(2,1)} %copy-done.4, bf16[256,512]{1,0:T(8,128)(2,1)} %get-tuple-element.116.latent_all, ...), custom_call_target="tpu_custom_call" | custom-call | tf_op jit(solution)/shard_map/pallas_call | solution.py:101
  (123 shorter events, 5.0 us)
Async XLA Ops:
  0.6 10.8 %copy-start.33 = (s32[3]{0:T(128)S(1)}, s32[3]{0:T(128)}, u32[]{:S(2)}) copy-start(s32[3]{0:T(128)} %param.45) | copy-start | bytes 40
  0.6 10.8 %copy-start.27 = (s32[3,512]{1,0:T(4,128)S(1)}, s32[3,512]{1,0:T(4,128)}, u32[]{:S(2)}) copy-start(s32[3,512]{1,0:T(4,128)} %param.44) | copy-start | bytes 18436
  0.7 9.5 %copy-start.28 = (s32[3,512]{1,0:T(4,128)S(1)}, s32[3,512]{1,0:T(4,128)}, u32[]{:S(2)}) copy-start(s32[3,512]{1,0:T(4,128)} %param.43) | copy-start | bytes 18436
  0.7 9.3 %copy-start.32 = (s32[16]{0:T(128)S(1)}, s32[16]{0:T(128)}, u32[]{:S(2)}) copy-start(s32[16]{0:T(128)} %param.42) | copy-start | bytes 196
  0.7 9.3 %copy-start.26 = (s32[16,32]{1,0:T(8,128)S(1)}, s32[16,32]{1,0:T(8,128)}, u32[]{:S(2)}) copy-start(s32[16,32]{1,0:T(8,128)} %param.41) | copy-start | bytes 6148
  0.7 9.2 %copy-start.25 = (s32[16,32]{1,0:T(8,128)S(1)}, s32[16,32]{1,0:T(8,128)}, u32[]{:S(2)}) copy-start(s32[16,32]{1,0:T(8,128)} %param.40) | copy-start | bytes 6148
  0.7 9.0 %copy-start.31 = (s32[3]{0:T(128)S(1)}, s32[3]{0:T(128)}, u32[]{:S(2)}) copy-start(s32[3]{0:T(128)} %param.39) | copy-start | bytes 40
  0.7 9.0 %copy-start.29 = (s32[3,256]{1,0:T(4,128)S(1)}, s32[3,256]{1,0:T(4,128)}, u32[]{:S(2)}) copy-start(s32[3,256]{1,0:T(4,128)} %param.38) | copy-start | bytes 9220
  0.7 9.1 %copy-start.30 = (s32[3,256]{1,0:T(4,128)S(1)}, s32[3,256]{1,0:T(4,128)}, u32[]{:S(2)}) copy-start(s32[3,256]{1,0:T(4,128)} %param.37) | copy-start | bytes 9220
  0.7 10.8 %collective-permute-start = (bf16[474,256]{1,0:T(8,128)(2,1)}, bf16[474,256]{1,0:T(8,128)(2,1)S(1)}, u32[]{:S(2)}, u32[]{:S(2)}) collective-permute-start(bf16[474,256]{1,0:T(8,128)(2,1)} %grid.3), channel_id=1, source_target_pairs={{0,1},{1,0},{2,3},{3,2},{4,5},{5,4},{6,7},{7,6},{8,9},{9,8},{10,11... | collective-permute-start | bytes 728072 | tf_op jit(solution)/shard_map/ppermute | solution.py:15
  1.3 10.2 %collective-permute-start.1 = (bf16[474,256]{1,0:T(8,128)(2,1)}, bf16[474,256]{1,0:T(8,128)(2,1)S(1)}, u32[]{:S(2)}, u32[]{:S(2)}) collective-permute-start(bf16[474,256]{1,0:T(8,128)(2,1)} %grid.3), channel_id=1, source_target_pairs={{0,15},{1,2},{2,1},{3,4},{4,3},{5,6},{6,5},{7,8},{8,7},{9,10},{10,... | collective-permute-start | bytes 728072 | tf_op jit(solution)/shard_map/ppermute | solution.py:24
  17.1 12.8 %all-to-all-start = ((bf16[8,24,512]{2,1,0:T(8,128)(2,1)}), bf16[8,24,512]{2,1,0:T(8,128)(2,1)S(1)}, u32[]{:S(2)}, u32[]{:S(2)}) async-start(bf16[8,24,512]{2,1,0:T(8,128)(2,1)} %get-tuple-element.75), calls=%async_computation | async-start | bytes 393216 | tf_op jit(solution)/shard_map/all_to_all | solution.py:38
  30.0 5.0 %copy-start.3 = (bf16[8,24,512]{2,1,0:T(8,128)(2,1)}, bf16[8,24,512]{2,1,0:T(8,128)(2,1)S(1)}, u32[]{:S(2)}) copy-start(bf16[8,24,512]{2,1,0:T(8,128)(2,1)S(1)} %all-to-all-done.chips_own) | copy-start | bytes 589828
  30.0 5.0 %collective-permute-start.2 = (bf16[8,24,512]{2,1,0:T(8,128)(2,1)S(1)}, bf16[8,24,512]{2,1,0:T(8,128)(2,1)S(1)}, u32[]{:S(2)}, u32[]{:S(2)}) collective-permute-start(bf16[8,24,512]{2,1,0:T(8,128)(2,1)S(1)} %all-to-all-done.chips_own), channel_id=1, source_target_pairs={{0,1},{1,0},{2,3},{3,2},{4,5},{5,4},{6,7},{7,6},{8,9},{9,8},{10,11... | collective-permute-start | bytes 589832 | tf_op jit(solution)/shard_map/ppermute | solution.py:15
  44.5 18.5 %all-to-all-start.1 = ((bf16[8,64,512]{2,1,0:T(8,128)(2,1)}), bf16[8,64,512]{2,1,0:T(8,128)(2,1)S(1)}, u32[]{:S(2)}, u32[]{:S(2)}) async-start(bf16[8,64,512]{2,1,0:T(8,128)(2,1)} %get-tuple-element.91), calls=%async_computation.1 | async-start | bytes 1048576 | tf_op jit(solution)/shard_map/all_to_all | solution.py:38
  63.0 5.9 %copy-start = (bf16[8,64,512]{2,1,0:T(8,128)(2,1)}, bf16[8,64,512]{2,1,0:T(8,128)(2,1)S(1)}, u32[]{:S(2)}) copy-start(bf16[8,64,512]{2,1,0:T(8,128)(2,1)S(1)} %all-to-all-done.1) | copy-start | bytes 1572868
  63.0 5.9 %collective-permute-start.3 = (bf16[512,512]{1,0:T(8,128)(2,1)S(1)}, bf16[512,512]{1,0:T(8,128)(2,1)S(1)}, u32[]{:S(2)}, u32[]{:S(2)}) collective-permute-start(bf16[512,512]{1,0:T(8,128)(2,1)S(1)} %bitcast.36), channel_id=1, source_target_pairs={{0,1},{1,0},{2,3},{3,2},{4,5},{5,4},{6,7},{7,6},{8,9},{9,8},{10,11... | collective-permute-start | bytes 1572872 | tf_op jit(solution)/shard_map/ppermute | solution.py:15
  75.1 7.0 %copy-start.34 = (bf16[256,512]{1,0:T(8,128)(2,1)S(1)}, bf16[256,512]{1,0:T(8,128)(2,1)}, u32[]{:S(2)}) copy-start(bf16[256,512]{1,0:T(8,128)(2,1)} %get-tuple-element.105) | copy-start | bytes 786436
  81.7 2.6 %collective-permute-start.4 = (bf16[512,512]{1,0:T(8,128)(2,1)}, bf16[512,512]{1,0:T(8,128)(2,1)S(1)}, u32[]{:S(2)}, u32[]{:S(2)}) collective-permute-start(bf16[512,512]{1,0:T(8,128)(2,1)} %get-tuple-element.103), channel_id=1, source_target_pairs={{0,1},{1,0},{2,3},{3,2},{4,5},{5,4},{6,7},{7,6},{8,9},{9,8},{10,11... | collective-permute-start | bytes 1572872 | tf_op jit(solution)/shard_map/ppermute | solution.py:15
  82.2 2.1 %collective-permute-start.5 = (bf16[256,512]{1,0:T(8,128)(2,1)S(1)}, bf16[256,512]{1,0:T(8,128)(2,1)S(1)}, u32[]{:S(2)}, u32[]{:S(2)}) collective-permute-start(bf16[256,512]{1,0:T(8,128)(2,1)S(1)} %copy-done.34), channel_id=1, source_target_pairs={{0,1},{1,0},{2,3},{3,2},{4,5},{5,4},{6,7},{7,6},{8,9},{9,8},{10,11... | collective-permute-start | bytes 786440 | tf_op jit(solution)/shard_map/ppermute | solution.py:15
  84.3 0.9 copy-start.6
  87.5 7.3 %collective-permute-start.6 = (bf16[112,512]{1,0:T(8,128)(2,1)}, bf16[112,512]{1,0:T(8,128)(2,1)S(1)}, u32[]{:S(2)}, u32[]{:S(2)}) collective-permute-start(bf16[112,512]{1,0:T(8,128)(2,1)} %get-tuple-element.108), channel_id=1, source_target_pairs={{0,2},{1,3},{2,0},{3,1},{4,6},{5,7},{6,4},{7,5},{8,10},{9,11},{10,... | collective-permute-start | bytes 344072 | tf_op jit(solution)/shard_map/ppermute | solution.py:29
  88.9 8.5 %collective-permute-start.7 = (bf16[112,512]{1,0:T(8,128)(2,1)}, bf16[112,512]{1,0:T(8,128)(2,1)S(1)}, u32[]{:S(2)}, u32[]{:S(2)}) collective-permute-start(bf16[112,512]{1,0:T(8,128)(2,1)} %get-tuple-element.109), channel_id=1, source_target_pairs={{0,4},{1,5},{2,6},{3,7},{4,0},{5,1},{6,2},{7,3},{8,12},{9,13},{10,... | collective-permute-start | bytes 344072 | tf_op jit(solution)/shard_map/ppermute | solution.py:29
  88.9 9.7 %collective-permute-start.8 = (bf16[112,512]{1,0:T(8,128)(2,1)}, bf16[112,512]{1,0:T(8,128)(2,1)S(1)}, u32[]{:S(2)}, u32[]{:S(2)}) collective-permute-start(bf16[112,512]{1,0:T(8,128)(2,1)} %get-tuple-element.110), channel_id=1, source_target_pairs={{0,6},{1,7},{2,4},{3,5},{4,2},{5,3},{6,0},{7,1},{8,14},{9,15},{10,... | collective-permute-start | bytes 344072 | tf_op jit(solution)/shard_map/ppermute | solution.py:29
  91.0 17.0 %collective-permute-start.9 = (bf16[112,512]{1,0:T(8,128)(2,1)}, bf16[112,512]{1,0:T(8,128)(2,1)S(1)}, u32[]{:S(2)}, u32[]{:S(2)}) collective-permute-start(bf16[112,512]{1,0:T(8,128)(2,1)} %get-tuple-element.111), channel_id=1, source_target_pairs={{0,8},{1,9},{2,10},{3,11},{4,12},{5,13},{6,14},{7,15},{8,0},{9,1},... | collective-permute-start | bytes 344072 | tf_op jit(solution)/shard_map/ppermute | solution.py:29
  91.1 19.5 %collective-permute-start.10 = (bf16[112,512]{1,0:T(8,128)(2,1)}, bf16[112,512]{1,0:T(8,128)(2,1)S(1)}, u32[]{:S(2)}, u32[]{:S(2)}) collective-permute-start(bf16[112,512]{1,0:T(8,128)(2,1)} %get-tuple-element.112), channel_id=1, source_target_pairs={{0,10},{1,11},{2,8},{3,9},{4,14},{5,15},{6,12},{7,13},{8,2},{9,3},... | collective-permute-start | bytes 344072 | tf_op jit(solution)/shard_map/ppermute | solution.py:29
  94.8 15.8 %copy-start.11 = (bf16[112,512]{1,0:T(8,128)(2,1)}, bf16[112,512]{1,0:T(8,128)(2,1)S(1)}, u32[]{:S(2)}) copy-start(bf16[112,512]{1,0:T(8,128)(2,1)S(1)} %collective-permute-done.6.refs_1_) | copy-start | bytes 344068
  94.8 15.8 %collective-permute-start.11 = (bf16[112,512]{1,0:T(8,128)(2,1)}, bf16[112,512]{1,0:T(8,128)(2,1)S(1)}, u32[]{:S(2)}, u32[]{:S(2)}) collective-permute-start(bf16[112,512]{1,0:T(8,128)(2,1)} %get-tuple-element.113), channel_id=1, source_target_pairs={{0,12},{1,13},{2,14},{3,15},{4,8},{5,9},{6,10},{7,11},{8,4},{9,5},... | collective-permute-start | bytes 344072 | tf_op jit(solution)/shard_map/ppermute | solution.py:29
  97.5 13.2 %copy-start.12 = (bf16[112,512]{1,0:T(8,128)(2,1)}, bf16[112,512]{1,0:T(8,128)(2,1)S(1)}, u32[]{:S(2)}) copy-start(bf16[112,512]{1,0:T(8,128)(2,1)S(1)} %collective-permute-done.7.refs_2_) | copy-start | bytes 344068
  97.5 13.2 %collective-permute-start.12 = (bf16[112,512]{1,0:T(8,128)(2,1)}, bf16[112,512]{1,0:T(8,128)(2,1)S(1)}, u32[]{:S(2)}, u32[]{:S(2)}) collective-permute-start(bf16[112,512]{1,0:T(8,128)(2,1)} %get-tuple-element.114), channel_id=1, source_target_pairs={{0,14},{1,15},{2,12},{3,13},{4,10},{5,11},{6,8},{7,9},{8,6},{9,7},... | collective-permute-start | bytes 344072 | tf_op jit(solution)/shard_map/ppermute | solution.py:29
  98.6 12.0 %copy-start.13 = (bf16[112,512]{1,0:T(8,128)(2,1)}, bf16[112,512]{1,0:T(8,128)(2,1)S(1)}, u32[]{:S(2)}) copy-start(bf16[112,512]{1,0:T(8,128)(2,1)S(1)} %collective-permute-done.8.refs_3_) | copy-start | bytes 344068
  107.9 2.7 %copy-start.14 = (bf16[112,512]{1,0:T(8,128)(2,1)}, bf16[112,512]{1,0:T(8,128)(2,1)S(1)}, u32[]{:S(2)}) copy-start(bf16[112,512]{1,0:T(8,128)(2,1)S(1)} %collective-permute-done.9.refs_4_) | copy-start | bytes 344068
  113.4 24.8 %copy-start.9 = (bf16[128,512]{1,0:T(8,128)(2,1)S(1)}, bf16[128,512]{1,0:T(8,128)(2,1)}, u32[]{:S(2)}) copy-start(bf16[128,512]{1,0:T(8,128)(2,1)} %get-tuple-element.117.src_own) | copy-start | bytes 393220
  113.4 10.5 %collective-permute-start.19 = (bf16[96,512]{1,0:T(8,128)(2,1)}, bf16[96,512]{1,0:T(8,128)(2,1)S(1)}, u32[]{:S(2)}, u32[]{:S(2)}) collective-permute-start(bf16[96,512]{1,0:T(8,128)(2,1)} %get-tuple-element.115.refs_0_), channel_id=1, source_target_pairs={{0,14},{1,15},{2,12},{3,13},{4,10},{5,11},{6,8},{7,9},{8,6},{9,7},... | collective-permute-start | bytes 294920 | tf_op jit(solution)/shard_map/ppermute | solution.py:29
  114.6 15.4 %collective-permute-start.18 = (bf16[96,512]{1,0:T(8,128)(2,1)}, bf16[96,512]{1,0:T(8,128)(2,1)S(1)}, u32[]{:S(2)}, u32[]{:S(2)}) collective-permute-start(bf16[96,512]{1,0:T(8,128)(2,1)} %get-tuple-element.115.refs_0_), channel_id=1, source_target_pairs={{0,12},{1,13},{2,14},{3,15},{4,8},{5,9},{6,10},{7,11},{8,4},{9,5},... | collective-permute-start | bytes 294920 | tf_op jit(solution)/shard_map/ppermute | solution.py:29
  117.9 15.8 %collective-permute-start.17 = (bf16[96,512]{1,0:T(8,128)(2,1)}, bf16[96,512]{1,0:T(8,128)(2,1)S(1)}, u32[]{:S(2)}, u32[]{:S(2)}) collective-permute-start(bf16[96,512]{1,0:T(8,128)(2,1)} %get-tuple-element.115.refs_0_), channel_id=1, source_target_pairs={{0,10},{1,11},{2,8},{3,9},{4,14},{5,15},{6,12},{7,13},{8,2},{9,3},... | collective-permute-start | bytes 294920 | tf_op jit(solution)/shard_map/ppermute | solution.py:29
  121.1 12.7 %collective-permute-start.16 = (bf16[96,512]{1,0:T(8,128)(2,1)}, bf16[96,512]{1,0:T(8,128)(2,1)S(1)}, u32[]{:S(2)}, u32[]{:S(2)}) collective-permute-start(bf16[96,512]{1,0:T(8,128)(2,1)} %get-tuple-element.115.refs_0_), channel_id=1, source_target_pairs={{0,8},{1,9},{2,10},{3,11},{4,12},{5,13},{6,14},{7,15},{8,0},{9,1},... | collective-permute-start | bytes 294920 | tf_op jit(solution)/shard_map/ppermute | solution.py:29
  121.1 12.7 %collective-permute-start.15 = (bf16[96,512]{1,0:T(8,128)(2,1)}, bf16[96,512]{1,0:T(8,128)(2,1)S(1)}, u32[]{:S(2)}, u32[]{:S(2)}) collective-permute-start(bf16[96,512]{1,0:T(8,128)(2,1)} %get-tuple-element.115.refs_0_), channel_id=1, source_target_pairs={{0,6},{1,7},{2,4},{3,5},{4,2},{5,3},{6,0},{7,1},{8,14},{9,15},{10,... | collective-permute-start | bytes 294920 | tf_op jit(solution)/shard_map/ppermute | solution.py:29
  123.9 10.9 %copy-start.18 = (bf16[96,512]{1,0:T(8,128)(2,1)}, bf16[96,512]{1,0:T(8,128)(2,1)S(1)}, u32[]{:S(2)}) copy-start(bf16[96,512]{1,0:T(8,128)(2,1)S(1)} %collective-permute-done.19.refs_7_) | copy-start | bytes 294916
  123.9 10.8 %collective-permute-start.14 = (bf16[96,512]{1,0:T(8,128)(2,1)}, bf16[96,512]{1,0:T(8,128)(2,1)S(1)}, u32[]{:S(2)}, u32[]{:S(2)}) collective-permute-start(bf16[96,512]{1,0:T(8,128)(2,1)} %get-tuple-element.115.refs_0_), channel_id=1, source_target_pairs={{0,4},{1,5},{2,6},{3,7},{4,0},{5,1},{6,2},{7,3},{8,12},{9,13},{10,... | collective-permute-start | bytes 294920 | tf_op jit(solution)/shard_map/ppermute | solution.py:29
  130.0 4.8 %copy-start.19 = (bf16[96,512]{1,0:T(8,128)(2,1)}, bf16[96,512]{1,0:T(8,128)(2,1)S(1)}, u32[]{:S(2)}) copy-start(bf16[96,512]{1,0:T(8,128)(2,1)S(1)} %collective-permute-done.18.refs_6_) | copy-start | bytes 294916
  130.0 4.8 %collective-permute-start.13 = (bf16[96,512]{1,0:T(8,128)(2,1)}, bf16[96,512]{1,0:T(8,128)(2,1)S(1)}, u32[]{:S(2)}, u32[]{:S(2)}) collective-permute-start(bf16[96,512]{1,0:T(8,128)(2,1)} %get-tuple-element.115.refs_0_), channel_id=1, source_target_pairs={{0,2},{1,3},{2,0},{3,1},{4,6},{5,7},{6,4},{7,5},{8,10},{9,11},{10,... | collective-permute-start | bytes 294920 | tf_op jit(solution)/shard_map/ppermute | solution.py:29
  133.6 1.2 copy-start.20
  133.7 1.1 copy-start.21
  133.7 1.1 copy-start.22
  138.2 3.4 %collective-permute-start.20 = (bf16[768,512]{1,0:T(8,128)(2,1)}, bf16[768,512]{1,0:T(8,128)(2,1)S(1)}, u32[]{:S(2)}, u32[]{:S(2)}) collective-permute-start(bf16[768,512]{1,0:T(8,128)(2,1)} %shard_map.271.own), channel_id=1, source_target_pairs={{0,1},{1,0},{2,3},{3,2},{4,5},{5,4},{6,7},{7,6},{8,9},{9,8},{10,11... | collective-permute-start | bytes 2359304 | tf_op jit(solution)/shard_map/ppermute | solution.py:15
  138.2 3.4 %collective-permute-start.21 = (bf16[128,512]{1,0:T(8,128)(2,1)S(1)}, bf16[128,512]{1,0:T(8,128)(2,1)S(1)}, u32[]{:S(2)}, u32[]{:S(2)}) collective-permute-start(bf16[128,512]{1,0:T(8,128)(2,1)S(1)} %copy-done.9), channel_id=1, source_target_pairs={{0,1},{1,0},{2,3},{3,2},{4,5},{5,4},{6,7},{7,6},{8,9},{9,8},{10,11... | collective-permute-start | bytes 393224 | tf_op jit(solution)/shard_map/ppermute | solution.py:15
  142.2 0.9 copy-start.4
  (11 other events, 7.6 us)

commit v3 on v2

--- a/solution.py
+++ b/solution.py
@@ -95,15 +95,112 @@
     return jnp.where(slot < count[:, None], index, -1)
 
 
-def call(body, outs, args, scalars=0, scratch=()):
+class Arriving:
+    def __init__(self, source, buffer, done):
+        self.buffer, self.shape = buffer, source.shape
+        self.copy = pltpu.make_async_copy(source, buffer, done)
+        self.copy.start()
+
+    def ready(self):
+        if self.copy is not None:
+            self.copy.wait()
+            self.copy = None
+
+    def __getitem__(self, at):
+        self.ready()
+        return self.buffer[at]
+
+
+class Leaving:
+    def __init__(self, target, buffer, done):
+        self.buffer, self.shape = buffer, target.shape
+        self.copy = pltpu.make_async_copy(buffer, target, done)
+        self.started = False
+
+    def __getitem__(self, at):
+        return self.buffer[at]
+
+    def __setitem__(self, at, value):
+        self.buffer[at] = value
+
+    def flush(self):
+        if not self.started:
+            self.copy.start()
+            self.started = True
+
+
+class Held:
+    def __init__(self, buffer):
+        self.buffer, self.shape = buffer, buffer.shape
+
+    def ready(self):
+        pass
+
+    def flush(self):
+        pass
+
+    def __getitem__(self, at):
+        return self.buffer[at]
+
+    def __setitem__(self, at, value):
+        self.buffer[at] = value
+
+
+def held_call(body, outs, args, scalars=0, scratch=(), limit=None):
     vmem = pl.BlockSpec(memory_space=pltpu.VMEM)
     smem = pl.BlockSpec(memory_space=pltpu.SMEM)
+    held = len(args) - scalars + len(outs)
+
+    def kernel(*refs):
+        numbers, refs = refs[:scalars], refs[scalars:]
+        body(*numbers, *[Held(r) for r in refs[:held]], *refs[held:])
+
     return pl.pallas_call(
-        body,
+        kernel,
         out_shape=[jax.ShapeDtypeStruct(shape, dtype) for shape, dtype in outs],
         in_specs=[smem] * scalars + [vmem] * (len(args) - scalars),
         out_specs=[vmem] * len(outs),
         scratch_shapes=[pltpu.VMEM(shape, dtype) for shape, dtype in scratch],
+        compiler_params=pltpu.CompilerParams(vmem_limit_bytes=limit),
+    )(*args)
+
+
+def call(body, outs, args, scalars=0, scratch=()):
+    if body in COPIES_ITSELF:
+        return copying_call(body, outs, args, scalars, scratch)
+    return held_call(body, outs, args, scalars, scratch, SMALL if body in STAYS_IN_VMEM else None)
+
+
+def copying_call(body, outs, args, scalars=0, scratch=()):
+    anywhere = pl.BlockSpec(memory_space=pl.ANY)
+    smem = pl.BlockSpec(memory_space=pltpu.SMEM)
+    ins = args[scalars:]
+    n, m = len(ins), len(outs)
+
+    def kernel(*refs):
+        numbers, refs = refs[:scalars], refs[scalars:]
+        sources, targets, refs = refs[:n], refs[n : n + m], refs[n + m :]
+        in_buffers, out_buffers, own = refs[:n], refs[n : n + m], refs[n + m : -2]
+        in_done, out_done = refs[-2], refs[-1]
+        arriving = [Arriving(s, v, in_done.at[i]) for i, (s, v) in enumerate(zip(sources, in_buffers))]
+        leaving = [Leaving(t, v, out_done.at[i]) for i, (t, v) in enumerate(zip(targets, out_buffers))]
+        body(*numbers, *arriving, *leaving, *own)
+        for x in arriving:
+            x.ready()
+        for x in leaving:
+            x.flush()
+        for x in leaving:
+            x.copy.wait()
+
+    buffers = [pltpu.VMEM(x.shape, x.dtype) for x in ins] + [pltpu.VMEM(shape, dtype) for shape, dtype in outs]
+    buffers += [pltpu.VMEM(shape, dtype) for shape, dtype in scratch]
+    buffers += [pltpu.SemaphoreType.DMA((n,)), pltpu.SemaphoreType.DMA((m,))]
+    return pl.pallas_call(
+        kernel,
+        out_shape=[jax.ShapeDtypeStruct(shape, dtype) for shape, dtype in outs],
+        in_specs=[smem] * scalars + [anywhere] * n,
+        out_specs=[anywhere] * m,
+        scratch_shapes=buffers,
     )(*args)
 
 
@@ -119,9 +216,9 @@
 def own_targets(hidden, dec_recv, cot, dec_node, pre, pre_near, target, pulled, pre_slope):
     target[...] = mm(hidden[...], dec_recv[...]).astype(BF)
     pulled[...] = mm_right_t(cot[...], dec_node[...])
-    pre_slope[0] = silu_slope(pre[...])
+    pre_slope[0] = silu_slope(pre[...]).astype(BF)
     for k in range(2):
-        pre_slope[k + 1] = silu_slope(pre_near[k])
+        pre_slope[k + 1] = silu_slope(pre_near[k]).astype(BF)
 
 
 def encode(
@@ -145,12 +242,14 @@
         into = by_slot(lines[1:2, at], mesh_rows)
         inputs = mm_left_t(by_slot(lines[0:1, at], rows), proj) + mm_left_t(into, target[...])
         message, grad = silu_both(inputs)
-        slope[at, :] = grad
+        slope[at, :] = grad.astype(BF)
         part = mm(into, message.astype(BF))
         agg = part if agg is None else agg + part
     rowwise, size = normalize(agg)
     unit[...] = rowwise
     scale[...] = size
+    for x in (pre, hidden, slope):
+        x.flush()
     rows = (mesh_init[...].astype(F32) + mm(rowwise.astype(BF), enc_node[...])).astype(BF)
     for c in range(latent.shape[0]):
         latent[c, :mesh_rows, :] = rows
@@ -158,16 +257,19 @@
 
 
 def decode(
-    where, chips_own, chips_other, first_row, mid_send, mid_recv, mid_node, gain, dec_send, dec_lines, dec_target, pulled,
+    where, chips_own, chips_other, mid_send, mid_recv, mid_node, gain, dec_send, dec_lines, dec_target, pulled,
     latent_all, proj_own, target_all, mid_slope, mid_line, packed, dec_norm, dec_edge, slope, proj_all,
 ):
     chips = chips_own.shape[0]
-    edges = first_row.shape[1]
+    edges = mid_line.shape[1]
     mesh_rows = latent_all.shape[0] // (2 * chips)
     for c in range(chips):
         latent_all[c * mesh_rows : (c + 1) * mesh_rows, :] = chips_own[c, :mesh_rows, :]
         latent_all[(chips + c) * mesh_rows : (chips + c + 1) * mesh_rows, :] = chips_other[c, :mesh_rows, :]
     all_rows = latent_all.shape[0]
+    block = lax.div(lax.broadcasted_iota(jnp.int32, (1, edges), 1), edges // (2 * chips))
+    side = jnp.where(jnp.bitwise_and(block, 1) == where[0], 0, chips)
+    first_row = (side + jnp.right_shift(block, 1)) * mesh_rows
     everyone = latent_all[...]
     proj = mm(everyone, mid_send[...]).astype(BF)
     proj_all[...] = proj
@@ -178,14 +280,14 @@
         ((chips_own, where[2], where[1]), (chips_other, where[2], where[3]), (chips_other, where[5], where[4]))
     ):
         words = gathered[chip, mesh_rows:, :].astype(F32)
-        source = first_row[...] + words[0:1, :edges].astype(jnp.int32)
+        source = first_row + words[0:1, :edges].astype(jnp.int32)
         line = words[1:2, :edges].astype(jnp.int32)
         into = by_slot(line, mesh_rows)
         rows = pl.ds(pl.multiple_of(start, mesh_rows), mesh_rows)
         inputs = mm_left_t(by_slot(source, all_rows), proj) + mm_left_t(into, target_all[rows, :])
         message, grad = silu_both(inputs)
         if k == 0:
-            mid_slope[...] = grad
+            mid_slope[...] = grad.astype(BF)
             mid_line[...] = line
         parts.append(mm(into, message.astype(BF)))
         latents.append(latent_all[rows, :])
@@ -209,6 +311,8 @@
         agg = part if agg is None else agg + part
     unit, scale = normalize(agg)
     dec_norm[...] = unit.astype(BF)
+    for x in (latent_all, proj_own, target_all, mid_slope, mid_line, dec_norm):
+        x.flush()
     cot = normalize_pull(unit, scale, pulled[...]).astype(BF)
     for k in range(3):
         at = slice(k * slots, (k + 1) * slots)
@@ -245,16 +349,19 @@
     own = proj_own[...]
     inputs = mm_left_t(by_slot(out_lines[0:1, :], own.shape[0]), own)
     inputs = inputs + mm_left_t(by_slot(out_lines[1:2, :], target_all.shape[0]), target_all[...])
-    out_slope[...] = silu_slope(inputs)
-
-
-def mesh_grads(
-    where, packed_own, packed_other, dec_send, mid_node, gain, in_line, out_lines,
-    in_slope, out_slope, mid_send, mid_recv, enc_node, enc_unit, enc_scale,
-    dec_src, unit_all, src_grad, enc_cot, two_grad, cot_all,
+    out_slope[...] = silu_slope(inputs).astype(BF)
+
+
+def pull_back(
+    where, packed_own, packed_other, dec_send, mid_node, gain, in_line, in_slope, out_lines, out_slope,
+    mid_send, mid_recv, enc_node, enc_unit, enc_scale,
+    lines, slope, hidden, hidden_near, enc_send, carried, pre_slope, grid, grid_p, grid_o,
+    src_grad, dec_src, unit_all, kept, sent, two_grad, cot_all,
 ):
     core, own = where[0], where[1]
     mesh_rows = enc_unit.shape[0]
+    packed_own.ready()
+    packed_other.ready()
     chips = packed_own.shape[0] // (4 * mesh_rows)
     step = jnp.where(core == 0, chips - 1, 1)
     back = jnp.where(core == 0, 1, chips - 1)
@@ -285,36 +392,31 @@
     cot_all[...] = cot
     mine = pl.ds(pl.multiple_of(own, mesh_rows), mesh_rows)
     into = by_slot(in_line[...], mesh_rows)
-    in_edge = (mm_left_t(into, cot_all[mine, :]) * in_slope[...]).astype(BF)
+    in_edge = (mm_left_t(into, cot_all[mine, :]) * in_slope[...].astype(F32)).astype(BF)
     dst = mm(into, in_edge).astype(BF)
-    out_edge = (mm_left_t(by_slot(out_lines[1:2, :], cot.shape[0]), cot) * out_slope[...]).astype(BF)
+    out_edge = (mm_left_t(by_slot(out_lines[1:2, :], cot.shape[0]), cot) * out_slope[...].astype(F32)).astype(BF)
     src = mm(by_slot(out_lines[0:1, :], mesh_rows), out_edge).astype(BF)
     src_grad[...] = src
     latent_grad = two_grad[mine, :]
     latent_grad = latent_grad + mm_right_t(src, mid_send[...]) + mm_right_t(dst, mid_recv[...])
     pulled = mm_right_t(latent_grad.astype(BF), enc_node[...])
-    enc_cot[...] = normalize_pull(enc_unit[...], enc_scale[...], pulled).astype(BF)
-
-
-def node_grads(
-    where, enc_cot, lines, slope, hidden, hidden_near, enc_send, carried, pre_slope, grid, grid_p, grid_o,
-    kept, sent,
-):
-    core = where[0]
-    mesh_rows = enc_cot.shape[0]
+    enc_cot = normalize_pull(enc_unit[...], enc_scale[...], pulled).astype(BF)
+    for x in (src_grad, dec_src, unit_all):
+        x.flush()
+
     rows = hidden.shape[0]
     slots = lines.shape[1] // 3
     encode_term, embed_term = None, None
     for k in range(3):
         at = slice(k * slots, (k + 1) * slots)
-        edge = (mm_left_t(by_slot(lines[1:2, at], mesh_rows), enc_cot[...]) * slope[at, :]).astype(BF)
+        edge = (mm_left_t(by_slot(lines[1:2, at], mesh_rows), enc_cot) * slope[at, :].astype(F32)).astype(BF)
         src = mm(by_slot(lines[0:1, at], rows), edge).astype(BF)
         part = mm_left_t(hidden[...] if k == 0 else hidden_near[k - 1], src)
         encode_term = part if k == 0 else encode_term + part
         grad = mm_right_t(src, enc_send[...])
         if k == 0:
             grad = grad + carried[...]
-        grad = grad * pre_slope[k]
+        grad = grad * pre_slope[k].astype(F32)
         part = mm((grid, grid_p, grid_o)[k][...], grad.astype(BF))
         embed_term = part if k == 0 else embed_term + part
 
@@ -385,6 +487,8 @@
     width = embed_grad.shape[1]
     channels = embed_grad.shape[0]
     room = own.shape[0] - width // 2
+    own.ready()
+    other.ready()
 
     @pl.when(core == 0)
     def _():
@@ -402,6 +506,11 @@
 
     half = src_own.shape[0]
     process_grad[...] = mm_left_t(latent_all[:half, :], src_own[...]) + mm_left_t(latent_all[half:, :], src_other[...])
+
+
+SMALL = 24 * 2**20
+COPIES_ITSELF = (pull_back,)
+STAYS_IN_VMEM = (fold, add_up, assemble, finish, mesh_terms)
 
 
 def shards(
@@ -463,8 +572,6 @@
     enc_lines = jnp.stack([near(enc_from).reshape(-1), near(live(enc_into, enc_count)).reshape(-1)])
     dec_lines = jnp.stack([near(dec_from).reshape(-1), near(live(dec_into, dec_count)).reshape(-1)])
     edges = count * cap_mid
-    block = lax.broadcasted_iota(jnp.int32, (count, cap_mid), 0)
-    first_row = ((jnp.where(block % 2 == core, 0, chips) + block // 2) * mesh_rows).reshape(1, edges)
     outer_chip = jnp.where(core == 1, (me + 1) % count, (me + count - 1) % count) // 2
     own_start = (me // 2) * mesh_rows
     where = jnp.stack(
@@ -478,7 +585,7 @@
         [
             ((2,) + nodes, F32),
             ((2,) + nodes, BF),
-            ((enc_slots, width), F32),
+            ((enc_slots, width), BF),
             ((mesh_rows, width), F32),
             ((mesh_rows, 1), F32),
             ((chips, mesh_rows + 8, width), BF),
@@ -492,7 +599,7 @@
     latent_chips = chip_exchange(latent)
     dec_target, dec_pulled, pre_slope = call(
         own_targets,
-        [(nodes, BF), (nodes, F32), ((3,) + nodes, F32)],
+        [(nodes, BF), (nodes, F32), ((3,) + nodes, BF)],
         (hidden, dec_recv, cotangent, dec_node, pre, pre_near),
     )
     latent_other = to_partner(latent_chips)
@@ -504,14 +611,14 @@
             (everyone, BF),
             ((mesh_rows, width), BF),
             (everyone, BF),
-            ((edges, width), F32),
+            ((edges, width), BF),
             ((1, edges), jnp.int32),
             ((chips, 4 * mesh_rows, width), BF),
             (nodes, BF),
             ((dec_slots, width), BF),
         ],
         (
-            where, latent_chips, latent_other, first_row, mid_send, mid_recv, mid_node, gain, dec_send, dec_lines,
+            where, latent_chips, latent_other, mid_send, mid_recv, mid_node, gain, dec_send, dec_lines,
             dec_target, dec_pulled,
         ),
         scalars=1,
@@ -536,7 +643,7 @@
     out_half = (width // 2, width)
     update, out_kept, out_sent, carried, out_slope = call(
         settle,
-        [(nodes, BF), (out_half, BF), (out_half, BF), (nodes, F32), ((edges, width), F32)],
+        [(nodes, BF), (out_half, BF), (out_half, BF), (nodes, F32), ((edges, width), BF)],
         (
             where, hidden, dec_norm, dec_node, cotangent, dec_edge, dec_lines, dec_recv, proj_own, target_all, out_lines,
         ),
@@ -544,26 +651,18 @@
     )
     out_came = to_partner(out_sent)
 
-    dec_src_all, unit_all, src_grad, enc_cot = call(
-        mesh_grads,
-        [(everyone, BF), (everyone, BF), ((mesh_rows, width), BF), ((mesh_rows, width), BF)],
+    piece = 16 * chips
+    room = -(-max(channels, width) // piece) * piece
+    src_grad, dec_src_all, unit_all, kept, sent = call(
+        pull_back,
+        [((mesh_rows, width), BF), (everyone, BF), (everyone, BF), ((room, width), BF), ((room, width), BF)],
         (
-            where, packed_chips, packed_other, dec_send, mid_node, gain, in_line, out_lines,
-            in_slope, out_slope, mid_send, mid_recv, enc_node, enc_unit, enc_scale,
+            where, packed_chips, packed_other, dec_send, mid_node, gain, in_line, in_slope, out_lines, out_slope,
+            mid_send, mid_recv, enc_node, enc_unit, enc_scale,
+            enc_lines, enc_slope, hidden, hidden_near, enc_send, carried, pre_slope, grid_in, grid_partner, grid_outer,
         ),
         scalars=1,
         scratch=[(everyone, F32), (everyone, BF)],
-    )
-    piece = 16 * chips
-    room = -(-max(channels, width) // piece) * piece
-    kept, sent = call(
-        node_grads,
-        [((room, width), BF), ((room, width), BF)],
-        (
-            where, enc_cot, enc_lines, enc_slope, hidden, hidden_near, enc_send, carried, pre_slope,
-            grid_in, grid_partner, grid_outer,
-        ),
-        scalars=1,
     )
     (decode_grad,) = call(
         mesh_terms, [((width, width), F32)], (latent_all, unit_all, mid_node, dec_src_all)

time: 147 us -> 136 us (0.925)
  Pallas kernels: 50.3 us -> 41.1 us
  local copies, waits for them, and re-layouts: 10.4 us -> 7.28 us
    pallas_call x12 -> x11, Pallas kernels: 50.3 us -> 41.1 us  [the longest x10 31.2 us: held_call(): pl.pallas_call(kernel, out_shape=[jax.ShapeDtypeStruct(shape, dtype) for...]
    unnamed x78 -> x56, local copies, waits for them, and re-layouts: 6.59 us -> 4.14 us
  transfers between devices with their start and end apart: 24 -> 24, of which waited for: 10 -> 9; matrix products, arithmetic and copies ran while one was open for 5% -> 4% of each run, Pallas kernels for 10% -> 10%
where the time goes in v3:
time: 136 us; the launch traced here: 135 us
  starting transfers between devices  42.9 us (32%)
  Pallas kernels  41.1 us (30%)
  waiting for transfers between devices  40.2 us (30%)
  local copies, waits for them, and re-layouts  7.28 us (5%)
  other arithmetic  2.78 us (2%)
    pallas_call x10, Pallas kernels, held_call(): pl.pallas_call(kernel, out_shape=[jax.ShapeDtypeStruct(shape, dtype) for...  31.2 us
    ppermute x14, starting transfers between devices, to_chip(): return lax.ppermute(x, 'mesh', [(i, i ^ 2 * m) for i in range(count)])  27.5 us
    all_to_all x2, waiting for transfers between devices, chip_exchange(): lax.all_to_all(x, 'mesh', split_axis=0, concat_axis=0, tiled=True, axis_i...  21 us
    ppermute x14, waiting for transfers between devices, to_chip(): return lax.ppermute(x, 'mesh', [(i, i ^ 2 * m) for i in range(count)])  16.7 us
    pallas_call x1, Pallas kernels, copying_call(): pl.pallas_call(kernel, out_shape=[jax.ShapeDtypeStruct(shape, dtype) for...  9.84 us
    all_to_all x2, starting transfers between devices, chip_exchange(): lax.all_to_all(x, 'mesh', split_axis=0, concat_axis=0, tiled=True, axis_i...  7.66 us
    ppermute x1, starting transfers between devices, to_outer(): lax.ppermute(x, 'mesh', [(i, outer_of(i, count)) for i in range(count)])  5.66 us
    unnamed x56, local copies, waits for them, and re-layouts  4.14 us
  transfers between devices with their start and end apart: 24, of which 9 were waited for; matrix products, arithmetic and copies ran while one was open for 4% of the time, Pallas kernels for 10%

profile of v3, /device:TPU:0, one launch (start us, length us, event | category | flops | bytes accessed | tf_op | source)
XLA Modules:
  0.0 135.2 jit_solution(3353688193643613340)
XLA Ops:
  0.7 0.6 collective-permute-start
  1.3 5.7 %collective-permute-start.1 = (bf16[474,256]{1,0:T(8,128)(2,1)}, bf16[474,256]{1,0:T(8,128)(2,1)S(1)}, u32[]{:S(2)}, u32[]{:S(2)}) collective-permute-start(bf16[474,256]{1,0:T(8,128)(2,1)} %refs_22_.1), channel_id=1, source_target_pairs={{0,15},{1,2},{2,1},{3,4},{4,3},{5,6},{6,5},{7,8},{8,7},{9,10},{10,... | collective-permute-start | bytes 728072 | tf_op jit(solution)/shard_map/ppermute | solution.py:24
  6.9 2.7 %shard_map.262 = (f32[256,512]{1,0:T(8,128)}, bf16[256,512]{1,0:T(8,128)(2,1)}, bf16[256,512]{1,0:T(8,128)(2,1)}, bf16[16,512]{1,0:T(8,128)(2,1)}) custom-call(bf16[474,256]{1,0:T(8,128)(2,1)} %refs_22_.1, bf16[474,512]{1,0:T(8,128)(2,1)} %refs_2_.5, bf16[512,512]{1,0:T(8,128)(2,1)} %refs_19_.1, bf16[512,512]{1,0:T(8,128)(2,1)} %refs_3_.6, ...), custom_call_target="tpu_custom_call" | custom-call | tf_op jit(solution)/shard_map/pallas_call | solution.py:158
  10.1 0.6 fusion.3.refs_9_
  10.7 0.6 pad_add_fusion.1.refs_6_.refs_15_
  11.4 0.7 copy-done.9
  12.2 4.7 %shard_map.263 = (f32[2,256,512]{2,1,0:T(8,128)}, bf16[2,256,512]{2,1,0:T(8,128)(2,1)}, bf16[768,512]{1,0:T(8,128)(2,1)}, f32[16,512]{1,0:T(8,128)}, f32[16,1]{1,0:T(8,128)}, /*index=5*/bf16[8,24,512]{2,1,0:T(8,128)(2,1)}) custom-call(bf16[474,256]{1,0:T(8,128)(2,1)} %copy-done.9, bf16[474,256]{1,0:T(8,128)(2,1)} %copy-done.10, bf16[474,512]{1,0:T(8,128)(2,1)} %refs_2_.5, ...), custom_call_target="tpu_custom_call" | custom-call | tf_op jit(solution)/shard_map/pallas_call | solution.py:158
  16.9 4.2 %all-to-all-start = ((bf16[8,24,512]{2,1,0:T(8,128)(2,1)}), bf16[8,24,512]{2,1,0:T(8,128)(2,1)S(1)}, u32[]{:S(2)}, u32[]{:S(2)}) async-start(bf16[8,24,512]{2,1,0:T(8,128)(2,1)} %get-tuple-element.74), calls=%async_computation | async-start | bytes 393216 | tf_op jit(solution)/shard_map/all_to_all | solution.py:38
  21.2 0.6 stack.36.refs_0_
  21.8 8.1 %all-to-all-done.refs_1_ = bf16[8,24,512]{2,1,0:T(8,128)(2,1)S(1)} async-done(((bf16[8,24,512]{2,1,0:T(8,128)(2,1)}), bf16[8,24,512]{2,1,0:T(8,128)(2,1)S(1)}, u32[]{:S(2)}, u32[]{:S(2)}) %all-to-all-start) | async-done | bytes 196640 | tf_op jit(solution)/shard_map/all_to_all | solution.py:38
  30.2 0.6 pad_add_fusion.refs_8_.refs_6_
  30.9 3.8 %shard_map.264 = (bf16[256,512]{1,0:T(8,128)(2,1)}, f32[256,512]{1,0:T(8,128)}, bf16[3,256,512]{2,1,0:T(8,128)(2,1)}) custom-call(bf16[256,512]{1,0:T(8,128)(2,1)} %get-tuple-element.64.refs_0_.refs_1_.refs_17_, bf16[512,512]{1,0:T(8,128)(2,1)} %refs_7_.5, bf16[256,512]{1,0:T(8,128)(2,1)} %refs_4_.6, bf16[512,512]{1,0:T(8,128)(2,1)} %refs_3_.10, ...), custom_call_target="tpu_custom_call" | custom-call | tf_op jit(solution)/shard_map/pallas_call | solution.py:158
  34.7 0.7 copy-done.13
  35.4 8.9 %shard_map.265 = (bf16[256,512]{1,0:T(8,128)(2,1)}, bf16[16,512]{1,0:T(8,128)(2,1)}, bf16[256,512]{1,0:T(8,128)(2,1)}, bf16[512,512]{1,0:T(8,128)(2,1)}, s32[1,5...) custom-call(s32[6]{0:T(128)} %stack.36.refs_0_, ...), custom_call_target="tpu_custom_call" | custom-call | tf_op jit(solution)/shard_map/pallas_call | solution.py:158
  44.3 3.5 %all-to-all-start.1 = ((bf16[8,64,512]{2,1,0:T(8,128)(2,1)}), bf16[8,64,512]{2,1,0:T(8,128)(2,1)S(1)}, u32[]{:S(2)}, u32[]{:S(2)}) async-start(bf16[8,64,512]{2,1,0:T(8,128)(2,1)} %get-tuple-element.90), calls=%async_computation.1 | async-start | bytes 1048576 | tf_op jit(solution)/shard_map/all_to_all | solution.py:38
  47.8 0.9 fusion.6
  48.9 0.9 fusion.7
  49.9 12.9 %all-to-all-done.1 = bf16[8,64,512]{2,1,0:T(8,128)(2,1)S(1)} async-done(((bf16[8,64,512]{2,1,0:T(8,128)(2,1)}), bf16[8,64,512]{2,1,0:T(8,128)(2,1)S(1)}, u32[]{:S(2)}, u32[]{:S(2)}) %all-to-all-start.1) | async-done | bytes 524320 | tf_op jit(solution)/shard_map/all_to_all | solution.py:38
  63.2 0.6 pad_add_fusion.2.refs_10_.refs_8_
  63.8 4.8 %shard_map.266 = (bf16[256,512]{1,0:T(8,128)(2,1)}, bf16[256,512]{1,0:T(8,128)(2,1)}, bf16[256,512]{1,0:T(8,128)(2,1)}, f32[256,512]{1,0:T(8,128)}, bf16[512,512]{1,0:T(8,128)(2,1)}) custom-call(s32[6]{0:T(128)} %stack.36.refs_0_, bf16[256,512]{1,0:T(8,128)(2,1)} %get-tuple-element.64.refs_0_.refs_1_.refs_17_, bf16[256,512]{1,0:T(8,128)(2,1)} %get-tuple-element.82.refs_2_, ...), custom_call_target="tpu_custom_call" | custom-call | tf_op jit(solution)/shard_map/pallas_call | solution.py:158
  68.6 0.8 copy-done.12
  69.4 9.8 %shard_map.267 = (bf16[16,512]{1,0:T(8,128)(2,1)}, bf16[256,512]{1,0:T(8,128)(2,1)}, bf16[256,512]{1,0:T(8,128)(2,1)}, bf16[512,512]{1,0:T(8,128)(2,1)}, bf16[512,512]{1,0:T(8,128)(2,1)}) custom-call(s32[6]{0:T(128)} %stack.36.refs_0_, bf16[512,512]{1,0:T(8,128)(2,1)} %bitcast.37, bf16[512,512]{1,0:T(8,128)(2,1)} %copy-done.12, bf16[512,512]{1,0:T(8,128)(2,1)} %refs_3_.11, ...), custom_call_target="tpu_custom_call" | custom-call | tf_op jit(solution)/shard_map/pallas_call | solution.py:198
  79.3 0.6 collective-permute-start.4
  79.9 2.0 %collective-permute-done.5.refs_4_ = bf16[256,512]{1,0:T(8,128)(2,1)S(1)} collective-permute-done((bf16[256,512]{1,0:T(8,128)(2,1)S(1)}, bf16[256,512]{1,0:T(8,128)(2,1)S(1)}, u32[]{:S(2)}, u32[]{:S(2)}) %collective-permute-start.5) | collective-permute-done | bytes 262176 | tf_op jit(solution)/shard_map/ppermute | solution.py:15
  82.0 1.0 copy-done.2
  83.0 0.7 copy-done.7
  83.7 0.7 shard_map.268
  84.5 1.5 %collective-permute-start.6 = (bf16[112,512]{1,0:T(8,128)(2,1)S(1)}, bf16[112,512]{1,0:T(8,128)(2,1)S(1)}, u32[]{:S(2)}, u32[]{:S(2)}) collective-permute-start(bf16[112,512]{1,0:T(8,128)(2,1)S(1)} %get-tuple-element.106), channel_id=1, source_target_pairs={{0,2},{1,3},{2,0},{3,1},{4,6},{5,7},{6,4},{7,5},{8,10},{9,11},{10,... | collective-permute-start | bytes 344072 | tf_op jit(solution)/shard_map/ppermute | solution.py:29
  86.0 2.0 %collective-permute-start.8 = (bf16[112,512]{1,0:T(8,128)(2,1)S(1)}, bf16[112,512]{1,0:T(8,128)(2,1)S(1)}, u32[]{:S(2)}, u32[]{:S(2)}) collective-permute-start(bf16[112,512]{1,0:T(8,128)(2,1)S(1)} %get-tuple-element.108), channel_id=1, source_target_pairs={{0,6},{1,7},{2,4},{3,5},{4,2},{5,3},{6,0},{7,1},{8,14},{9,15},{10,... | collective-permute-start | bytes 344072 | tf_op jit(solution)/shard_map/ppermute | solution.py:29
  88.2 3.7 %collective-permute-start.10 = (bf16[112,512]{1,0:T(8,128)(2,1)S(1)}, bf16[112,512]{1,0:T(8,128)(2,1)S(1)}, u32[]{:S(2)}, u32[]{:S(2)}) collective-permute-start(bf16[112,512]{1,0:T(8,128)(2,1)S(1)} %get-tuple-element.110), channel_id=1, source_target_pairs={{0,10},{1,11},{2,8},{3,9},{4,14},{5,15},{6,12},{7,13},{8,2},{9,3},... | collective-permute-start | bytes 344072 | tf_op jit(solution)/shard_map/ppermute | solution.py:29
  91.9 1.4 %collective-permute-start.11 = (bf16[112,512]{1,0:T(8,128)(2,1)S(1)}, bf16[112,512]{1,0:T(8,128)(2,1)S(1)}, u32[]{:S(2)}, u32[]{:S(2)}) collective-permute-start(bf16[112,512]{1,0:T(8,128)(2,1)S(1)} %get-tuple-element.111), channel_id=1, source_target_pairs={{0,12},{1,13},{2,14},{3,15},{4,8},{5,9},{6,10},{7,11},{8,4},{9,5},... | collective-permute-start | bytes 344072 | tf_op jit(solution)/shard_map/ppermute | solution.py:29
  93.3 1.0 collective-permute-done.7.refs_3_
  94.3 1.4 %collective-permute-start.12 = (bf16[112,512]{1,0:T(8,128)(2,1)S(1)}, bf16[112,512]{1,0:T(8,128)(2,1)S(1)}, u32[]{:S(2)}, u32[]{:S(2)}) collective-permute-start(bf16[112,512]{1,0:T(8,128)(2,1)S(1)} %get-tuple-element.112), channel_id=1, source_target_pairs={{0,14},{1,15},{2,12},{3,13},{4,10},{5,11},{6,8},{7,9},{8,6},{9,7},... | collective-permute-start | bytes 344072 | tf_op jit(solution)/shard_map/ppermute | solution.py:29
  95.7 9.1 %collective-permute-done.9.refs_5_ = bf16[112,512]{1,0:T(8,128)(2,1)S(1)} collective-permute-done((bf16[112,512]{1,0:T(8,128)(2,1)S(1)}, bf16[112,512]{1,0:T(8,128)(2,1)S(1)}, u32[]{:S(2)}, u32[]{:S(2)}) %collective-permute-start.9) | collective-permute-done | bytes 114720 | tf_op jit(solution)/shard_map/ppermute | solution.py:29
  104.8 2.7 %collective-permute-done.10.refs_6_ = bf16[112,512]{1,0:T(8,128)(2,1)S(1)} collective-permute-done((bf16[112,512]{1,0:T(8,128)(2,1)S(1)}, bf16[112,512]{1,0:T(8,128)(2,1)S(1)}, u32[]{:S(2)}, u32[]{:S(2)}) %collective-permute-start.10) | collective-permute-done | bytes 114720 | tf_op jit(solution)/shard_map/ppermute | solution.py:29
  107.5 0.6 shard_map.269
  108.1 1.3 collective-permute-start.19
  109.5 3.2 %collective-permute-start.18 = (bf16[96,512]{1,0:T(8,128)(2,1)S(1)}, bf16[96,512]{1,0:T(8,128)(2,1)S(1)}, u32[]{:S(2)}, u32[]{:S(2)}) collective-permute-start(bf16[96,512]{1,0:T(8,128)(2,1)S(1)} %get-tuple-element.113.refs_1_), channel_id=1, source_target_pairs={{0,12},{1,13},{2,14},{3,15},{4,8},{5,9},{6,10},{7,11},{8,4},{9,5},... | collective-permute-start | bytes 294920 | tf_op jit(solution)/shard_map/ppermute | solution.py:29
  112.7 4.4 %collective-permute-start.17 = (bf16[96,512]{1,0:T(8,128)(2,1)S(1)}, bf16[96,512]{1,0:T(8,128)(2,1)S(1)}, u32[]{:S(2)}, u32[]{:S(2)}) collective-permute-start(bf16[96,512]{1,0:T(8,128)(2,1)S(1)} %get-tuple-element.113.refs_1_), channel_id=1, source_target_pairs={{0,10},{1,11},{2,8},{3,9},{4,14},{5,15},{6,12},{7,13},{8,2},{9,3},... | collective-permute-start | bytes 294920 | tf_op jit(solution)/shard_map/ppermute | solution.py:29
  117.1 2.8 %collective-permute-start.15 = (bf16[96,512]{1,0:T(8,128)(2,1)S(1)}, bf16[96,512]{1,0:T(8,128)(2,1)S(1)}, u32[]{:S(2)}, u32[]{:S(2)}) collective-permute-start(bf16[96,512]{1,0:T(8,128)(2,1)S(1)} %get-tuple-element.113.refs_1_), channel_id=1, source_target_pairs={{0,6},{1,7},{2,4},{3,5},{4,2},{5,3},{6,0},{7,1},{8,14},{9,15},{10,... | collective-permute-start | bytes 294920 | tf_op jit(solution)/shard_map/ppermute | solution.py:29
  119.9 4.1 %collective-permute-start.14 = (bf16[96,512]{1,0:T(8,128)(2,1)S(1)}, bf16[96,512]{1,0:T(8,128)(2,1)S(1)}, u32[]{:S(2)}, u32[]{:S(2)}) collective-permute-start(bf16[96,512]{1,0:T(8,128)(2,1)S(1)} %get-tuple-element.113.refs_1_), channel_id=1, source_target_pairs={{0,4},{1,5},{2,6},{3,7},{4,0},{5,1},{6,2},{7,3},{8,12},{9,13},{10,... | collective-permute-start | bytes 294920 | tf_op jit(solution)/shard_map/ppermute | solution.py:29
  123.9 1.5 %collective-permute-start.13 = (bf16[96,512]{1,0:T(8,128)(2,1)S(1)}, bf16[96,512]{1,0:T(8,128)(2,1)S(1)}, u32[]{:S(2)}, u32[]{:S(2)}) collective-permute-start(bf16[96,512]{1,0:T(8,128)(2,1)S(1)} %get-tuple-element.113.refs_1_), channel_id=1, source_target_pairs={{0,2},{1,3},{2,0},{3,1},{4,6},{5,7},{6,4},{7,5},{8,10},{9,11},{10,... | collective-permute-start | bytes 294920 | tf_op jit(solution)/shard_map/ppermute | solution.py:29
  125.5 2.9 %collective-permute-done.17.refs_6_ = bf16[96,512]{1,0:T(8,128)(2,1)S(1)} collective-permute-done((bf16[96,512]{1,0:T(8,128)(2,1)S(1)}, bf16[96,512]{1,0:T(8,128)(2,1)S(1)}, u32[]{:S(2)}, u32[]{:S(2)}) %collective-permute-start.17) | collective-permute-done | bytes 98336 | tf_op jit(solution)/shard_map/ppermute | solution.py:29
  128.4 1.0 collective-permute-done.14.refs_3_
  129.3 0.6 shard_map.270.refs_1_
  130.0 0.5 collective-permute-start.21
  130.5 1.6 %shard_map.272 = f32[512,512]{1,0:T(8,128)} custom-call(bf16[256,512]{1,0:T(8,128)(2,1)S(1)} %copy-done.1, bf16[256,512]{1,0:T(8,128)(2,1)S(1)} %copy-done.4, bf16[512,512]{1,0:T(8,128)(2,1)S(1)} %copy-done, bf16[256,512]{1,0:T(8,128)(2,1)S(1)} %copy-done.3), custom_call_target="tpu_custom_call" | custom-call | tf_op jit(solution)/shard_map/pallas_call | solution.py:158
  132.5 2.8 %shard_map.271 = (f32[474,512]{1,0:T(8,128)}, f32[512,512]{1,0:T(8,128)}, f32[512,512]{1,0:T(8,128)}, f32[512,512]{1,0:T(8,128)}) custom-call(s32[6]{0:T(128)S(1)} %copy-done.6, bf16[768,512]{1,0:T(8,128)(2,1)S(1)} %shard_map.270.refs_1_, bf16[768,512]{1,0:T(8,128)(2,1)S(1)} %collective-permute-done.20.refs_2_, bf16[256,512]{1,0:T(8,128)(2,1)S(1)} %copy-done.1, ...), custom_call_target="tpu_custom_call" | custom-call | tf_op jit(solution)/shard_map/pallas_call | solution.py:158
  (95 shorter events, 2.3 us)
Async XLA Ops:
  0.6 10.7 %copy-start.22 = (s32[3]{0:T(128)S(1)}, s32[3]{0:T(128)}, u32[]{:S(2)}) copy-start(s32[3]{0:T(128)} %param.45) | copy-start | bytes 40
  0.6 10.7 %copy-start.16 = (s32[3,512]{1,0:T(4,128)S(1)}, s32[3,512]{1,0:T(4,128)}, u32[]{:S(2)}) copy-start(s32[3,512]{1,0:T(4,128)} %param.44) | copy-start | bytes 18436
  0.7 9.4 %copy-start.17 = (s32[3,512]{1,0:T(4,128)S(1)}, s32[3,512]{1,0:T(4,128)}, u32[]{:S(2)}) copy-start(s32[3,512]{1,0:T(4,128)} %param.43) | copy-start | bytes 18436
  0.7 9.3 %copy-start.21 = (s32[16]{0:T(128)S(1)}, s32[16]{0:T(128)}, u32[]{:S(2)}) copy-start(s32[16]{0:T(128)} %param.42) | copy-start | bytes 196
  0.7 9.3 %copy-start.15 = (s32[16,32]{1,0:T(8,128)S(1)}, s32[16,32]{1,0:T(8,128)}, u32[]{:S(2)}) copy-start(s32[16,32]{1,0:T(8,128)} %param.41) | copy-start | bytes 6148
  0.7 9.1 %copy-start.14 = (s32[16,32]{1,0:T(8,128)S(1)}, s32[16,32]{1,0:T(8,128)}, u32[]{:S(2)}) copy-start(s32[16,32]{1,0:T(8,128)} %param.40) | copy-start | bytes 6148
  0.7 9.0 %copy-start.20 = (s32[3]{0:T(128)S(1)}, s32[3]{0:T(128)}, u32[]{:S(2)}) copy-start(s32[3]{0:T(128)} %param.39) | copy-start | bytes 40
  0.7 9.0 %copy-start.18 = (s32[3,256]{1,0:T(4,128)S(1)}, s32[3,256]{1,0:T(4,128)}, u32[]{:S(2)}) copy-start(s32[3,256]{1,0:T(4,128)} %param.38) | copy-start | bytes 9220
  0.7 9.0 %copy-start.19 = (s32[3,256]{1,0:T(4,128)S(1)}, s32[3,256]{1,0:T(4,128)}, u32[]{:S(2)}) copy-start(s32[3,256]{1,0:T(4,128)} %param.37) | copy-start | bytes 9220
  0.7 10.7 %collective-permute-start = (bf16[474,256]{1,0:T(8,128)(2,1)}, bf16[474,256]{1,0:T(8,128)(2,1)S(1)}, u32[]{:S(2)}, u32[]{:S(2)}) collective-permute-start(bf16[474,256]{1,0:T(8,128)(2,1)} %refs_22_.1), channel_id=1, source_target_pairs={{0,1},{1,0},{2,3},{3,2},{4,5},{5,4},{6,7},{7,6},{8,9},{9,8},{10,11... | collective-permute-start | bytes 728072 | tf_op jit(solution)/shard_map/ppermute | solution.py:15
  1.3 10.1 %collective-permute-start.1 = (bf16[474,256]{1,0:T(8,128)(2,1)}, bf16[474,256]{1,0:T(8,128)(2,1)S(1)}, u32[]{:S(2)}, u32[]{:S(2)}) collective-permute-start(bf16[474,256]{1,0:T(8,128)(2,1)} %refs_22_.1), channel_id=1, source_target_pairs={{0,15},{1,2},{2,1},{3,4},{4,3},{5,6},{6,5},{7,8},{8,7},{9,10},{10,... | collective-permute-start | bytes 728072 | tf_op jit(solution)/shard_map/ppermute | solution.py:24
  11.4 0.7 copy-start.9
  11.4 0.8 copy-start.10
  16.9 13.0 %all-to-all-start = ((bf16[8,24,512]{2,1,0:T(8,128)(2,1)}), bf16[8,24,512]{2,1,0:T(8,128)(2,1)S(1)}, u32[]{:S(2)}, u32[]{:S(2)}) async-start(bf16[8,24,512]{2,1,0:T(8,128)(2,1)} %get-tuple-element.74), calls=%async_computation | async-start | bytes 393216 | tf_op jit(solution)/shard_map/all_to_all | solution.py:38
  29.9 4.8 %copy-start.11 = (bf16[8,24,512]{2,1,0:T(8,128)(2,1)}, bf16[8,24,512]{2,1,0:T(8,128)(2,1)S(1)}, u32[]{:S(2)}) copy-start(bf16[8,24,512]{2,1,0:T(8,128)(2,1)S(1)} %all-to-all-done.refs_1_) | copy-start | bytes 589828
  29.9 4.8 %collective-permute-start.2 = (bf16[8,24,512]{2,1,0:T(8,128)(2,1)S(1)}, bf16[8,24,512]{2,1,0:T(8,128)(2,1)S(1)}, u32[]{:S(2)}, u32[]{:S(2)}) collective-permute-start(bf16[8,24,512]{2,1,0:T(8,128)(2,1)S(1)} %all-to-all-done.refs_1_), channel_id=1, source_target_pairs={{0,1},{1,0},{2,3},{3,2},{4,5},{5,4},{6,7},{7,6},{8,9},{9,8},{10,11... | collective-permute-start | bytes 589832 | tf_op jit(solution)/shard_map/ppermute | solution.py:15
  34.7 0.7 copy-start.13
  44.3 18.5 %all-to-all-start.1 = ((bf16[8,64,512]{2,1,0:T(8,128)(2,1)}), bf16[8,64,512]{2,1,0:T(8,128)(2,1)S(1)}, u32[]{:S(2)}, u32[]{:S(2)}) async-start(bf16[8,64,512]{2,1,0:T(8,128)(2,1)} %get-tuple-element.90), calls=%async_computation.1 | async-start | bytes 1048576 | tf_op jit(solution)/shard_map/all_to_all | solution.py:38
  62.8 5.8 %copy-start.8 = (bf16[8,64,512]{2,1,0:T(8,128)(2,1)}, bf16[8,64,512]{2,1,0:T(8,128)(2,1)S(1)}, u32[]{:S(2)}) copy-start(bf16[8,64,512]{2,1,0:T(8,128)(2,1)S(1)} %all-to-all-done.1) | copy-start | bytes 1572868
  62.8 5.8 %collective-permute-start.3 = (bf16[512,512]{1,0:T(8,128)(2,1)S(1)}, bf16[512,512]{1,0:T(8,128)(2,1)S(1)}, u32[]{:S(2)}, u32[]{:S(2)}) collective-permute-start(bf16[512,512]{1,0:T(8,128)(2,1)S(1)} %bitcast.36), channel_id=1, source_target_pairs={{0,1},{1,0},{2,3},{3,2},{4,5},{5,4},{6,7},{7,6},{8,9},{9,8},{10,11... | collective-permute-start | bytes 1572872 | tf_op jit(solution)/shard_map/ppermute | solution.py:15
  68.6 0.8 copy-start.12
  69.4 10.4 %copy-start.23 = (bf16[256,512]{1,0:T(8,128)(2,1)S(1)}, bf16[256,512]{1,0:T(8,128)(2,1)}, u32[]{:S(2)}) copy-start(bf16[256,512]{1,0:T(8,128)(2,1)} %get-tuple-element.103) | copy-start | bytes 786436
  69.4 12.6 %copy-start.5 = (bf16[256,512]{1,0:T(8,128)(2,1)S(1)}, bf16[256,512]{1,0:T(8,128)(2,1)}, u32[]{:S(2)}) copy-start(bf16[256,512]{1,0:T(8,128)(2,1)} %get-tuple-element.102.refs_3_) | copy-start | bytes 786436
  69.4 12.6 %copy-start.6 = (s32[6]{0:T(128)S(1)}, s32[6]{0:T(128)}, u32[]{:S(2)}) copy-start(s32[6]{0:T(128)} %stack.36.refs_0_) | copy-start | bytes 76
  79.3 2.7 %collective-permute-start.4 = (bf16[512,512]{1,0:T(8,128)(2,1)}, bf16[512,512]{1,0:T(8,128)(2,1)S(1)}, u32[]{:S(2)}, u32[]{:S(2)}) collective-permute-start(bf16[512,512]{1,0:T(8,128)(2,1)} %get-tuple-element.101), channel_id=1, source_target_pairs={{0,1},{1,0},{2,3},{3,2},{4,5},{5,4},{6,7},{7,6},{8,9},{9,8},{10,11... | collective-permute-start | bytes 1572872 | tf_op jit(solution)/shard_map/ppermute | solution.py:15
  79.8 2.1 %collective-permute-start.5 = (bf16[256,512]{1,0:T(8,128)(2,1)S(1)}, bf16[256,512]{1,0:T(8,128)(2,1)S(1)}, u32[]{:S(2)}, u32[]{:S(2)}) collective-permute-start(bf16[256,512]{1,0:T(8,128)(2,1)S(1)} %copy-done.23), channel_id=1, source_target_pairs={{0,1},{1,0},{2,3},{3,2},{4,5},{5,4},{6,7},{7,6},{8,9},{9,8},{10,11... | collective-permute-start | bytes 786440 | tf_op jit(solution)/shard_map/ppermute | solution.py:15
  82.0 1.0 copy-start.2
  83.0 0.7 copy-start.7
  84.4 46.1 %copy-start = (bf16[512,512]{1,0:T(8,128)(2,1)S(1)}, bf16[512,512]{1,0:T(8,128)(2,1)}, u32[]{:S(2)}) copy-start(bf16[512,512]{1,0:T(8,128)(2,1)} %refs_2_.7) | copy-start | bytes 1572868
  84.5 46.1 %copy-start.1 = (bf16[256,512]{1,0:T(8,128)(2,1)S(1)}, bf16[256,512]{1,0:T(8,128)(2,1)}, u32[]{:S(2)}) copy-start(bf16[256,512]{1,0:T(8,128)(2,1)} %get-tuple-element.114.refs_3_.refs_0_) | copy-start | bytes 786436
  84.5 46.1 %copy-start.3 = (bf16[256,512]{1,0:T(8,128)(2,1)S(1)}, bf16[256,512]{1,0:T(8,128)(2,1)}, u32[]{:S(2)}) copy-start(bf16[256,512]{1,0:T(8,128)(2,1)} %get-tuple-element.120.refs_3_) | copy-start | bytes 786436
  84.5 46.1 %copy-start.4 = (bf16[256,512]{1,0:T(8,128)(2,1)S(1)}, bf16[256,512]{1,0:T(8,128)(2,1)}, u32[]{:S(2)}) copy-start(bf16[256,512]{1,0:T(8,128)(2,1)} %get-tuple-element.119.refs_1_) | copy-start | bytes 786436
  84.5 7.4 %collective-permute-start.6 = (bf16[112,512]{1,0:T(8,128)(2,1)S(1)}, bf16[112,512]{1,0:T(8,128)(2,1)S(1)}, u32[]{:S(2)}, u32[]{:S(2)}) collective-permute-start(bf16[112,512]{1,0:T(8,128)(2,1)S(1)} %get-tuple-element.106), channel_id=1, source_target_pairs={{0,2},{1,3},{2,0},{3,1},{4,6},{5,7},{6,4},{7,5},{8,10},{9,11},{10,... | collective-permute-start | bytes 344072 | tf_op jit(solution)/shard_map/ppermute | solution.py:29
  86.0 8.3 %collective-permute-start.7 = (bf16[112,512]{1,0:T(8,128)(2,1)S(1)}, bf16[112,512]{1,0:T(8,128)(2,1)S(1)}, u32[]{:S(2)}, u32[]{:S(2)}) collective-permute-start(bf16[112,512]{1,0:T(8,128)(2,1)S(1)} %get-tuple-element.107), channel_id=1, source_target_pairs={{0,4},{1,5},{2,6},{3,7},{4,0},{5,1},{6,2},{7,3},{8,12},{9,13},{10,... | collective-permute-start | bytes 344072 | tf_op jit(solution)/shard_map/ppermute | solution.py:29
  86.0 9.7 %collective-permute-start.8 = (bf16[112,512]{1,0:T(8,128)(2,1)S(1)}, bf16[112,512]{1,0:T(8,128)(2,1)S(1)}, u32[]{:S(2)}, u32[]{:S(2)}) collective-permute-start(bf16[112,512]{1,0:T(8,128)(2,1)S(1)} %get-tuple-element.108), channel_id=1, source_target_pairs={{0,6},{1,7},{2,4},{3,5},{4,2},{5,3},{6,0},{7,1},{8,14},{9,15},{10,... | collective-permute-start | bytes 344072 | tf_op jit(solution)/shard_map/ppermute | solution.py:29
  88.0 16.7 %collective-permute-start.9 = (bf16[112,512]{1,0:T(8,128)(2,1)S(1)}, bf16[112,512]{1,0:T(8,128)(2,1)S(1)}, u32[]{:S(2)}, u32[]{:S(2)}) collective-permute-start(bf16[112,512]{1,0:T(8,128)(2,1)S(1)} %get-tuple-element.109), channel_id=1, source_target_pairs={{0,8},{1,9},{2,10},{3,11},{4,12},{5,13},{6,14},{7,15},{8,0},{9,1},... | collective-permute-start | bytes 344072 | tf_op jit(solution)/shard_map/ppermute | solution.py:29
  88.2 19.3 %collective-permute-start.10 = (bf16[112,512]{1,0:T(8,128)(2,1)S(1)}, bf16[112,512]{1,0:T(8,128)(2,1)S(1)}, u32[]{:S(2)}, u32[]{:S(2)}) collective-permute-start(bf16[112,512]{1,0:T(8,128)(2,1)S(1)} %get-tuple-element.110), channel_id=1, source_target_pairs={{0,10},{1,11},{2,8},{3,9},{4,14},{5,15},{6,12},{7,13},{8,2},{9,3},... | collective-permute-start | bytes 344072 | tf_op jit(solution)/shard_map/ppermute | solution.py:29
  91.9 15.6 %collective-permute-start.11 = (bf16[112,512]{1,0:T(8,128)(2,1)S(1)}, bf16[112,512]{1,0:T(8,128)(2,1)S(1)}, u32[]{:S(2)}, u32[]{:S(2)}) collective-permute-start(bf16[112,512]{1,0:T(8,128)(2,1)S(1)} %get-tuple-element.111), channel_id=1, source_target_pairs={{0,12},{1,13},{2,14},{3,15},{4,8},{5,9},{6,10},{7,11},{8,4},{9,5},... | collective-permute-start | bytes 344072 | tf_op jit(solution)/shard_map/ppermute | solution.py:29
  94.3 13.1 %collective-permute-start.12 = (bf16[112,512]{1,0:T(8,128)(2,1)S(1)}, bf16[112,512]{1,0:T(8,128)(2,1)S(1)}, u32[]{:S(2)}, u32[]{:S(2)}) collective-permute-start(bf16[112,512]{1,0:T(8,128)(2,1)S(1)} %get-tuple-element.112), channel_id=1, source_target_pairs={{0,14},{1,15},{2,12},{3,13},{4,10},{5,11},{6,8},{7,9},{8,6},{9,7},... | collective-permute-start | bytes 344072 | tf_op jit(solution)/shard_map/ppermute | solution.py:29
  108.1 11.7 %collective-permute-start.19 = (bf16[96,512]{1,0:T(8,128)(2,1)S(1)}, bf16[96,512]{1,0:T(8,128)(2,1)S(1)}, u32[]{:S(2)}, u32[]{:S(2)}) collective-permute-start(bf16[96,512]{1,0:T(8,128)(2,1)S(1)} %get-tuple-element.113.refs_1_), channel_id=1, source_target_pairs={{0,14},{1,15},{2,12},{3,13},{4,10},{5,11},{6,8},{7,9},{8,6},{9,7},... | collective-permute-start | bytes 294920 | tf_op jit(solution)/shard_map/ppermute | solution.py:29
  109.5 14.5 %collective-permute-start.18 = (bf16[96,512]{1,0:T(8,128)(2,1)S(1)}, bf16[96,512]{1,0:T(8,128)(2,1)S(1)}, u32[]{:S(2)}, u32[]{:S(2)}) collective-permute-start(bf16[96,512]{1,0:T(8,128)(2,1)S(1)} %get-tuple-element.113.refs_1_), channel_id=1, source_target_pairs={{0,12},{1,13},{2,14},{3,15},{4,8},{5,9},{6,10},{7,11},{8,4},{9,5},... | collective-permute-start | bytes 294920 | tf_op jit(solution)/shard_map/ppermute | solution.py:29
  112.7 15.7 %collective-permute-start.17 = (bf16[96,512]{1,0:T(8,128)(2,1)S(1)}, bf16[96,512]{1,0:T(8,128)(2,1)S(1)}, u32[]{:S(2)}, u32[]{:S(2)}) collective-permute-start(bf16[96,512]{1,0:T(8,128)(2,1)S(1)} %get-tuple-element.113.refs_1_), channel_id=1, source_target_pairs={{0,10},{1,11},{2,8},{3,9},{4,14},{5,15},{6,12},{7,13},{8,2},{9,3},... | collective-permute-start | bytes 294920 | tf_op jit(solution)/shard_map/ppermute | solution.py:29
  117.1 11.3 %collective-permute-start.16 = (bf16[96,512]{1,0:T(8,128)(2,1)S(1)}, bf16[96,512]{1,0:T(8,128)(2,1)S(1)}, u32[]{:S(2)}, u32[]{:S(2)}) collective-permute-start(bf16[96,512]{1,0:T(8,128)(2,1)S(1)} %get-tuple-element.113.refs_1_), channel_id=1, source_target_pairs={{0,8},{1,9},{2,10},{3,11},{4,12},{5,13},{6,14},{7,15},{8,0},{9,1},... | collective-permute-start | bytes 294920 | tf_op jit(solution)/shard_map/ppermute | solution.py:29
  117.1 11.3 %collective-permute-start.15 = (bf16[96,512]{1,0:T(8,128)(2,1)S(1)}, bf16[96,512]{1,0:T(8,128)(2,1)S(1)}, u32[]{:S(2)}, u32[]{:S(2)}) collective-permute-start(bf16[96,512]{1,0:T(8,128)(2,1)S(1)} %get-tuple-element.113.refs_1_), channel_id=1, source_target_pairs={{0,6},{1,7},{2,4},{3,5},{4,2},{5,3},{6,0},{7,1},{8,14},{9,15},{10,... | collective-permute-start | bytes 294920 | tf_op jit(solution)/shard_map/ppermute | solution.py:29
  119.9 9.5 %collective-permute-start.14 = (bf16[96,512]{1,0:T(8,128)(2,1)S(1)}, bf16[96,512]{1,0:T(8,128)(2,1)S(1)}, u32[]{:S(2)}, u32[]{:S(2)}) collective-permute-start(bf16[96,512]{1,0:T(8,128)(2,1)S(1)} %get-tuple-element.113.refs_1_), channel_id=1, source_target_pairs={{0,4},{1,5},{2,6},{3,7},{4,0},{5,1},{6,2},{7,3},{8,12},{9,13},{10,... | collective-permute-start | bytes 294920 | tf_op jit(solution)/shard_map/ppermute | solution.py:29
  123.9 5.4 %collective-permute-start.13 = (bf16[96,512]{1,0:T(8,128)(2,1)S(1)}, bf16[96,512]{1,0:T(8,128)(2,1)S(1)}, u32[]{:S(2)}, u32[]{:S(2)}) collective-permute-start(bf16[96,512]{1,0:T(8,128)(2,1)S(1)} %get-tuple-element.113.refs_1_), channel_id=1, source_target_pairs={{0,2},{1,3},{2,0},{3,1},{4,6},{5,7},{6,4},{7,5},{8,10},{9,11},{10,... | collective-permute-start | bytes 294920 | tf_op jit(solution)/shard_map/ppermute | solution.py:29
  130.0 2.5 %collective-permute-start.20 = (bf16[768,512]{1,0:T(8,128)(2,1)S(1)}, bf16[768,512]{1,0:T(8,128)(2,1)S(1)}, u32[]{:S(2)}, u32[]{:S(2)}) collective-permute-start(bf16[768,512]{1,0:T(8,128)(2,1)S(1)} %shard_map.270.refs_1_), channel_id=1, source_target_pairs={{0,1},{1,0},{2,3},{3,2},{4,5},{5,4},{6,7},{7,6},{8,9},{9,8},{10,11... | collective-permute-start | bytes 2359304 | tf_op jit(solution)/shard_map/ppermute | solution.py:15
  130.0 2.5 %collective-permute-start.21 = (bf16[128,512]{1,0:T(8,128)(2,1)S(1)}, bf16[128,512]{1,0:T(8,128)(2,1)S(1)}, u32[]{:S(2)}, u32[]{:S(2)}) collective-permute-start(bf16[128,512]{1,0:T(8,128)(2,1)S(1)} %get-tuple-element.115.refs_4_), channel_id=1, source_target_pairs={{0,1},{1,0},{2,3},{3,2},{4,5},{5,4},{6,7},{7,6},{8,9},{9,8},{10,11... | collective-permute-start | bytes 393224 | tf_op jit(solution)/shard_map/ppermute | solution.py:15
